TPU v7x, 256 devices: a whole 4x4x8 slice. The times are simulated.
256 devices in a mesh: dp: 32 (over x, y, core), head: 8 (over z).
Axes of the slice: x: 4, y: 4, z: 8, core: 2. Of those that a mesh axis runs over, the one named last changes fastest.
Arguments:
- queries: bfloat16 [1280, 128, 1024], P('dp', None, 'head'), may hold values from -8 to 8
- resp_keys: bfloat16 [1280, 128, 128], P('dp'), may hold values from -6 to 6
- resp_values: bfloat16 [1280, 128, 128], P('dp'), may hold values from -6 to 6
- prompt_keys: bfloat16 [128, 512, 128], P('dp'), may hold values from -8 to 8
- prompt_values: bfloat16 [128, 512, 128], P('dp'), may hold values from -6 to 6
- grad_out: bfloat16 [1280, 128, 1024], P('dp', None, 'head'), may hold values from -6 to 6
- slot_prompt: int32 [1280], P('dp'), may hold values from -1 to 127, as said below
- slot_length: int32 [1280], P('dp'), may hold values from 0 to 128, as said below
Outputs:
- attn_out: bfloat16 [1280, 128, 1024], P('dp', None, 'head')
- grad_queries: bfloat16 [1280, 128, 1024], P('dp', None, 'head')
- grad_resp_keys: float32 [1280, 128, 128], P('dp', 'head')
- grad_resp_values: float32 [1280, 128, 128], P('dp', 'head')
- grad_prompt_keys: float32 [128, 512, 128], P('dp')
- grad_prompt_values: float32 [128, 512, 128], P('dp')
Inputs may be any that keep to these rules, and one draw needn't show every extreme that they name: `slot_prompt`: prompt p is held by index p // 4 of dp. Every prompt is named by exactly 8 slots. At most 2 slots of one device name prompts held by one same device, and this is reached. On some device all 40 slots are live. `slot_length`: 0 exactly in the slots where slot_prompt is -1, else 1 or more; 128 is reached.
All inputs are finite; a program needn't handle non-finite values.
Results may differ from a plain program's by a relative error of at most 0.015.
Values may be sent and summed in bfloat16 or wider, within the bound.
A program may use at most 128 MiB of HBM per device.

v0:
```python
import jax
import jax.numpy as jnp
from jax import lax
from jax.sharding import PartitionSpec as P

FANOUT = 8


def copy_for_each(value, axis):
    copies = jnp.broadcast_to(value, (lax.axis_size(axis), *value.shape))
    return lax.all_to_all(copies, axis, split_axis=0, concat_axis=0, tiled=True)


def joined_along(blocks, dim):
    blocks = jnp.moveaxis(blocks, 0, dim)
    dims = blocks.shape
    return blocks.reshape(*dims[:dim], dims[dim] * dims[dim + 1], *dims[dim + 2 :])


def gather_directly(value, axis, dim):
    blocks = copy_for_each(value, axis)
    return joined_along(blocks, dim)


def sent_together(arrays, axis, split_dim, concat_dim, along):
    ends, at = ([], 0)
    for a in arrays[:-1]:
        at += a.shape[along]
        ends.append(at)
    both = jnp.concatenate(arrays, axis=along)
    return tuple(
        jnp.split(
            lax.all_to_all(both, axis, split_axis=split_dim, concat_axis=concat_dim, tiled=True),
            ends,
            axis=along,
        )
    )


def sent_together_2(arrays, axis, dim, along):
    both = jnp.concatenate(arrays, axis=along)
    result, at, outs = (lax.psum_scatter(both, axis, scatter_dimension=dim, tiled=True), 0, [])
    for a in arrays:
        outs.append(lax.slice_in_dim(result, at, at + a.shape[along], axis=along))
        at += a.shape[along]
    return tuple(outs)


def causal_table(resp_len):
    positions = jnp.arange(resp_len, dtype=jnp.int32)
    return positions[:, None] >= positions[None, :]


def prefix_forward(query_rows, key_rows, value_rows, factor):
    scores = (
        jnp.einsum("rhd,nd->hrn", query_rows, key_rows, preferred_element_type=jnp.float32) * factor
    )
    maximum = jnp.max(scores, axis=2)
    exp_terms = jnp.exp(scores - maximum[:, :, None])
    row_sums = jnp.sum(exp_terms, axis=2)
    result = jnp.einsum(
        "hrn,nd->rhd",
        exp_terms.astype(jnp.bfloat16),
        value_rows,
        preferred_element_type=jnp.float32,
    )
    return (result / jnp.transpose(row_sums)[:, :, None], maximum + jnp.log(row_sums))


def prefix_backward(query_rows, grad_rows, log_total, delta_rows, key_rows, value_rows, factor):
    scores = (
        jnp.einsum("rhd,nd->hrn", query_rows, key_rows, preferred_element_type=jnp.float32) * factor
    )
    prob_rows = jnp.exp(scores - log_total[:, :, None])
    dprob_rows = jnp.einsum(
        "rhd,nd->hrn", grad_rows, value_rows, preferred_element_type=jnp.float32
    )
    dscore = (prob_rows * (dprob_rows - delta_rows[:, :, None])).astype(jnp.bfloat16)
    grad_query = (
        jnp.einsum("hrn,nd->rhd", dscore, key_rows, preferred_element_type=jnp.float32) * factor
    ).astype(jnp.bfloat16)
    grad_keys = (
        jnp.einsum("hrn,rhd->nd", dscore, query_rows, preferred_element_type=jnp.float32) * factor
    )
    grad_values = jnp.einsum(
        "hrn,rhd->nd", prob_rows.astype(jnp.bfloat16), grad_rows, preferred_element_type=jnp.float32
    )
    return (grad_query, grad_keys, grad_values)


def response_forward(query_rows, key_rows, value_rows, factor):
    causal = causal_table(query_rows.shape[1])
    scores = (
        jnp.einsum("sthd,sud->shtu", query_rows, key_rows, preferred_element_type=jnp.float32)
        * factor
    )
    masked = jnp.where(causal, scores, -1e30)
    maximum = jnp.max(masked, axis=3)
    exp_terms = jnp.where(causal, jnp.exp(masked - maximum[..., None]), 0.0)
    row_sums = jnp.sum(exp_terms, axis=3)
    result = jnp.einsum(
        "shtu,sud->sthd",
        exp_terms.astype(jnp.bfloat16),
        value_rows,
        preferred_element_type=jnp.float32,
    )
    return (result / jnp.transpose(row_sums, (0, 2, 1))[..., None], maximum + jnp.log(row_sums))


def response_backward(query_rows, grad_rows, log_total, delta_rows, key_rows, value_rows, factor):
    causal = causal_table(query_rows.shape[1])
    scores = (
        jnp.einsum("sthd,sud->shtu", query_rows, key_rows, preferred_element_type=jnp.float32)
        * factor
    )
    prob_rows = jnp.where(
        causal, jnp.exp(jnp.where(causal, scores, -1e30) - log_total[..., None]), 0.0
    )
    dprob_rows = jnp.einsum(
        "sthd,sud->shtu", grad_rows, value_rows, preferred_element_type=jnp.float32
    )
    dscore = (prob_rows * (dprob_rows - delta_rows[..., None])).astype(jnp.bfloat16)
    grad_query = (
        jnp.einsum("shtu,sud->sthd", dscore, key_rows, preferred_element_type=jnp.float32) * factor
    )
    grad_keys = (
        jnp.einsum("shtu,sthd->sud", dscore, query_rows, preferred_element_type=jnp.float32)
        * factor
    )
    grad_values = jnp.einsum(
        "shtu,sthd->sud",
        prob_rows.astype(jnp.bfloat16),
        grad_rows,
        preferred_element_type=jnp.float32,
    )
    return (grad_query, grad_keys, grad_values)


def body(
    queries, resp_keys, resp_values, prompt_keys, prompt_values, grad_out, slot_prompt, slot_length
):
    dp_count = lax.axis_size("dp")
    my_index = lax.axis_index("dp")
    slot_count, resp_len, row_width = queries.shape
    held_count, prompt_len, head_dim = prompt_keys.shape
    head_count = row_width // head_dim
    factor = head_dim ** (-0.5)
    pair_limit = max(2, FANOUT * held_count // dp_count)
    item_count = dp_count * pair_limit
    group_rows = FANOUT * resp_len
    all_prompt = gather_directly(slot_prompt, "dp", 0)
    slot_ids = jnp.arange(slot_count, dtype=jnp.int32)
    before = slot_ids[None, :] < slot_ids[:, None]
    holder_own = jnp.where(slot_prompt >= 0, slot_prompt // held_count, -1)
    order_own = jnp.sum((holder_own[:, None] == holder_own[None, :]) & before, axis=1)
    target = jnp.where(holder_own >= 0, holder_own * pair_limit + order_own, -1)
    item_ids = jnp.arange(item_count, dtype=jnp.int32)
    send_hit = target[None, :] == item_ids[:, None]
    send_slot = jnp.sum(jnp.where(send_hit, slot_ids[None, :], 0), axis=1)
    send_live = jnp.any(send_hit, axis=1)
    fetch_index = jnp.maximum(target, 0)
    owner_grid = jnp.where(all_prompt >= 0, all_prompt // held_count, -1).reshape(
        dp_count, slot_count
    )
    order_all = jnp.sum(
        (owner_grid[:, :, None] == owner_grid[:, None, :]) & before[None], axis=2
    ).reshape(-1)
    item_all = (
        jnp.arange(dp_count * slot_count, dtype=jnp.int32) // slot_count * pair_limit + order_all
    )
    my_prompts = my_index * held_count + jnp.arange(held_count, dtype=jnp.int32)
    member = all_prompt[None, :] == my_prompts[:, None]
    ranking = jnp.cumsum(member.astype(jnp.int32), axis=1) - 1
    chosen = member[:, None, :] & (
        ranking[:, None, :] == jnp.arange(FANOUT, dtype=jnp.int32)[None, :, None]
    )
    group_item = jnp.sum(jnp.where(chosen, item_all[None, None, :], 0), axis=2).reshape(-1)
    back_hit = group_item[None, :] == item_ids[:, None]
    back_index = jnp.sum(
        jnp.where(back_hit, jnp.arange(held_count * FANOUT, dtype=jnp.int32)[None, :], 0), axis=1
    )
    back_live = jnp.any(back_hit, axis=1)

    def outgoing(value, index, present):
        picked = value[index]
        keep_mask = present.reshape((-1,) + (1,) * (value.ndim - 1))
        return jnp.where(keep_mask, picked, jnp.zeros_like(picked)).reshape(
            (dp_count, pair_limit) + value.shape[1:]
        )

    def grouped(value):
        return value.reshape((item_count,) + value.shape[2:])[group_item]

    def arriving(value):
        return value.reshape((item_count,) + value.shape[2:])[fetch_index]

    def statistic(value):
        return jnp.transpose(
            grouped(value).reshape(held_count, FANOUT, head_count, resp_len), (0, 2, 1, 3)
        ).reshape(held_count, head_count, group_rows)

    received = lax.all_to_all(
        outgoing(queries, send_slot, send_live), "dp", split_axis=0, concat_axis=0, tiled=True
    )
    group_query = grouped(received).reshape(held_count, group_rows, head_count, head_dim)

    def forward_prompt(inputs):
        return prefix_forward(inputs[0], inputs[1], inputs[2], factor)

    prefix_out, prefix_lse = lax.map(forward_prompt, (group_query, prompt_keys, prompt_values))
    out_items = prefix_out.reshape(held_count * FANOUT, resp_len, row_width)
    lse_items = jnp.transpose(
        prefix_lse.reshape(held_count, head_count, FANOUT, resp_len), (0, 2, 1, 3)
    ).reshape(held_count * FANOUT, head_count, resp_len)
    back_out, back_lse = sent_together(
        (outgoing(out_items, back_index, back_live), outgoing(lse_items, back_index, back_live)),
        "dp",
        0,
        0,
        2,
    )
    part_out = arriving(back_out).reshape(slot_count, resp_len, head_count, head_dim)
    part_lse = arriving(back_lse)
    query4 = queries.reshape(slot_count, resp_len, head_count, head_dim)
    local_out, local_lse = response_forward(query4, resp_keys, resp_values, factor)
    log_total = jnp.logaddexp(part_lse, local_lse)
    weight_part = jnp.transpose(jnp.exp(part_lse - log_total), (0, 2, 1))[..., None]
    weight_local = jnp.transpose(jnp.exp(local_lse - log_total), (0, 2, 1))[..., None]
    positions = jnp.arange(resp_len, dtype=jnp.int32)
    is_live = (positions[None, :] < slot_length[:, None]) & (slot_prompt[:, None] >= 0)
    merged = weight_part * part_out + weight_local * local_out
    attn4 = jnp.where(is_live[:, :, None, None], merged, 0.0).astype(jnp.bfloat16)
    attn_out = attn4.reshape(slot_count, resp_len, row_width)
    grad_live = jnp.where(is_live[:, :, None], grad_out, jnp.zeros_like(grad_out))
    grad4 = grad_live.reshape(slot_count, resp_len, head_count, head_dim)
    delta = jnp.transpose(
        jnp.sum(grad4.astype(jnp.float32) * attn4.astype(jnp.float32), axis=3), (0, 2, 1)
    )
    sent_grad = lax.all_to_all(
        outgoing(grad_live, send_slot, send_live), "dp", split_axis=0, concat_axis=0, tiled=True
    )
    sent_lse, sent_delta = sent_together(
        (outgoing(log_total, send_slot, send_live), outgoing(delta, send_slot, send_live)),
        "dp",
        0,
        0,
        1,
    )
    back_grad = grouped(sent_grad).reshape(held_count, group_rows, head_count, head_dim)

    def backward_prompt(inputs):
        return prefix_backward(
            inputs[0], inputs[1], inputs[2], inputs[3], inputs[4], inputs[5], factor
        )

    prefix_dq, prefix_dk, prefix_dv = lax.map(
        backward_prompt,
        (
            group_query,
            back_grad,
            statistic(sent_lse),
            statistic(sent_delta),
            prompt_keys,
            prompt_values,
        ),
    )
    grad_prompt_keys, grad_prompt_values = lax.psum((prefix_dk, prefix_dv), "head")
    returned = lax.all_to_all(
        outgoing(
            prefix_dq.reshape(held_count * FANOUT, resp_len, row_width), back_index, back_live
        ),
        "dp",
        split_axis=0,
        concat_axis=0,
        tiled=True,
    )
    part_dq = (
        arriving(returned).reshape(slot_count, resp_len, head_count, head_dim).astype(jnp.float32)
    )
    local_dq, local_dk, local_dv = response_backward(
        query4, grad4, log_total, delta, resp_keys, resp_values, factor
    )
    has_prompt = (slot_prompt >= 0)[:, None, None, None]
    grad_queries = (
        jnp.where(has_prompt, part_dq + local_dq, 0.0)
        .astype(jnp.bfloat16)
        .reshape(slot_count, resp_len, row_width)
    )
    grad_resp_keys, grad_resp_values = sent_together_2((local_dk, local_dv), "head", 1, 0)
    return (
        attn_out,
        grad_queries,
        grad_resp_keys,
        grad_resp_values,
        grad_prompt_keys,
        grad_prompt_values,
    )


def solution(mesh):
    return jax.shard_map(
        body,
        mesh=mesh,
        in_specs=(
            P("dp", None, "head"),
            P("dp", None, None),
            P("dp", None, None),
            P("dp", None, None),
            P("dp", None, None),
            P("dp", None, "head"),
            P("dp"),
            P("dp"),
        ),
        out_specs=(
            P("dp", None, "head"),
            P("dp", None, "head"),
            P("dp", "head", None),
            P("dp", "head", None),
            P("dp", None, None),
            P("dp", None, None),
        ),
        check_vma=False,
    )
```

profile of v0, /device:TPU:1, one launch (start us, length us, event | category | flops | bytes accessed | tf_op | source)
XLA Modules:
  0.0 363.4 jit_solution(14403466841583603955)
XLA Ops:
  7.2 1.4 broadcast_in_dim.215
  8.6 8.6 %all-to-all-start = ((s32[32,1,40]{2,1,0:T(1,128)}), s32[32,1,40]{2,1,0:T(1,128)S(1)}, u32[]{:S(2)}, u32[]{:S(2)}) async-start(s32[32,1,40]{2,1,0:T(1,128)} %broadcast_in_dim.215), calls=%async_computation | async-start | bytes 32768 | tf_op jit(solution)/shard_map/all_to_all | solution.py:11
  19.0 2.2 gather_fusion
  21.2 3.1 broadcast_select_fusion.2
  24.3 7.4 %all-to-all-start.1 = ((bf16[32,2,128,128]{3,2,1,0:T(8,128)(2,1)}), bf16[32,2,128,128]{3,2,1,0:T(8,128)(2,1)}, u32[]{:S(2)}, u32[]{:S(2)}) async-start(bf16[32,2,128,128]{3,2,1,0:T(8,128)(2,1)} %broadcast_select_fusion.2), calls=%async_computation.1 | async-start | bytes 4194304 | tf_op jit(solution)/shard_map/all_to_all | solution.py:202
  36.6 23.5 %all-to-all-done.1 = bf16[32,2,128,128]{3,2,1,0:T(8,128)(2,1)} async-done(((bf16[32,2,128,128]{3,2,1,0:T(8,128)(2,1)}), bf16[32,2,128,128]{3,2,1,0:T(8,128)(2,1)}, u32[]{:S(2)}, u32[]{:S(2)}) %all-to-all-start.1) | async-done | bytes 2097184 | tf_op jit(solution)/shard_map/all_to_all | solution.py:202
  60.1 2.3 gather_fusion.1
  62.5 17.0 %while.26 = (s32[]{:T(128)}, f32[4,1024,1,128]{3,1,0,2:T(8,128)}, f32[4,1,1024]{2,1,0:T(1,128)S(1)}, bf16[4,512,128]{2,1,0:T(8,128)(2,1)}, bf16[4,512,128]{2,1,0...) while((s32[]{:T(128)}, f32[4,1024,1,128]{3,1,0,2:T(8,128)}, f32[4,1,1024]{2,1,0:T(1,128)S(1)}, ...), condition=%wide.region_11.12_spmd, body=%wide.region_8.11_spmd.sunk | while | flops 272759808 | bytes 9479265 | solution.py:210
  62.5 1.4 multiply_reduce_fusion.2
  64.2 1.4 fusion.137
  66.7 1.3 multiply_reduce_fusion.2
  68.5 1.4 fusion.137
  71.0 1.3 multiply_reduce_fusion.2
  72.7 1.4 fusion.137
  75.2 1.3 multiply_reduce_fusion.2
  77.0 1.4 fusion.137
  80.1 4.4 %gather_fusion.2 = f32[64,128,128]{2,1,0:T(8,128)} fusion(f32[32,128,128]{2,1,0:T(8,128)} %bitcast.313, s32[1024]{0:T(1024)S(1)} %pad_clamp_fusion.1), kind=kCustom, calls=%fused_computation.2 | custom fusion | bytes 8388864 | tf_op jit(solution)/shard_map/gather | solution.py:185
  84.7 2.5 broadcast_select_fusion
  87.6 4.2 %copy.77 = f32[32,2,129,128]{3,1,2,0:T(2,128)} copy(f32[32,2,129,128]{3,2,1,0:T(8,128)S(1)} %pad_maximum_fusion.1) | data formatting | bytes 8454144 | tf_op jit(solution)/shard_map/concatenate | solution.py:30
  91.8 5.4 %all-to-all-start.2 = ((f32[32,2,129,128]{3,1,2,0:T(2,128)}), f32[32,2,129,128]{3,1,2,0:T(2,128)}, u32[]{:S(2)}, u32[]{:S(2)}) async-start(f32[32,2,129,128]{3,1,2,0:T(2,128)} %copy.77), calls=%async_computation.2 | async-start | bytes 8454144 | tf_op jit(solution)/shard_map/all_to_all | solution.py:33
  97.6 2.4 fusion.102
  100.0 1.5 copy-done.2
  102.0 47.8 %all-to-all-done.2 = f32[32,2,129,128]{3,1,2,0:T(2,128)} async-done(((f32[32,2,129,128]{3,1,2,0:T(2,128)}), f32[32,2,129,128]{3,1,2,0:T(2,128)}, u32[]{:S(2)}, u32[]{:S(2)}) %all-to-all-start.2) | async-done | bytes 4227104 | tf_op jit(solution)/shard_map/all_to_all | solution.py:33
  149.8 2.5 split.17
  152.3 2.6 copy.100
  154.9 4.4 %gather_fusion.5 = f32[40,128,128]{2,1,0:T(8,128)} fusion(f32[64,128,128]{2,1,0:T(8,128)} %bitcast.309, s32[1024]{0:T(1024)S(1)} %pad_clamp_fusion), kind=kCustom, calls=%fused_computation.5 | custom fusion | bytes 5243040 | tf_op jit(solution)/shard_map/gather | solution.py:195
  160.8 7.8 %fusion.59 = (f32[40,128]{1,0:T(8,128)S(1)}, bf16[40,128,128]{2,1,0:T(8,128)(2,1)S(1)}, bf16[40,128,1,128]{3,1,0,2:T(8,128)(2,1)}) fusion(bf16[40,128,128]{2,1,0:T(8,128)(2,1)} %param.17, pred[40,128]{1,0:T(8,128)(4,1)S(1)} %fusion.83, f32[40,128]{1,0:T(8,128)S(1)} %fusion.66, bf16[40,128,128]{2,1,0:T(8,128)(2,1)} %param.14, ...), kind=kOutput, calls=%fused_computation.90 | convolution fusion | flops 176942080 | bytes 10609664 | tf_op jit(solution)/shard_map/shtu,sud->sthd/dot_general | solution.py:101
  173.0 2.9 pad_maximum_fusion
  177.2 2.2 gather_fusion.9
  180.2 7.1 %all-to-all-start.3 = ((f32[32,4,1,128]{3,2,1,0:T(1,128)}), f32[32,4,1,128]{3,2,1,0:T(1,128)S(1)}, u32[]{:S(2)}, u32[]{:S(2)}) async-start(f32[32,4,1,128]{3,2,1,0:T(1,128)} %pad_maximum_fusion.2), calls=%async_computation.3 | async-start | bytes 131072 | tf_op jit(solution)/shard_map/all_to_all | solution.py:33
  187.3 3.2 broadcast_select_fusion.1
  190.5 4.2 %all-to-all-done.3 = f32[32,4,1,128]{3,2,1,0:T(1,128)S(1)} async-done(((f32[32,4,1,128]{3,2,1,0:T(1,128)}), f32[32,4,1,128]{3,2,1,0:T(1,128)S(1)}, u32[]{:S(2)}, u32[]{:S(2)}) %all-to-all-start.3) | async-done | bytes 65568 | tf_op jit(solution)/shard_map/all_to_all | solution.py:33
  194.6 4.7 %all-to-all-start.4 = ((bf16[32,2,128,128]{3,2,1,0:T(8,128)(2,1)}), bf16[32,2,128,128]{3,2,1,0:T(8,128)(2,1)}, u32[]{:S(2)}, u32[]{:S(2)}) async-start(bf16[32,2,128,128]{3,2,1,0:T(8,128)(2,1)} %broadcast_select_fusion.1), calls=%async_computation.4 | async-start | bytes 4194304 | tf_op jit(solution)/shard_map/all_to_all | solution.py:239
  200.6 27.3 %all-to-all-done.4 = bf16[32,2,128,128]{3,2,1,0:T(8,128)(2,1)} async-done(((bf16[32,2,128,128]{3,2,1,0:T(8,128)(2,1)}), bf16[32,2,128,128]{3,2,1,0:T(8,128)(2,1)}, u32[]{:S(2)}, u32[]{:S(2)}) %all-to-all-start.4) | async-done | bytes 2097184 | tf_op jit(solution)/shard_map/all_to_all | solution.py:239
  227.9 2.3 gather_fusion.10
  230.2 29.3 %while.27 = (s32[]{:T(128)}, bf16[4,1024,1,128]{3,1,0,2:T(8,128)(2,1)}, f32[4,512,128]{2,1,0:T(8,128)}, f32[4,512,128]{2,1,0:T(8,128)}, bf16[4,512,128]{2,1,0:T(...) while((s32[]{:T(128)}, ...), condition=%wide.region_17.18_spmd, body=%wide.region_16.17_spmd.sunk | while | flops 675610624 | bytes 12746881 | solution.py:256
  230.2 1.3 fusion.148
  231.6 1.5 fusion.149
  233.1 1.2 fusion.152
  234.3 1.2 fusion.150
  235.5 1.2 fusion.151
  237.6 1.3 fusion.148
  238.9 1.5 fusion.149
  240.4 1.2 fusion.152
  241.6 1.2 fusion.150
  242.8 1.2 fusion.151
  244.9 1.3 fusion.148
  246.2 1.5 fusion.149
  247.7 1.2 fusion.152
  248.9 1.2 fusion.150
  250.1 1.2 fusion.151
  252.2 1.3 fusion.148
  253.5 1.5 fusion.149
  255.0 1.2 fusion.152
  256.2 1.2 fusion.150
  259.5 2.2 gather_fusion.12
  261.7 1.6 broadcast_select_fusion.3
  263.3 5.2 %all-to-all-start.5 = ((bf16[32,2,128,128]{3,2,1,0:T(8,128)(2,1)}), bf16[32,2,128,128]{3,2,1,0:T(8,128)(2,1)}, u32[]{:S(2)}, u32[]{:S(2)}) async-start(bf16[32,2,128,128]{3,2,1,0:T(8,128)(2,1)} %broadcast_select_fusion.3), calls=%async_computation.5 | async-start | bytes 4194304 | tf_op jit(solution)/shard_map/all_to_all | solution.py:268
  269.2 27.7 %all-to-all-done.5 = bf16[32,2,128,128]{3,2,1,0:T(8,128)(2,1)} async-done(((bf16[32,2,128,128]{3,2,1,0:T(8,128)(2,1)}), bf16[32,2,128,128]{3,2,1,0:T(8,128)(2,1)}, u32[]{:S(2)}, u32[]{:S(2)}) %all-to-all-start.5) | async-done | bytes 2097184 | tf_op jit(solution)/shard_map/all_to_all | solution.py:268
  296.9 3.5 gather_fusion.13
  300.4 3.6 %fusion.68 = bf16[40,128,128]{2,1,0:T(8,128)(2,1)} fusion(bf16[40,128,128]{1,2,0:T(8,128)(2,1)S(1)} %copy-done.7, bf16[40,128,128]{2,1,0:T(8,128)(2,1)} %param.13, bf16[40,128,128]{2,1,0:T(8,128)(2,1)} %gather_fusion.13, pred[40]{0:T(512)(128)(4,1)S(1)} %broadcast_compare_fusion.1), kind=kOutput, calls=%fused_computation.109 | convolution fusion | flops 171048960 | bytes 5242920 | tf_op jit(solution)/shard_map/shtu,sud->sthd/dot_general | solution.py:124
  304.0 2.0 fusion.99
  306.0 47.2 %all-reduce.3.cloned.1.call-done = (f32[4,512,128]{2,1,0:T(8,128)}, f32[4,512,128]{2,1,0:T(8,128)}) async-done(((f32[4,512,128]{2,1,0:T(8,128)}, f32[4,512,128]{2,1,0:T(8,128)}), (f32[4,512,128]{2,1,0:T(8,128)}, f32[4,512,128]{2,1,0:T(8,128)})) %all-reduce.3.cloned.1.call-update) | async-done | bytes 2097168 | tf_op jit(solution)/shard_map/psum | solution.py:267
  353.2 2.4 copy.140
  (125 shorter events, 29.8 us)
Async XLA Ops:
  7.2 11.8 %copy-start = (bf16[40,128,128]{2,1,0:T(8,128)(2,1)S(1)}, bf16[40,128,128]{2,1,0:T(8,128)(2,1)}, u32[]{:S(2)}) copy-start(bf16[40,128,128]{2,1,0:T(8,128)(2,1)} %param.12) | copy-start | bytes 3932164
  8.6 15.7 %all-to-all-start = ((s32[32,1,40]{2,1,0:T(1,128)}), s32[32,1,40]{2,1,0:T(1,128)S(1)}, u32[]{:S(2)}, u32[]{:S(2)}) async-start(s32[32,1,40]{2,1,0:T(1,128)} %broadcast_in_dim.215), calls=%async_computation | async-start | bytes 32768 | tf_op jit(solution)/shard_map/all_to_all | solution.py:11
  24.3 35.8 %all-to-all-start.1 = ((bf16[32,2,128,128]{3,2,1,0:T(8,128)(2,1)}), bf16[32,2,128,128]{3,2,1,0:T(8,128)(2,1)}, u32[]{:S(2)}, u32[]{:S(2)}) async-start(bf16[32,2,128,128]{3,2,1,0:T(8,128)(2,1)} %broadcast_select_fusion.2), calls=%async_computation.1 | async-start | bytes 4194304 | tf_op jit(solution)/shard_map/all_to_all | solution.py:202
  91.8 5.7 %copy-start.10 = (s32[40]{0:T(128)S(1)}, s32[40]{0:T(128)}, u32[]{:S(2)}) copy-start(s32[40]{0:T(128)} %param.18) | copy-start | bytes 484
  91.8 5.7 %copy-start.11 = (s32[40]{0:T(128)S(1)}, s32[40]{0:T(128)}, u32[]{:S(2)}) copy-start(s32[40]{0:T(128)} %param.19) | copy-start | bytes 484
  91.8 58.0 %all-to-all-start.2 = ((f32[32,2,129,128]{3,1,2,0:T(2,128)}), f32[32,2,129,128]{3,1,2,0:T(2,128)}, u32[]{:S(2)}, u32[]{:S(2)}) async-start(f32[32,2,129,128]{3,1,2,0:T(2,128)} %copy.77), calls=%async_computation.2 | async-start | bytes 8454144 | tf_op jit(solution)/shard_map/all_to_all | solution.py:33
  97.2 206.8 %reduce-scatter.2.cloned.1.call-start = ((), (), s32[]{:S(2)}) async-start(), calls=%async_computation.7 | async-start | bytes 5898240 | tf_op jit(solution)/shard_map/reduce_scatter | solution.py:42
  99.9 1.5 copy-start.2
  160.7 7.8 %copy-start.3 = (f32[40,1,128,128]{2,3,0,1:T(8,128)S(1)}, f32[40,1,128,128]{2,3,0,1:T(8,128)}, u32[]{:S(2)}) copy-start(f32[40,1,128,128]{2,3,0,1:T(8,128)} %copy-done.2) | copy-start | bytes 7864324
  168.6 1.1 copy-start.4
  168.6 1.8 copy-start.8
  171.4 1.1 copy-start.6
  175.9 1.3 copy-start.5
  180.2 14.4 %all-to-all-start.3 = ((f32[32,4,1,128]{3,2,1,0:T(1,128)}), f32[32,4,1,128]{3,2,1,0:T(1,128)S(1)}, u32[]{:S(2)}, u32[]{:S(2)}) async-start(f32[32,4,1,128]{3,2,1,0:T(1,128)} %pad_maximum_fusion.2), calls=%async_computation.3 | async-start | bytes 131072 | tf_op jit(solution)/shard_map/all_to_all | solution.py:33
  194.6 33.2 %all-to-all-start.4 = ((bf16[32,2,128,128]{3,2,1,0:T(8,128)(2,1)}), bf16[32,2,128,128]{3,2,1,0:T(8,128)(2,1)}, u32[]{:S(2)}, u32[]{:S(2)}) async-start(bf16[32,2,128,128]{3,2,1,0:T(8,128)(2,1)} %broadcast_select_fusion.1), calls=%async_computation.4 | async-start | bytes 4194304 | tf_op jit(solution)/shard_map/all_to_all | solution.py:239
  263.3 33.7 %all-to-all-start.5 = ((bf16[32,2,128,128]{3,2,1,0:T(8,128)(2,1)}), bf16[32,2,128,128]{3,2,1,0:T(8,128)(2,1)}, u32[]{:S(2)}, u32[]{:S(2)}) async-start(bf16[32,2,128,128]{3,2,1,0:T(8,128)(2,1)} %broadcast_select_fusion.3), calls=%async_computation.5 | async-start | bytes 4194304 | tf_op jit(solution)/shard_map/all_to_all | solution.py:268
  268.4 84.7 %all-reduce.3.cloned.1.call-start = ((), (), s32[]{:S(2)}) async-start(), calls=%async_computation.8 | async-start | bytes 4194304 | tf_op jit(solution)/shard_map/psum | solution.py:267
  268.5 31.9 %copy-start.7 = (bf16[40,128,128]{1,2,0:T(8,128)(2,1)S(1)}, bf16[40,128,128]{1,2,0:T(8,128)(2,1)}, u32[]{:S(2)}) copy-start(bf16[40,128,128]{1,2,0:T(8,128)(2,1)} %copy-done.6) | copy-start | bytes 3932164
  353.2 2.4 copy-start.9
  353.2 3.4 copy-start.1
Sparse Core Ops, SparseCore 0:
  176.0 67.4 reduce-scatter.1
  272.2 80.8 all-reduce.2
where the time goes:
time: 368 us; the launch traced here: 363 us
  waiting for transfers between devices  178 us (48%)
  local copies, waits for them, and re-layouts  57 us (15%)
  matrix products  52.6 us (14%)
  starting transfers between devices  38.6 us (10%)
  other arithmetic  22.1 us (6%)
  between operations  14.5 us (4%)
    all_to_all x2, waiting for transfers between devices, sent_together(): lax.all_to_all(both, axis, split_axis=split_dim, concat_axis=concat_dim,...  52 us
    psum x1, waiting for transfers between devices, body(): lax.psum((prefix_dk, prefix_dv), 'head')  47.2 us
    all_to_all x1, waiting for transfers between devices, body(): lax.all_to_all(outgoing(prefix_dq.reshape(held_count * FANOUT, resp_len,...  27.7 us
    all_to_all x1, waiting for transfers between devices, body(): lax.all_to_all(outgoing(grad_live, send_slot, send_live), 'dp', split_axi...  27.3 us
    all_to_all x1, waiting for transfers between devices, body(): lax.all_to_all(outgoing(queries, send_slot, send_live), 'dp', split_axis=...  23.5 us
    gather x7, local copies, waits for them, and re-layouts, outgoing(): picked = value[index]  12.8 us
    all_to_all x2, starting transfers between devices, sent_together(): lax.all_to_all(both, axis, split_axis=split_dim, concat_axis=concat_dim,...  12.4 us
    select_n x6, other arithmetic, outgoing(): jnp.where(keep_mask, picked, jnp.zeros_like(picked))  10.7 us
  transfers between devices with their start and end apart: 8, of which 6 were waited for; matrix products, arithmetic and copies ran while one was open for 19% of the time, Pallas kernels for 0%

commit v1 on v0

v1 whole, which is shorter than its diff:
```python
import functools
import math

import jax
import jax.numpy as jnp
from jax import lax
from jax.experimental import pallas as pl
from jax.experimental.pallas import tpu as pltpu
from jax.sharding import PartitionSpec as P

FANOUT = 8
LOG2E = math.log2(math.e)
F32 = jnp.float32
BF16 = jnp.bfloat16
STAT = 16


def dot(a, b, dims):
    return lax.dot_general(a, b, (dims, ((), ())), preferred_element_type=F32)


NT = ((1,), (1,))
NN = ((1,), (0,))
TN = ((0,), (0,))


def two_parts(value):
    high = value.astype(BF16)
    low = (value - high.astype(F32)).astype(BF16)
    return high.astype(F32), low.astype(F32)


def pack_rows(first, second):
    width = first.shape[1]
    rows = lax.broadcasted_iota(jnp.int32, (STAT, width), 0)
    a, b = two_parts(first)
    c, d = two_parts(second)
    packed = jnp.where(rows == 0, a, jnp.where(rows == 1, b, jnp.where(rows == 2, c, d)))
    return jnp.where(rows < 4, packed, 0.0).astype(BF16)


def unpack_rows(packed):
    rows = packed.astype(F32)
    return rows[0:1] + rows[1:2], rows[2:3] + rows[3:4]


def live_rows(grad, length):
    row = lax.broadcasted_iota(jnp.int32, grad.shape, 0)
    return jnp.where(row < length, grad, jnp.zeros_like(grad))


def causal(shape):
    return lax.broadcasted_iota(jnp.int32, shape, 0) <= lax.broadcasted_iota(jnp.int32, shape, 1)


def pack_kernel(scale, per_step, slot_ref, length_ref, q_ref, g_ref, k_ref, v_ref, send_ref):
    rows = q_ref.shape[1]
    step = pl.program_id(0)
    for j in range(per_step):
        slot = slot_ref[step * per_step + j]
        query = q_ref[slot]
        grad = live_rows(g_ref[slot], length_ref[slot])
        scores = dot(k_ref[slot], query, NT) * scale
        scores = jnp.where(causal(scores.shape), scores, -1e30)
        top = jnp.max(scores, axis=0, keepdims=True)
        exps = jnp.exp2(scores - top)
        total = jnp.sum(exps, axis=0, keepdims=True)
        grad_prob = dot(v_ref[slot], grad, NT)
        row_sum = jnp.sum(exps * grad_prob, axis=0, keepdims=True) / total
        send_ref[j, 0:rows, :] = query
        send_ref[j, rows : 2 * rows, :] = grad
        send_ref[j, 2 * rows :, :] = pack_rows(top + jnp.log2(total), row_sum)


def pack(slots, lengths, queries, grads, keys, values, scale):
    items = slots.shape[0]
    count, rows, dim = queries.shape
    per_step = 8
    whole = pl.BlockSpec((count, rows, dim), lambda i, a, b: (0, 0, 0))
    return pl.pallas_call(
        functools.partial(pack_kernel, scale, per_step),
        out_shape=jax.ShapeDtypeStruct((items, 2 * rows + STAT, dim), BF16),
        grid_spec=pltpu.PrefetchScalarGridSpec(
            num_scalar_prefetch=2,
            grid=(items // per_step,),
            in_specs=[whole] * 4,
            out_specs=pl.BlockSpec((per_step, 2 * rows + STAT, dim), lambda i, a, b: (i, 0, 0)),
        ),
    )(slots, lengths, queries, grads, keys, values)


def holder_kernel(scale, factor, item_ref, a_ref, b_ref, k_ref, v_ref, out_ref, stat_ref, dk_ref, dv_ref, kt, vt):
    step = pl.program_id(1)

    @pl.when(step == 0)
    def _():
        kt[...] = jnp.transpose(k_ref[0])
        vt[...] = jnp.transpose(v_ref[0])
        dk_ref[...] = jnp.zeros_like(dk_ref)
        dv_ref[...] = jnp.zeros_like(dv_ref)

    half = a_ref.shape[1]
    rows = (half - STAT) // 2
    query = jnp.concatenate([a_ref[0, 0:rows, :], b_ref[0, 0:rows, :]], axis=0)
    grad = jnp.concatenate([a_ref[0, rows : 2 * rows, :], b_ref[0, rows : 2 * rows, :]], axis=0)
    lse_a, sum_a = unpack_rows(a_ref[0, 2 * rows :, :])
    lse_b, sum_b = unpack_rows(b_ref[0, 2 * rows :, :])
    resp_lse = jnp.concatenate([lse_a, lse_b], axis=1)
    resp_sum = jnp.concatenate([sum_a, sum_b], axis=1)
    scores = dot(k_ref[0], query, NT) * scale
    grad_prob = dot(v_ref[0], grad, NT)
    top = jnp.max(scores, axis=0, keepdims=True)
    exps = jnp.exp2(scores - top)
    total = jnp.sum(exps, axis=0, keepdims=True)
    row_sum = jnp.sum(exps * grad_prob, axis=0, keepdims=True)
    prefix_lse = top + jnp.log2(total)
    high = jnp.maximum(prefix_lse, resp_lse)
    lse = high + jnp.log2(jnp.exp2(prefix_lse - high) + jnp.exp2(resp_lse - high))
    weight = jnp.exp2(prefix_lse - lse) / total
    delta = weight * row_sum + jnp.exp2(resp_lse - lse) * resp_sum
    prob = exps * weight
    dscore = (prob * (grad_prob - delta)).astype(BF16)
    prob = prob.astype(BF16)
    dk_ref[0] += dot(dscore, query, NN) * factor
    dv_ref[0] += dot(prob, grad, NN)
    out = jnp.transpose(dot(vt[...], prob, NN)).astype(BF16)
    dq = jnp.transpose(dot(kt[...], dscore, NN) * factor).astype(BF16)
    for j in range(2):
        part = slice(j * rows, (j + 1) * rows)
        out_ref[j, 0:rows, :] = out[part]
        out_ref[j, rows:, :] = dq[part]
        stat_ref[j] = pack_rows(lse[:, part], delta[:, part])


def holder(items, received, keys, values, scale, factor):
    count, height, dim = received.shape
    held, length, _ = keys.shape
    rows = (height - STAT) // 2
    steps = FANOUT // 2
    slot = lambda k: pl.BlockSpec((1, height, dim), lambda p, j, ids: (ids[p * FANOUT + 2 * j + k], 0, 0))
    whole = pl.BlockSpec((1, length, dim), lambda p, j, ids: (p, 0, 0))
    return pl.pallas_call(
        functools.partial(holder_kernel, scale, factor),
        out_shape=(
            jax.ShapeDtypeStruct((held * FANOUT, 2 * rows, dim), BF16),
            jax.ShapeDtypeStruct((held * FANOUT, STAT, dim), BF16),
            jax.ShapeDtypeStruct((held, length, dim), F32),
            jax.ShapeDtypeStruct((held, length, dim), F32),
        ),
        grid_spec=pltpu.PrefetchScalarGridSpec(
            num_scalar_prefetch=1,
            grid=(held, steps),
            in_specs=[slot(0), slot(1), whole, whole],
            out_specs=(
                pl.BlockSpec((2, 2 * rows, dim), lambda p, j, ids: (p * steps + j, 0, 0)),
                pl.BlockSpec((2, STAT, dim), lambda p, j, ids: (p * steps + j, 0, 0)),
                whole,
                whole,
            ),
            scratch_shapes=[pltpu.VMEM((dim, length), BF16)] * 2,
        ),
    )(items, received, received, keys, values)


def local_kernel(
    scale, factor, per_step, fetch_ref, prompt_ref, length_ref, stat_ref, q_ref, g_ref, k_ref, v_ref, out_ref, dq_ref, dkv_ref
):
    step = pl.program_id(0)
    for j in range(per_step):
        slot = step * per_step + j
        live = prompt_ref[slot] >= 0
        lse, delta = unpack_rows(stat_ref[fetch_ref[slot]])
        lse = jnp.where(live, lse, 1e30)
        delta = jnp.where(live, delta, 0.0)
        query = q_ref[j]
        grad = live_rows(g_ref[j], length_ref[slot])
        scores = dot(k_ref[j], query, NT) * scale
        mask = causal(scores.shape)
        prob = jnp.where(mask, jnp.exp2(jnp.where(mask, scores, -1e30) - lse), 0.0)
        grad_prob = dot(v_ref[j], grad, NT)
        dscore = (prob * (grad_prob - delta)).astype(BF16)
        prob = prob.astype(BF16)
        dkv_ref[0, j] = dot(dscore, query, NN) * factor
        dkv_ref[1, j] = dot(prob, grad, NN)
        out_ref[j] = dot(prob, v_ref[j], TN).astype(BF16)
        dq_ref[j] = (dot(dscore, k_ref[j], TN) * factor).astype(BF16)


def local(fetch, prompts, lengths, stats, queries, grads, keys, values, scale, factor):
    count, rows, dim = queries.shape
    per_step = 5
    some = pl.BlockSpec((per_step, rows, dim), lambda i, a, b, c: (i, 0, 0))
    return pl.pallas_call(
        functools.partial(local_kernel, scale, factor, per_step),
        out_shape=(
            jax.ShapeDtypeStruct((count, rows, dim), BF16),
            jax.ShapeDtypeStruct((count, rows, dim), BF16),
            jax.ShapeDtypeStruct((2, count, rows, dim), F32),
        ),
        grid_spec=pltpu.PrefetchScalarGridSpec(
            num_scalar_prefetch=3,
            grid=(count // per_step,),
            in_specs=[pl.BlockSpec(stats.shape, lambda i, a, b, c: (0, 0, 0)), some, some, some, some],
            out_specs=(some, some, pl.BlockSpec((2, per_step, rows, dim), lambda i, a, b, c: (0, i, 0, 0))),
        ),
    )(fetch, prompts, lengths, stats, queries, grads, keys, values)


def merge_kernel(per_step, fetch_ref, prompt_ref, length_ref, *refs):
    back_refs = refs[:per_step]
    out_part, dq_part, out_ref, dq_ref = refs[per_step:]
    rows = out_part.shape[1]
    step = pl.program_id(0)
    for j in range(per_step):
        slot = step * per_step + j
        live = prompt_ref[slot] >= 0
        row = lax.broadcasted_iota(jnp.int32, out_part.shape[1:], 0)
        back = back_refs[j]
        out = back[0, 0:rows, :].astype(F32) + out_part[j].astype(F32)
        dq = back[0, rows : 2 * rows, :].astype(F32) + dq_part[j].astype(F32)
        length = jnp.where(live, length_ref[slot], 0)
        out_ref[j] = jnp.where(row < length, out, 0.0).astype(BF16)
        dq_ref[j] = jnp.where(row < length, dq, 0.0).astype(BF16)


def merge(fetch, prompts, lengths, back, out_part, dq_part):
    count, rows, dim = out_part.shape
    per_step = 8
    some = pl.BlockSpec((per_step, rows, dim), lambda i, a, b, c: (i, 0, 0))

    def one(j):
        return pl.BlockSpec((1, 2 * rows, dim), lambda i, a, b, c: (a[i * per_step + j], 0, 0))

    return pl.pallas_call(
        functools.partial(merge_kernel, per_step),
        out_shape=(jax.ShapeDtypeStruct((count, rows, dim), BF16),) * 2,
        grid_spec=pltpu.PrefetchScalarGridSpec(
            num_scalar_prefetch=3,
            grid=(count // per_step,),
            in_specs=[one(j) for j in range(per_step)] + [some, some],
            out_specs=(some, some),
        ),
    )(fetch, prompts, lengths, *([back] * per_step), out_part, dq_part)


def exchange(value):
    count = lax.axis_size("dp")
    shaped = value.reshape((count, -1) + value.shape[2:])
    return lax.all_to_all(shaped, "dp", split_axis=0, concat_axis=0, tiled=True).reshape(value.shape)


def body(queries, resp_keys, resp_values, prompt_keys, prompt_values, grad_out, slot_prompt, slot_length):
    dp_count = lax.axis_size("dp")
    slot_count, resp_len, dim = queries.shape
    held_count, prompt_len, _ = prompt_keys.shape
    factor = dim ** (-0.5)
    scale = factor * LOG2E
    pair_limit = max(2, FANOUT * held_count // dp_count)
    item_count = dp_count * pair_limit
    slot_ids = jnp.arange(slot_count, dtype=jnp.int32)
    item_ids = jnp.arange(item_count, dtype=jnp.int32)
    holder_own = jnp.where(slot_prompt >= 0, slot_prompt // held_count, -1)
    before = slot_ids[None, :] < slot_ids[:, None]
    order_own = jnp.sum((holder_own[:, None] == holder_own[None, :]) & before, axis=1, dtype=jnp.int32)
    target = jnp.where(holder_own >= 0, holder_own * pair_limit + order_own, -1)
    fetch = jnp.maximum(target, 0)
    send_hit = target[None, :] == item_ids[:, None]
    send_slot = jnp.sum(jnp.where(send_hit, slot_ids[None, :], 0), axis=1, dtype=jnp.int32)
    send_prompt = jnp.sum(jnp.where(send_hit, (slot_prompt % held_count)[None, :] + 1, 0), axis=1, dtype=jnp.int32) - 1
    item_prompt = exchange(send_prompt.reshape(item_count, 1)).reshape(item_count)
    earlier = item_ids[None, :] < item_ids[:, None]
    order_in = jnp.sum((item_prompt[:, None] == item_prompt[None, :]) & earlier, axis=1, dtype=jnp.int32)
    place = jnp.where(item_prompt >= 0, item_prompt * FANOUT + order_in, -1)
    group_ids = jnp.arange(held_count * FANOUT, dtype=jnp.int32)
    group_hit = place[None, :] == group_ids[:, None]
    group_item = jnp.sum(jnp.where(group_hit, item_ids[None, :], 0), axis=1, dtype=jnp.int32)
    back_index = jnp.maximum(place, 0)

    packed = pack(send_slot, slot_length, queries, grad_out, resp_keys, resp_values, scale)
    received = exchange(packed)
    result, stats, prefix_dk, prefix_dv = holder(group_item, received, prompt_keys, prompt_values, scale, factor)
    back_stats = exchange(stats[back_index])
    back = exchange(result[back_index])
    local_out, local_dq, local_dkv = local(
        fetch, slot_prompt, slot_length, back_stats, queries, grad_out, resp_keys, resp_values, scale, factor
    )
    attn_out, grad_queries = merge(fetch, slot_prompt, slot_length, back, local_out, local_dq)
    grad_prompt_keys, grad_prompt_values = lax.psum((prefix_dk, prefix_dv), "head")
    shared = lax.psum_scatter(local_dkv, "head", scatter_dimension=2, tiled=True)
    return (attn_out, grad_queries, shared[0], shared[1], grad_prompt_keys, grad_prompt_values)


def solution(mesh):
    return jax.shard_map(
        body,
        mesh=mesh,
        in_specs=(
            P("dp", None, "head"),
            P("dp", None, None),
            P("dp", None, None),
            P("dp", None, None),
            P("dp", None, None),
            P("dp", None, "head"),
            P("dp"),
            P("dp"),
        ),
        out_specs=(
            P("dp", None, "head"),
            P("dp", None, "head"),
            P("dp", "head", None),
            P("dp", "head", None),
            P("dp", None, None),
            P("dp", None, None),
        ),
        check_vma=False,
    )
```

time: 368 us -> 300 us (0.82)
  matrix products: 52.6 us -> 0 us
  Pallas kernels: 0 us -> 48.9 us
  local copies, waits for them, and re-layouts: 57 us -> 13.1 us
  other arithmetic: 22.1 us -> 3.59 us
  starting transfers between devices: 38.6 us -> 20.7 us
  blocking collectives: 0 us -> 16.1 us
    dot_general x34 -> x0, matrix products: 52.6 us -> none  [the longest x1 7.8 us: response_forward(): jnp.einsum('shtu,sud->sthd', exp_terms.astype(jnp.bfloat16), value_rows,...]
    pallas_call x0 -> x4, Pallas kernels: none -> 48.9 us  [the longest x1 18.8 us: holder(): pl.pallas_call(functools.partial(holder_kernel, scale, factor), out_shape...]
    psum x1, waiting for transfers between devices: 47.2 us -> 74.2 us  [body(): lax.psum((prefix_dk, prefix_dv), 'head')]
    all_to_all x6 -> x3, waiting for transfers between devices: 130 us -> 104 us  [exchange(): lax.all_to_all(shaped, 'dp', split_axis=0, concat_axis=0, tiled=True)]
    gather x14 -> x2, local copies, waits for them, and re-layouts: 27 us -> 4.69 us  [the longest x1 3.15 us: body(): back = exchange(result[back_index])]
    all_to_all x6 -> x3, starting transfers between devices: 38.4 us -> 20.7 us  [exchange(): lax.all_to_all(shaped, 'dp', split_axis=0, concat_axis=0, tiled=True)]
    all_to_all x0 -> x1, blocking collectives: none -> 16.1 us  [exchange(): lax.all_to_all(shaped, 'dp', split_axis=0, concat_axis=0, tiled=True)]
    select_n x11 -> x1, other arithmetic: 11.4 us -> 0.01 us  [body(): place = jnp.where(item_prompt >= 0, item_prompt * FANOUT + order_in, -1)]
  transfers between devices with their start and end apart: 8 -> 5, of which waited for: 6 -> 3; matrix products, arithmetic and copies ran while one was open for 19% -> 3% of each run, Pallas kernels for 0% -> 5%
where the time goes in v1:
time: 300 us; the launch traced here: 295 us
  waiting for transfers between devices  179 us (60%)
  Pallas kernels  48.9 us (16%)
  starting transfers between devices  20.7 us (7%)
  blocking collectives  16.1 us (5%)
  between operations  14.1 us (5%)
  local copies, waits for them, and re-layouts  13.1 us (4%)
  other arithmetic  3.59 us (1%)
    all_to_all x3, waiting for transfers between devices, exchange(): lax.all_to_all(shaped, 'dp', split_axis=0, concat_axis=0, tiled=True)  104 us
    psum x1, waiting for transfers between devices, body(): lax.psum((prefix_dk, prefix_dv), 'head')  74.2 us
    all_to_all x3, starting transfers between devices, exchange(): lax.all_to_all(shaped, 'dp', split_axis=0, concat_axis=0, tiled=True)  20.7 us
    pallas_call x1, Pallas kernels, holder(): pl.pallas_call(functools.partial(holder_kernel, scale, factor), out_shape...  18.8 us
    all_to_all x1, blocking collectives, exchange(): lax.all_to_all(shaped, 'dp', split_axis=0, concat_axis=0, tiled=True)  16.1 us
    pallas_call x1, Pallas kernels, local(): pl.pallas_call(functools.partial(local_kernel, scale, factor, per_step),...  14.3 us
    pallas_call x1, Pallas kernels, pack(): pl.pallas_call(functools.partial(pack_kernel, scale, per_step), out_shape...  9.25 us
    pallas_call x1, Pallas kernels, merge(): pl.pallas_call(functools.partial(merge_kernel, per_step), out_shape=(jax....  6.52 us
  transfers between devices with their start and end apart: 5, of which 3 were waited for; matrix products, arithmetic and copies ran while one was open for 3% of the time, Pallas kernels for 5%

profile of v1, /device:TPU:1, one launch (start us, length us, event | category | flops | bytes accessed | tf_op | source)
XLA Modules:
  0.0 295.5 jit_solution(5819464872317135292)
XLA Ops:
  7.2 0.7 fusion.2
  7.8 0.2 convert_reduce_fusion.1
  8.0 0.5 broadcast_maximum_fusion
  8.5 0.6 select_reduce_fusion
  9.1 0.7 sub.14
  9.9 8.6 %all-to-all-start = ((s32[32,1,2]{2,1,0:T(1,128)}), s32[32,1,2]{2,1,0:T(1,128)S(1)}, u32[]{:S(2)}, u32[]{:S(2)}) async-start(s32[32,1,2]{2,1,0:T(1,128)} %bitcast), calls=%async_computation | async-start | bytes 32768 | tf_op jit(solution)/shard_map/all_to_all | solution.py:249
  18.4 9.3 %shard_map.127 = bf16[64,272,128]{2,1,0:T(8,128)(2,1)} custom-call(s32[64]{0:T(128)} %get-tuple-element.26.slot_ref, s32[40]{0:T(128)} %length_ref.5, bf16[40,128,128]{2,1,0:T(8,128)(2,1)} %q_ref.3, bf16[40,128,128]{2,1,0:T(8,128)(2,1)} %g_ref.3, bf16[40,128,128]{2,1,0:T(8,128)(2,1)} %k_ref.5, bf16[40,128,128]{2,1,0:T(8,128)(2,1)} %v_ref.5), custom_call_target="tpu_custom_call" | custom-call | tf_op jit(solution)/shard_map/pallas_call | solution.py:80
  27.7 0.0 all-to-all-done
  27.7 7.4 %all-to-all-start.1 = ((bf16[32,544,128]{2,1,0:T(8,128)(2,1)}), bf16[32,544,128]{2,1,0:T(8,128)(2,1)}, u32[]{:S(2)}, u32[]{:S(2)}) async-start(bf16[32,544,128]{2,1,0:T(8,128)(2,1)} %bitcast.21), calls=%async_computation.1 | async-start | bytes 8912896 | tf_op jit(solution)/shard_map/all_to_all | solution.py:249
  35.1 0.0 reduce-scatter.2.cloned.1.call-start
  35.2 0.1 compare_reduce_fusion
  35.2 0.1 ge.29
  35.4 0.5 broadcast.125
  35.9 0.7 multiply_reduce_fusion
  36.6 0.1 mul.33
  36.7 0.1 reshape_reshape.4
  36.8 0.2 convert_reduce_fusion
  37.0 0.6 select_reduce_fusion.2.item_ref
  37.7 52.7 %all-to-all-done.1 = bf16[32,544,128]{2,1,0:T(8,128)(2,1)} async-done(((bf16[32,544,128]{2,1,0:T(8,128)(2,1)}), bf16[32,544,128]{2,1,0:T(8,128)(2,1)}, u32[]{:S(2)}, u32[]{:S(2)}) %all-to-all-start.1) | async-done | bytes 4456480 | tf_op jit(solution)/shard_map/all_to_all | solution.py:249
  90.4 18.8 %shard_map.128 = (bf16[32,256,128]{2,1,0:T(8,128)(2,1)}, bf16[32,16,128]{2,1,0:T(8,128)(2,1)}, f32[4,512,128]{2,1,0:T(8,128)}, f32[4,512,128]{2,1,0:T(8,128)}) custom-call(s32[32]{0:T(128)} %select_reduce_fusion.2.item_ref, bf16[64,272,128]{2,1,0:T(8,128)(2,1)} %bitcast.2.a_ref.b_ref, bf16[64,272,128]{2,1,0:T(8,128)(2,1)} %bitcast.2.a_ref.b_ref, ...), custom_call_target="tpu_custom_call" | custom-call | tf_op jit(solution)/shard_map/pallas_call | solution.py:142
  109.2 1.5 gather_fusion.1
  110.7 16.1 %all_to_all.21 = bf16[32,32,128]{2,1,0:T(8,128)(2,1)} all-to-all(bf16[32,32,128]{2,1,0:T(8,128)(2,1)S(1)} %bitcast.24), channel_id=1, replica_groups=mesh['dp'=32,'head'=8] {'dp'}, dimensions={0} | all-to-all | bytes 524288 | tf_op jit(solution)/shard_map/all_to_all | solution.py:249
  126.8 14.3 %shard_map.129 = (bf16[40,128,128]{2,1,0:T(8,128)(2,1)}, bf16[40,128,128]{2,1,0:T(8,128)(2,1)}, f32[2,40,128,128]{3,2,1,0:T(8,128)}) custom-call(s32[40]{0:T(128)} %get-tuple-element.30.fetch_ref, s32[40]{0:T(128)} %prompt_ref.3, s32[40]{0:T(128)} %length_ref.5, bf16[64,16,128]{2,1,0:T(8,128)(2,1)} %bitcast.23, bf16[40,128,128]{2,1,0:T(8,128)(2,1)} %q_ref.3, ...), custom_call_target="tpu_custom_call" | custom-call | tf_op jit(solution)/shard_map/pallas_call | solution.py:193
  141.1 0.0 copy-start
  141.1 0.0 reduce-scatter.2.cloned.1.call-update
  141.1 1.6 copy-done
  142.7 3.2 %gather_fusion = bf16[64,256,128]{2,1,0:T(8,128)(2,1)} fusion(bf16[32,256,128]{2,1,0:T(8,128)(2,1)S(1)} %copy-done, s32[1024]{0:T(1024)S(1)} %pad_clamp_fusion), kind=kCustom, calls=%fused_computation | custom fusion | bytes 8388864 | tf_op jit(solution)/shard_map/gather | solution.py:283
  145.8 4.7 %all-to-all-start.2 = ((bf16[32,512,128]{2,1,0:T(8,128)(2,1)}), bf16[32,512,128]{2,1,0:T(8,128)(2,1)}, u32[]{:S(2)}, u32[]{:S(2)}) async-start(bf16[32,512,128]{2,1,0:T(8,128)(2,1)} %bitcast.22), calls=%async_computation.2 | async-start | bytes 8388608 | tf_op jit(solution)/shard_map/all_to_all | solution.py:249
  150.5 0.0 all-reduce.3.cloned.1.call-start
  150.5 0.7 all-reduce.3.cloned.1.call-update
  151.2 51.4 %all-to-all-done.2 = bf16[32,512,128]{2,1,0:T(8,128)(2,1)} async-done(((bf16[32,512,128]{2,1,0:T(8,128)(2,1)}), bf16[32,512,128]{2,1,0:T(8,128)(2,1)}, u32[]{:S(2)}, u32[]{:S(2)}) %all-to-all-start.2) | async-done | bytes 4194336 | tf_op jit(solution)/shard_map/all_to_all | solution.py:249
  202.7 6.5 %shard_map.130 = (bf16[40,128,128]{2,1,0:T(8,128)(2,1)}, bf16[40,128,128]{2,1,0:T(8,128)(2,1)}) custom-call(s32[40]{0:T(128)} %get-tuple-element.30.fetch_ref, s32[40]{0:T(128)} %prompt_ref.3, s32[40]{0:T(128)} %length_ref.5, bf16[64,256,128]{2,1,0:T(8,128)(2,1)} %bitcast.6.refs_0_.refs_1_.refs_2_.refs_3_.refs_4_.refs_5_.refs_6_.refs_7_, ...), custom_call_target="tpu_custom_call" | custom-call | tf_op jit(solution)/shard_map/pallas_call | solution.py:234
  209.2 0.0 reduce-scatter.2.cloned.1.call-done
  209.2 1.9 slice_bitcast_fusion
  211.2 74.2 %all-reduce.3.cloned.1.call-done = (f32[4,512,128]{2,1,0:T(8,128)}, f32[4,512,128]{2,1,0:T(8,128)}) async-done(((f32[4,512,128]{2,1,0:T(8,128)}, f32[4,512,128]{2,1,0:T(8,128)}), (f32[4,512,128]{2,1,0:T(8,128)}, f32[4,512,128]{2,1,0:T(8,128)})) %all-reduce.3.cloned.1.call-update) | async-done | bytes 2097168 | tf_op jit(solution)/shard_map/psum | solution.py:288
  285.3 0.0 copy-start.1
  285.3 2.4 copy.18
  287.7 0.0 copy-done.1
  287.7 1.0 copy.19
  (4 shorter events, 0.0 us)
Async XLA Ops:
  9.9 17.8 %all-to-all-start = ((s32[32,1,2]{2,1,0:T(1,128)}), s32[32,1,2]{2,1,0:T(1,128)S(1)}, u32[]{:S(2)}, u32[]{:S(2)}) async-start(s32[32,1,2]{2,1,0:T(1,128)} %bitcast), calls=%async_computation | async-start | bytes 32768 | tf_op jit(solution)/shard_map/all_to_all | solution.py:249
  27.7 62.7 %all-to-all-start.1 = ((bf16[32,544,128]{2,1,0:T(8,128)(2,1)}), bf16[32,544,128]{2,1,0:T(8,128)(2,1)}, u32[]{:S(2)}, u32[]{:S(2)}) async-start(bf16[32,544,128]{2,1,0:T(8,128)(2,1)} %bitcast.21), calls=%async_computation.1 | async-start | bytes 8912896 | tf_op jit(solution)/shard_map/all_to_all | solution.py:249
  35.1 174.1 %reduce-scatter.2.cloned.1.call-start = ((), (), s32[]{:S(2)}) async-start(), calls=%async_computation.5 | async-start | bytes 5898240 | tf_op jit(solution)/shard_map/reduce_scatter | solution.py:289
  141.1 1.6 copy-start
  145.8 56.8 %all-to-all-start.2 = ((bf16[32,512,128]{2,1,0:T(8,128)(2,1)}), bf16[32,512,128]{2,1,0:T(8,128)(2,1)}, u32[]{:S(2)}, u32[]{:S(2)}) async-start(bf16[32,512,128]{2,1,0:T(8,128)(2,1)} %bitcast.22), calls=%async_computation.2 | async-start | bytes 8388608 | tf_op jit(solution)/shard_map/all_to_all | solution.py:249
  150.5 134.8 %all-reduce.3.cloned.1.call-start = ((), (), s32[]{:S(2)}) async-start(), calls=%async_computation.6 | async-start | bytes 4194304 | tf_op jit(solution)/shard_map/psum | solution.py:288
  285.3 2.4 copy-start.1
Sparse Core Ops, SparseCore 0:
  141.2 64.0 reduce-scatter.1
  208.3 76.9 all-reduce.2

commit v2 on v1

v2 whole, which is shorter than its diff:
```python
import functools
import math

import jax
import jax.numpy as jnp
from jax import lax
from jax.experimental import pallas as pl
from jax.experimental.pallas import tpu as pltpu
from jax.sharding import PartitionSpec as P

FANOUT = 8
LOG2E = math.log2(math.e)
F32 = jnp.float32
BF16 = jnp.bfloat16
STAT = 16


MESH = pl.DeviceIdType.MESH
SIDE = 4

def place():
    me = lax.axis_index("dp")
    core = lax.rem(me, 2)
    y = lax.rem(me // 2, SIDE)
    x = me // (2 * SIDE)
    return x, y, core

def device(k, a, b, core):
    x, y = (a, b) if k == 0 else (b, a)
    return {"dp": (x * SIDE + y) * 2 + core}

def step_by(value, by):
    return lax.rem(value + by + SIDE, SIDE)

def neighbours():
    x, y, core = place()
    out = [device(0, x, y, 1 - core)]
    for by in (1, -1):
        for c in range(2):
            out.append(device(0, step_by(x, by), y, c))
            out.append(device(0, x, step_by(y, by), c))
    return out

def everyone():
    x, y, core = place()
    me = (x * SIDE + y) * 2 + core
    return [{"dp": lax.rem(me + k, 2 * SIDE * SIDE)} for k in range(1, 2 * SIDE * SIDE)]


def greet(near):
    barrier = pltpu.get_barrier_semaphore()
    for who in near:
        pl.semaphore_signal(barrier, inc=1, device_id=who, device_id_type=MESH)
    pl.semaphore_wait(barrier, len(near))

def remote(src, dst, send, recv, who):
    return pltpu.make_async_remote_copy(src_ref=src, dst_ref=dst, send_sem=send, recv_sem=recv, device_id=who, device_id_type=MESH)

class Route:
    def __init__(self, k, send, final, mid, rel1, rel2, sems):
        self.k, self.send, self.final, self.mid, self.rel1, self.rel2 = k, send, final, mid, rel1, rel2
        x, y, self.c = place()
        self.a, self.b = (x, y) if k == 0 else (y, x)
        (self.s1, self.r1, self.s1d, self.r1d, self.s1f, self.r1f,
         self.s2, self.r2, self.s2d, self.r2d, self.s2f, self.r2f, self.s0, self.r0, self.local) = sems
    def to_a(self, by): return device(self.k, step_by(self.a, by), self.b, self.c)
    def to_b(self, by, c): return device(self.k, self.a, step_by(self.b, by), c)
    def first_direct(self, side, j):
        by = 1 if side == 0 else -1
        b = step_by(self.b, j)
        r = 3 if side == 0 else 1
        return remote(self.send.at[step_by(self.a, by), b], self.mid.at[r - 1, b], self.s1.at[side, j], self.r1.at[side, j], self.to_a(by))
    def first_far(self, side, j):
        by = 1 if side == 0 else -1
        b = 2 * side + j
        return remote(self.send.at[step_by(self.a, 2), b], self.rel1.at[side, j], self.s1d.at[side, j], self.r1d.at[side, j], self.to_a(by))
    def first_forward(self, side, j):
        by = 1 if side == 0 else -1
        b = 2 * side + j
        return remote(self.rel1.at[side, j], self.mid.at[1, b], self.s1f.at[side, j], self.r1f.at[side, j], self.to_a(by))
    def source(self, r, b):
        return self.send.at[self.a, b] if r == 0 else self.mid.at[r - 1, b]
    def second_direct(self, r, side, c):
        by = 1 if side == 0 else -1
        rb = 3 if side == 0 else 1
        return remote(self.source(r, step_by(self.b, by)).at[c], self.final.at[r, rb, self.c], self.s2.at[r, side, c], self.r2.at[r, side, self.c], self.to_b(by, c))
    def second_far(self, r):
        side = r // 2
        by = 1 if side == 0 else -1
        return remote(self.source(r, step_by(self.b, 2)), self.rel2.at[side, r % 2], self.s2d.at[r], self.r2d.at[r], self.to_b(by, self.c))
    def second_forward(self, r, c):
        side = r // 2
        by = 1 if side == 0 else -1
        return remote(self.rel2.at[side, r % 2, c], self.final.at[r, 2, self.c], self.s2f.at[r, c], self.r2f.at[r, self.c], self.to_b(by, c))
    def cross(self, r):
        return remote(self.source(r, self.b).at[1 - self.c], self.final.at[r, 0, self.c], self.s0.at[r], self.r0.at[r], self.to_b(0, 1 - self.c))
    def own(self, r):
        return pltpu.make_async_copy(self.source(r, self.b).at[self.c], self.final.at[r, 0, self.c], self.local.at[r])

def wait_second_direct(route, r, side):
    for c in range(2):
        by = 1 if side == 0 else -1
        rb = 3 if side == 0 else 1
        d = route.final.at[r, rb, c]
        remote(d, d, route.s2.at[r, side, c], route.r2.at[r, side, c], route.to_b(by, c)).wait_recv()

def wait_second_forward(route, r):
    side = r // 2
    by = 1 if side == 0 else -1
    for c in range(2):
        d = route.final.at[r, 2, c]
        remote(d, d, route.s2f.at[r, c], route.r2f.at[r, c], route.to_b(by, c)).wait_recv()

def wait_cross(route, r):
    d = route.final.at[r, 0, 1 - route.c]
    remote(d, d, route.s0.at[r], route.r0.at[r], route.to_b(0, 1 - route.c)).wait_recv()

def route_sems():
    D = pltpu.SemaphoreType.DMA
    return [D((2, 4)), D((2, 4)), D((2, 2)), D((2, 2)), D((2, 2)), D((2, 2)),
            D((4, 2, 2)), D((4, 2, 2)), D((4,)), D((4,)), D((4, 2)), D((4, 2)), D((4,)), D((4,)), D((4,))]

def route_scratch(height, dim, dtype):
    V = pltpu.VMEM
    return [V((3, 4, 2, height, dim), dtype), V((2, 2, 2, height, dim), dtype), V((2, 2, 2, height, dim), dtype)]

def stages(routes):
    started = []
    def go(copy):
        copy.start(); started.append(copy)
    def second(route, r):
        go(route.second_far(r))
        for side in range(2):
            for c in range(2):
                go(route.second_direct(r, side, c))
        go(route.cross(r)); go(route.own(r))
    def s0():
        for j in range(2):
            for side in range(2):
                for route in routes: go(route.first_far(side, j))
        for route in routes: second(route, 0)
        for j in (2, 1, 3, 0):
            for side in range(2):
                for route in routes: go(route.first_direct(side, j))
    def s1():
        for j in range(2):
            for side in range(2):
                for route in routes:
                    route.first_far(side, j).wait_recv()
                    go(route.first_forward(side, j))
    def relay(route, r):
        route.second_far(r).wait_recv()
        for c in range(2): go(route.second_forward(r, c))
    def s2():
        for route in routes: relay(route, 0)
    def s3():
        for side in range(2):
            r = 3 if side == 0 else 1
            for route in routes:
                for j in range(4): route.first_direct(side, j).wait_recv()
                second(route, r)
    def s4():
        for route in routes:
            for side in range(2):
                for j in range(2): route.first_forward(side, j).wait_recv()
            second(route, 2)
    def s5():
        for r in (3, 1, 2):
            for route in routes: relay(route, r)
    def s6():
        for r in (0, 3, 1, 2):
            for route in routes:
                for side in range(2): wait_second_direct(route, r, side)
                wait_second_forward(route, r); wait_cross(route, r)
    def s7():
        for copy in started:
            if copy.is_remote: copy.wait_send()
            else: copy.wait()
    return [s0, s1, s2, s3, s4, s5, s6, s7]

def exchange_kernel(send_ref, final_ref, *scratch):
    greet(neighbours())
    n = 3 + 15
    routes = []
    for k in range(2):
        part = scratch[k * n:(k + 1) * n]
        routes.append(Route(k, send_ref.at[k], final_ref.at[k], part[0], part[1], part[2], part[3:]))
    for stage in stages(routes): stage()

def torus_exchange(send, cid):
    h, d = send.shape[-2:]
    scratch = []
    for _ in range(2): scratch += route_scratch(h, d, send.dtype) + route_sems()
    return pl.pallas_call(exchange_kernel, out_shape=jax.ShapeDtypeStruct(send.shape, send.dtype),
        in_specs=[pl.BlockSpec(memory_space=pl.ANY)], out_specs=pl.BlockSpec(memory_space=pl.ANY),
        scratch_shapes=scratch, compiler_params=pltpu.CompilerParams(collective_id=cid, has_side_effects=True))(send)


def dot(a, b, dims):
    return lax.dot_general(a, b, (dims, ((), ())), preferred_element_type=F32)


NT = ((1,), (1,))
NN = ((1,), (0,))
TN = ((0,), (0,))


def two_parts(value):
    high = value.astype(BF16)
    low = (value - high.astype(F32)).astype(BF16)
    return high.astype(F32), low.astype(F32)


def pack_rows(first, second, third=0.0):
    width = first.shape[1]
    rows = lax.broadcasted_iota(jnp.int32, (STAT, width), 0)
    a, b = two_parts(first)
    c, d = two_parts(second)
    packed = jnp.where(rows == 0, a, jnp.where(rows == 1, b, jnp.where(rows == 2, c, d)))
    return jnp.where(rows < 4, packed, third).astype(BF16)


def unpack_rows(packed):
    rows = packed.astype(F32)
    return rows[0:1] + rows[1:2], rows[2:3] + rows[3:4]


def live_rows(grad, length):
    row = lax.broadcasted_iota(jnp.int32, grad.shape, 0)
    return jnp.where(row < length, grad, jnp.zeros_like(grad))


def causal(shape):
    return lax.broadcasted_iota(jnp.int32, shape, 0) <= lax.broadcasted_iota(jnp.int32, shape, 1)


def pack_kernel(scale, per_step, slot_ref, prompt_ref, length_ref, q_ref, g_ref, k_ref, v_ref, send_ref):
    rows = q_ref.shape[1]
    step = pl.program_id(0)
    for j in range(per_step):
        slot = slot_ref[step * per_step + j]
        query = q_ref[slot]
        grad = live_rows(g_ref[slot], length_ref[slot])
        scores = dot(k_ref[slot], query, NT) * scale
        scores = jnp.where(causal(scores.shape), scores, -1e30)
        top = jnp.max(scores, axis=0, keepdims=True)
        exps = jnp.exp2(scores - top)
        total = jnp.sum(exps, axis=0, keepdims=True)
        grad_prob = dot(v_ref[slot], grad, NT)
        row_sum = jnp.sum(exps * grad_prob, axis=0, keepdims=True) / total
        send_ref[j, 0:rows, :] = query
        send_ref[j, rows : 2 * rows, :] = grad
        prompt = prompt_ref[step * per_step + j].astype(F32)
        send_ref[j, 2 * rows :, :] = pack_rows(top + jnp.log2(total), row_sum, prompt)


def pack(slots, prompts, lengths, queries, grads, keys, values, scale):
    items = slots.shape[0]
    count, rows, dim = queries.shape
    per_step = 8
    whole = pl.BlockSpec((count, rows, dim), lambda i, a, b, c: (0, 0, 0))
    return pl.pallas_call(
        functools.partial(pack_kernel, scale, per_step),
        out_shape=jax.ShapeDtypeStruct((items, 2 * rows + STAT, dim), BF16),
        grid_spec=pltpu.PrefetchScalarGridSpec(
            num_scalar_prefetch=3,
            grid=(items // per_step,),
            in_specs=[whole] * 4,
            out_specs=pl.BlockSpec((per_step, 2 * rows + STAT, dim), lambda i, a, b, c: (i, 0, 0)),
        ),
    )(slots, prompts, lengths, queries, grads, keys, values)


def holder_kernel(
    scale, factor, item_ref, back_ref, stat_to_ref, a_ref, b_ref, k_ref, v_ref,
    out_ref, stat_ref, dk_ref, dv_ref, kt, vt, out_buf, stat_buf, out_sem, stat_sem,
):
    prompt, step = pl.program_id(0), pl.program_id(1)
    count = pl.num_programs(1)
    index = prompt * count + step

    @pl.when(step == 0)
    def _():
        kt[...] = jnp.transpose(k_ref[0])
        vt[...] = jnp.transpose(v_ref[0])
        dk_ref[...] = jnp.zeros_like(dk_ref)
        dv_ref[...] = jnp.zeros_like(dv_ref)

    def leaving(at, j):
        slot = lax.rem(at, 2)
        item = item_ref[2 * at + j]
        return (
            pltpu.make_async_copy(out_buf.at[slot, j], out_ref.at[back_ref[item]], out_sem.at[slot, j]),
            pltpu.make_async_copy(stat_buf.at[slot, j], stat_ref.at[stat_to_ref[item]], stat_sem.at[slot, j]),
        )

    half = a_ref.shape[1]
    rows = (half - STAT) // 2
    query = jnp.concatenate([a_ref[0, 0:rows, :], b_ref[0, 0:rows, :]], axis=0)
    grad = jnp.concatenate([a_ref[0, rows : 2 * rows, :], b_ref[0, rows : 2 * rows, :]], axis=0)
    lse_a, sum_a = unpack_rows(a_ref[0, 2 * rows :, :])
    lse_b, sum_b = unpack_rows(b_ref[0, 2 * rows :, :])
    resp_lse = jnp.concatenate([lse_a, lse_b], axis=1)
    resp_sum = jnp.concatenate([sum_a, sum_b], axis=1)
    scores = dot(k_ref[0], query, NT) * scale
    grad_prob = dot(v_ref[0], grad, NT)
    top = jnp.max(scores, axis=0, keepdims=True)
    exps = jnp.exp2(scores - top)
    total = jnp.sum(exps, axis=0, keepdims=True)
    row_sum = jnp.sum(exps * grad_prob, axis=0, keepdims=True)
    prefix_lse = top + jnp.log2(total)
    high = jnp.maximum(prefix_lse, resp_lse)
    lse = high + jnp.log2(jnp.exp2(prefix_lse - high) + jnp.exp2(resp_lse - high))
    weight = jnp.exp2(prefix_lse - lse) / total
    delta = weight * row_sum + jnp.exp2(resp_lse - lse) * resp_sum
    prob = exps * weight
    dscore = (prob * (grad_prob - delta)).astype(BF16)
    prob = prob.astype(BF16)
    dk_ref[0] += dot(dscore, query, NN) * factor
    dv_ref[0] += dot(prob, grad, NN)
    out = jnp.transpose(dot(vt[...], prob, NN)).astype(BF16)
    dq = jnp.transpose(dot(kt[...], dscore, NN) * factor).astype(BF16)

    @pl.when(index >= 2)
    def _():
        for j in range(2):
            for copy in leaving(index - 2, j):
                copy.wait()

    slot = lax.rem(index, 2)
    for j in range(2):
        part = slice(j * rows, (j + 1) * rows)
        out_buf[slot, j, 0:rows, :] = out[part]
        out_buf[slot, j, rows:, :] = dq[part]
        stat_buf[slot, j] = pack_rows(lse[:, part], delta[:, part])
        for copy in leaving(index, j):
            copy.start()

    @pl.when(index == pl.num_programs(0) * count - 1)
    def _():
        for at in (index - 1, index):
            for j in range(2):
                for copy in leaving(at, j):
                    copy.wait()


def holder(items, back_to, stat_to, received, keys, values, scale, factor):
    count, height, dim = received.shape
    held, length, _ = keys.shape
    rows = (height - STAT) // 2
    steps = FANOUT // 2

    def one(k):
        return pl.BlockSpec((1, height, dim), lambda p, j, ids, b, c: (ids[p * FANOUT + 2 * j + k], 0, 0))

    whole = pl.BlockSpec((1, length, dim), lambda p, j, ids, b, c: (p, 0, 0))
    return pl.pallas_call(
        functools.partial(holder_kernel, scale, factor),
        out_shape=(
            jax.ShapeDtypeStruct((count, 2 * rows, dim), BF16),
            jax.ShapeDtypeStruct((count, STAT, dim), BF16),
            jax.ShapeDtypeStruct((held, length, dim), F32),
            jax.ShapeDtypeStruct((held, length, dim), F32),
        ),
        grid_spec=pltpu.PrefetchScalarGridSpec(
            num_scalar_prefetch=3,
            grid=(held, steps),
            in_specs=[one(0), one(1), whole, whole],
            out_specs=(
                pl.BlockSpec(memory_space=pl.ANY),
                pl.BlockSpec(memory_space=pl.ANY),
                whole,
                whole,
            ),
            scratch_shapes=[
                pltpu.VMEM((dim, length), BF16),
                pltpu.VMEM((dim, length), BF16),
                pltpu.VMEM((2, 2, 2 * rows, dim), BF16),
                pltpu.VMEM((2, 2, STAT, dim), BF16),
                pltpu.SemaphoreType.DMA((2, 2)),
                pltpu.SemaphoreType.DMA((2, 2)),
            ],
        ),
    )(items, back_to, stat_to, received, received, keys, values)


HEADS = 8


class Ring:
    def __init__(self, own, right, left, sent, came, send_sem, recv_sem):
        self.own, self.sent, self.came, self.send_sem, self.recv_sem = own, sent, came, send_sem, recv_sem
        self.me = lax.axis_index("head")
        self.lanes = ((1, right, 0), (-1, left, right))

    def copy(self, by, at):
        who = {"head": lax.rem(self.me + by + HEADS, HEADS)}
        return remote(self.sent.at[at], self.came.at[at], self.send_sem.at[at], self.recv_sem.at[at], who)

    def step(self, number):
        for by, hops, base in self.lanes:
            if number <= hops:
                target = lax.rem(self.me + by * (hops + 1 - number) + HEADS, HEADS)
                value = self.own(target)
                at = base + number - 1
                if number > 1:
                    self.copy(by, at - 1).wait_recv()
                    value = value + self.came[at - 1].astype(F32)
                self.sent[at] = value.astype(BF16)
                self.copy(by, at).start()

    def result(self):
        value = self.own(self.me)
        for by, hops, base in self.lanes:
            at = base + hops - 1
            self.copy(by, at).wait_recv()
            value = value + self.came[at].astype(F32)
        return value

    def close(self):
        for by, hops, base in self.lanes:
            for at in range(base, base + hops):
                self.copy(by, at).wait_send()


class Spread:
    def __init__(self, all_parts, right, left, send_sem, recv_sem):
        self.all_parts, self.send_sem, self.recv_sem = all_parts, send_sem, recv_sem
        self.me = lax.axis_index("head")
        self.lanes = ((1, right, 0), (-1, left, right))

    def copy(self, by, number, base):
        whose = lax.rem(self.me - by * (number - 1) + HEADS, HEADS)
        who = {"head": lax.rem(self.me + by + HEADS, HEADS)}
        at = base + number - 1
        part = self.all_parts.at[whose]
        return remote(part, part, self.send_sem.at[at], self.recv_sem.at[at], who)

    def arrival(self, by, number, base):
        whose = lax.rem(self.me - by * number + HEADS, HEADS)
        who = {"head": lax.rem(self.me + by + HEADS, HEADS)}
        at = base + number - 1
        part = self.all_parts.at[whose]
        return remote(part, part, self.send_sem.at[at], self.recv_sem.at[at], who)

    def step(self, number):
        for by, hops, base in self.lanes:
            if number <= hops:
                if number > 1:
                    self.arrival(by, number - 1, base).wait_recv()
                self.copy(by, number, base).start()

    def close(self):
        for by, hops, base in self.lanes:
            self.arrival(by, hops, base).wait_recv()
            for number in range(1, hops + 1):
                self.copy(by, number, base).wait_send()


def return_kernel(
    scale, factor, fetch_ref, prompt_ref, length_ref,
    back_ref, stat_ref, pdk_ref, pdv_ref, q_ref, g_ref, k_ref, v_ref,
    final_ref, out_ref, dq_ref, drk_ref, drv_ref, all_k, all_v,
    q, g, k, v, pdk, pdv, dk, dv, stat_in, load_sem, stat_send, stat_recv, *scratch
):
    loads = [
        pltpu.make_async_copy(src, dst, load_sem.at[i])
        for i, (src, dst) in enumerate(
            ((pdk_ref, pdk), (pdv_ref, pdv), (q_ref, q), (g_ref, g), (k_ref, k), (v_ref, v))
        )
    ]
    for load in loads:
        load.start()
    x, y, core = place()
    me = (x * SIDE + y) * 2 + core
    n_dp = 2 * SIDE * SIDE
    head = lax.axis_index("head")
    around = [{"head": lax.rem(head + by, HEADS)} for by in (1, HEADS - 1)]
    greet(everyone() + around)

    own_stat = pltpu.make_async_copy(stat_ref.at[me], stat_in.at[me], load_sem.at[6])
    own_stat.start()
    stats = []
    for i in range(1, n_dp):
        peer = lax.rem(me + i, n_dp)
        copy = remote(stat_ref.at[peer], stat_in.at[me], stat_send.at[i], stat_recv.at[i], {"dp": peer})
        copy.start()
        stats.append(copy)

    n = 3 + 15
    routes = []
    for half in range(2):
        part = scratch[half * n : (half + 1) * n]
        routes.append(Route(half, back_ref.at[half], final_ref.at[half], part[0], part[1], part[2], part[3:]))
    ring_scratch = scratch[2 * n :]
    bulk = stages(routes)
    bulk[0]()

    prompt_rows = pdk.shape[1] // HEADS
    slot_rows = q.shape[1] // HEADS

    def prompt_part(ref):
        return lambda t: ref[:, pl.ds(pl.multiple_of(t * prompt_rows, prompt_rows), prompt_rows), :]

    def slot_part(ref):
        return lambda t: ref[:, pl.ds(pl.multiple_of(t * slot_rows, slot_rows), slot_rows), :]

    rings = []
    for i, own in enumerate((prompt_part(pdk), prompt_part(pdv), slot_part(dk), slot_part(dv))):
        right, left = (4, 3) if i % 2 == 0 else (3, 4)
        rings.append(Ring(own, right, left, *ring_scratch[4 * i : 4 * i + 4]))
    spreads = [
        Spread(all_k, 4, 3, *ring_scratch[16:18]),
        Spread(all_v, 3, 4, *ring_scratch[18:20]),
    ]

    loads[0].wait()
    loads[1].wait()
    for ring in rings[:2]:
        ring.step(1)
    for load in loads[2:]:
        load.wait()
    bulk[1]()
    for ring in rings[:2]:
        ring.step(2)
    own_stat.wait()
    for copy in stats:
        copy.wait_recv()
    bulk[2]()

    def local_slot(slot):
        live = prompt_ref[slot] >= 0
        lse, delta = unpack_rows(stat_in[fetch_ref[slot] // 2, lax.rem(fetch_ref[slot], 2)])
        lse = jnp.where(live, lse, 1e30)
        delta = jnp.where(live, delta, 0.0)
        query = q[slot]
        grad = live_rows(g[slot], length_ref[slot])
        scores = dot(k[slot], query, NT) * scale
        mask = causal(scores.shape)
        prob = jnp.where(mask, jnp.exp2(jnp.where(mask, scores, -1e30) - lse), 0.0)
        grad_prob = dot(v[slot], grad, NT)
        dscore = (prob * (grad_prob - delta)).astype(BF16)
        prob = prob.astype(BF16)
        dk[slot] = dot(dscore, query, NN) * factor
        dv[slot] = dot(prob, grad, NN)
        out_ref[slot] = dot(prob, v[slot], TN).astype(BF16)
        dq_ref[slot] = (dot(dscore, k[slot], TN) * factor).astype(BF16)

    count = q.shape[0]
    per = 5
    pieces = 4

    def local_piece(piece):
        def go(i, carry):
            for j in range(per):
                local_slot((piece * (count // per // pieces) + i) * per + j)
            return carry

        lax.fori_loop(0, count // per // pieces, go, 0)

    local_piece(0)
    for ring in rings[:2]:
        ring.step(3)
    local_piece(1)
    for ring in rings[:2]:
        ring.step(4)
    bulk[3]()
    local_piece(2)
    all_k[head] = rings[0].result().astype(BF16)
    all_v[head] = rings[1].result().astype(BF16)
    for spread in spreads:
        spread.step(1)
    local_piece(3)
    for ring in rings[2:]:
        ring.step(1)
    bulk[4]()
    for spread in spreads:
        spread.step(2)
    for ring in rings[2:]:
        ring.step(2)
    for spread in spreads:
        spread.step(3)
    bulk[5]()
    for ring in rings[2:]:
        ring.step(3)
    for spread in spreads:
        spread.step(4)
    for ring in rings[2:]:
        ring.step(4)
    drk_ref[...] = rings[2].result()
    drv_ref[...] = rings[3].result()
    for spread in spreads:
        spread.close()
    bulk[6]()
    bulk[7]()
    for ring in rings:
        ring.close()
    for copy in stats:
        copy.wait_send()


def give_back(fetch, prompts, lengths, back, stats, pdk, pdv, queries, grads, keys, values, scale, factor):
    count, rows, dim = queries.shape
    held, length, _ = pdk.shape
    height = back.shape[-2]
    n_dp = 2 * SIDE * SIDE
    V, D = pltpu.VMEM, pltpu.SemaphoreType.DMA
    resp = (count, rows, dim)
    scratch = [V(resp, BF16)] * 4 + [V(pdk.shape, F32)] * 2 + [V(resp, F32)] * 2
    scratch += [V((n_dp, 2, STAT, dim), BF16), D((7,)), D((n_dp,)), D((n_dp,))]
    for _ in range(2):
        scratch += route_scratch(height, dim, BF16) + route_sems()
    for shape in ((held, length // HEADS, dim),) * 2 + ((count, rows // HEADS, dim),) * 2:
        scratch += [V((7,) + shape, BF16), V((7,) + shape, BF16), D((7,)), D((7,))]
    scratch += [D((7,))] * 4
    smem = pl.BlockSpec(memory_space=pltpu.SMEM)
    anywhere = pl.BlockSpec(memory_space=pl.ANY)
    vmem = pl.BlockSpec(memory_space=pltpu.VMEM)
    part = jax.ShapeDtypeStruct((count, rows // HEADS, dim), F32)
    parts = jax.ShapeDtypeStruct((HEADS, held, length // HEADS, dim), BF16)
    return pl.pallas_call(
        functools.partial(return_kernel, scale, factor),
        out_shape=(
            jax.ShapeDtypeStruct(back.shape, BF16),
            jax.ShapeDtypeStruct(resp, BF16),
            jax.ShapeDtypeStruct(resp, BF16),
            part,
            part,
            parts,
            parts,
        ),
        in_specs=[smem] * 3 + [anywhere] * 8,
        out_specs=(anywhere, vmem, vmem, vmem, vmem, vmem, vmem),
        scratch_shapes=scratch,
        compiler_params=pltpu.CompilerParams(collective_id=2, has_side_effects=True),
    )(fetch, prompts, lengths, back, stats, pdk, pdv, queries, grads, keys, values)


def merge_kernel(per_step, fetch_ref, prompt_ref, length_ref, *refs):
    back_refs = refs[:per_step]
    out_part, dq_part, out_ref, dq_ref = refs[per_step:]
    rows = out_part.shape[1]
    step = pl.program_id(0)
    for j in range(per_step):
        slot = step * per_step + j
        live = prompt_ref[slot] >= 0
        row = lax.broadcasted_iota(jnp.int32, out_part.shape[1:], 0)
        back = back_refs[j]
        out = back[0, 0:rows, :].astype(F32) + out_part[j].astype(F32)
        dq = back[0, rows : 2 * rows, :].astype(F32) + dq_part[j].astype(F32)
        length = jnp.where(live, length_ref[slot], 0)
        out_ref[j] = jnp.where(row < length, out, 0.0).astype(BF16)
        dq_ref[j] = jnp.where(row < length, dq, 0.0).astype(BF16)


def merge(fetch, prompts, lengths, back, out_part, dq_part):
    count, rows, dim = out_part.shape
    per_step = 8
    some = pl.BlockSpec((per_step, rows, dim), lambda i, a, b, c: (i, 0, 0))

    def one(j):
        return pl.BlockSpec((1, 2 * rows, dim), lambda i, a, b, c: (a[i * per_step + j], 0, 0))

    return pl.pallas_call(
        functools.partial(merge_kernel, per_step),
        out_shape=(jax.ShapeDtypeStruct((count, rows, dim), BF16),) * 2,
        grid_spec=pltpu.PrefetchScalarGridSpec(
            num_scalar_prefetch=3,
            grid=(count // per_step,),
            in_specs=[one(j) for j in range(per_step)] + [some, some],
            out_specs=(some, some),
        ),
    )(fetch, prompts, lengths, *([back] * per_step), out_part, dq_part)


def body(queries, resp_keys, resp_values, prompt_keys, prompt_values, grad_out, slot_prompt, slot_length):
    slot_count, rows, dim = queries.shape
    held, length, _ = prompt_keys.shape
    factor = dim ** (-0.5)
    scale = factor * LOG2E
    n_dp = 2 * SIDE * SIDE
    items = 2 * n_dp
    x, y, core = place()
    ids = jnp.arange(slot_count, dtype=jnp.int32)
    at = jnp.arange(items, dtype=jnp.int32)
    own = jnp.where(slot_prompt >= 0, slot_prompt // held, -1)
    before = ids[None, :] < ids[:, None]
    order = jnp.sum((own[:, None] == own[None, :]) & before, axis=1, dtype=jnp.int32)
    hx, hy, hc = own // (2 * SIDE), own // 2 % SIDE, own % 2
    first, second = jnp.where(order == 0, hx, hy), jnp.where(order == 0, hy, hx)
    here_first, here_second = jnp.where(order == 0, x, y), jnp.where(order == 0, y, x)
    live = own >= 0
    target = jnp.where(live, ((order * SIDE + first) * SIDE + second) * 2 + hc, -1)
    near_first, near_second = (first - here_first + SIDE) % SIDE, (second - here_second + SIDE) % SIDE
    fetch = jnp.where(live, ((order * SIDE + near_first) * SIDE + near_second) * 2 + hc, 0)
    stat_fetch = jnp.where(live, own * 2 + order, 0)
    hit = target[None, :] == at[:, None]
    send_slot = jnp.sum(jnp.where(hit, ids[None, :], 0), axis=1, dtype=jnp.int32)
    send_prompt = jnp.sum(jnp.where(hit, (slot_prompt % held)[None, :] + 1, 0), axis=1, dtype=jnp.int32) - 1
    half, r_first, r_second, from_core = at // n_dp, at // (2 * SIDE) % SIDE, at // 2 % SIDE, at % 2
    from_first = (jnp.where(half == 0, x, y) + r_first) % SIDE
    from_second = (jnp.where(half == 0, y, x) + r_second) % SIDE
    back_to = ((half * SIDE + from_first) * SIDE + from_second) * 2 + from_core
    from_x, from_y = jnp.where(half == 0, from_first, from_second), jnp.where(half == 0, from_second, from_first)
    stat_to = ((from_x * SIDE + from_y) * 2 + from_core) * 2 + half

    packed = pack(send_slot, send_prompt, slot_length, queries, grad_out, resp_keys, resp_values, scale)
    grid = (2, SIDE, SIDE, 2)
    received = torus_exchange(packed.reshape(grid + packed.shape[1:]), 1).reshape(packed.shape)
    item_prompt = received[:, 2 * rows + 4, 0].astype(jnp.int32)
    order_in = jnp.sum((item_prompt[:, None] == item_prompt[None, :]) & (at[None, :] < at[:, None]), axis=1, dtype=jnp.int32)
    spot = jnp.where(item_prompt >= 0, item_prompt * FANOUT + order_in, -1)
    group_hit = spot[None, :] == jnp.arange(held * FANOUT, dtype=jnp.int32)[:, None]
    group_item = jnp.sum(jnp.where(group_hit, at[None, :], 0), axis=1, dtype=jnp.int32)

    result, stats, pdk, pdv = holder(
        group_item, back_to, stat_to, received, prompt_keys, prompt_values, scale, factor
    )
    back, local_out, local_dq, drk, drv, all_k, all_v = give_back(
        stat_fetch, slot_prompt, slot_length, result.reshape(grid + result.shape[1:]),
        stats.reshape((n_dp, 2) + stats.shape[1:]), pdk, pdv, queries, grad_out, resp_keys, resp_values, scale, factor,
    )
    attn_out, grad_queries = merge(fetch, slot_prompt, slot_length, back.reshape(result.shape), local_out, local_dq)

    def joined(parts):
        return jnp.swapaxes(parts, 0, 1).reshape(held, length, dim).astype(F32)

    return (attn_out, grad_queries, drk, drv, joined(all_k), joined(all_v))


def solution(mesh):
    return jax.shard_map(
        body,
        mesh=mesh,
        in_specs=(
            P("dp", None, "head"),
            P("dp", None, None),
            P("dp", None, None),
            P("dp", None, None),
            P("dp", None, None),
            P("dp", None, "head"),
            P("dp"),
            P("dp"),
        ),
        out_specs=(
            P("dp", None, "head"),
            P("dp", None, "head"),
            P("dp", "head", None),
            P("dp", "head", None),
            P("dp", None, None),
            P("dp", None, None),
        ),
        check_vma=False,
    )
```

time: 300 us -> 185 us (0.62); the launches traced: 295 us -> 184 us
  waiting for transfers between devices: 179 us -> 0 us
  Pallas kernels: 48.9 us -> 173 us
  starting transfers between devices: 20.7 us -> 0 us
  blocking collectives: 16.1 us -> 0 us
  between operations: 14.1 us -> 0.75 us
  local copies, waits for them, and re-layouts: 13.1 us -> 3.63 us
  other arithmetic: 3.59 us -> 6.8 us
    pallas_call x1 -> x2, Pallas kernels: 14.3 us -> 137 us  [the longest x1 79.8 us: give_back(): pl.pallas_call(functools.partial(return_kernel, scale, factor), out_shape...]
    all_to_all x3 -> x0, waiting for transfers between devices: 104 us -> none  [exchange(): lax.all_to_all(shaped, 'dp', split_axis=0, concat_axis=0, tiled=True)]
    psum x1 -> x0, waiting for transfers between devices: 74.2 us -> none  [body(): lax.psum((prefix_dk, prefix_dv), 'head')]
    all_to_all x3 -> x0, starting transfers between devices: 20.7 us -> none  [exchange(): lax.all_to_all(shaped, 'dp', split_axis=0, concat_axis=0, tiled=True)]
    all_to_all x1 -> x0, blocking collectives: 16.1 us -> none  [exchange(): lax.all_to_all(shaped, 'dp', split_axis=0, concat_axis=0, tiled=True)]
    gather x2 -> x0, local copies, waits for them, and re-layouts: 4.69 us -> none  [the longest x1 3.15 us: body(): back = exchange(result[back_index])]
    unnamed x6 -> x10, local copies, waits for them, and re-layouts: 4.89 us -> 1.47 us
  transfers between devices with their start and end apart: 5 -> 0, of which waited for: 3 -> 0; matrix products, arithmetic and copies ran while one was open for 3% -> 0% of each run, Pallas kernels for 5% -> 0%
where the time goes in v2:
time: 185 us; the launch traced here: 184 us
  Pallas kernels  173 us (94%)
  other arithmetic  6.8 us (4%)
  local copies, waits for them, and re-layouts  3.63 us (2%)
    pallas_call x1, Pallas kernels, give_back(): pl.pallas_call(functools.partial(return_kernel, scale, factor), out_shape...  79.8 us
    pallas_call x1, Pallas kernels, torus_exchange(): pl.pallas_call(exchange_kernel, out_shape=jax.ShapeDtypeStruct(send.shape...  57.6 us
    pallas_call x1, Pallas kernels, holder(): pl.pallas_call(functools.partial(holder_kernel, scale, factor), out_shape...  19.8 us
    pallas_call x1, Pallas kernels, pack(): pl.pallas_call(functools.partial(pack_kernel, scale, per_step), out_shape...  9.23 us
    pallas_call x1, Pallas kernels, merge(): pl.pallas_call(functools.partial(merge_kernel, per_step), out_shape=(jax....  6.63 us

profile of v2, /device:TPU:1, one launch (start us, length us, event | category | flops | bytes accessed | tf_op | source)
XLA Modules:
  0.0 184.3 jit_solution(8887522891814032122)
XLA Ops:
  0.7 0.7 fusion.8
  1.3 0.2 convert_reduce_fusion.1
  1.5 0.6 multiply_add_fusion
  2.1 0.5 add_select_fusion
  2.6 0.6 add_select_fusion.2.fetch_ref
  3.2 0.6 select_reduce_fusion
  3.8 0.5 broadcast_add_fusion.prompt_ref
  4.3 9.2 %shard_map.127 = bf16[64,272,128]{2,1,0:T(8,128)(2,1)} custom-call(s32[64]{0:T(128)} %get-tuple-element.33.slot_ref, s32[64]{0:T(128)} %broadcast_add_fusion.prompt_ref, s32[40]{0:T(128)} %length_ref.5, bf16[40,128,128]{2,1,0:T(8,128)(2,1)} %q_ref.3, bf16[40,128,128]{2,1,0:T(8,128)(2,1)} %g_ref.3, bf16[40,128,128]{2,1,0:T(8,128)(2,1)} %k_ref.5, ...), custom_call_target="tpu_custom_call" | custom-call | tf_op jit(solution)/shard_map/pallas_call | solution.py:262
  13.5 57.6 %shard_map.128 = bf16[2,4,4,2,272,128]{5,4,3,2,1,0:T(8,128)(2,1)} custom-call(bf16[2,4,4,2,272,128]{5,4,3,2,1,0:T(8,128)(2,1)} %bitcast.22), custom_call_target="tpu_custom_call" | custom-call | tf_op jit(solution)/shard_map/pallas_call | solution.py:194
  71.1 2.1 %fusion = s32[64]{0:T(128)S(1)} fusion(bf16[64,272,128]{2,1,0:T(8,128)(2,1)} %bitcast.19), kind=kLoop, calls=%fused_computation.3 | loop fusion | flops 64 | bytes 384 | tf_op jit(solution)/shard_map/convert_element_type | solution.py:710
  73.3 0.2 convert_reduce_fusion
  73.5 0.6 select_reduce_fusion.2.item_ref
  74.1 19.8 %shard_map.129 = (bf16[64,256,128]{2,1,0:T(8,128)(2,1)}, bf16[64,16,128]{2,1,0:T(8,128)(2,1)}, f32[4,512,128]{2,1,0:T(8,128)}, f32[4,512,128]{2,1,0:T(8,128)}) custom-call(s32[32]{0:T(128)} %select_reduce_fusion.2.item_ref, s32[64]{0:T(128)} %get-tuple-element.40.back_ref, s32[64]{0:T(128)} %get-tuple-element.39.stat_to_ref, bf16[64,272,128]{2,1,0:T(8,128)(2,1)} %bitcast.20, ...), custom_call_target="tpu_custom_call" | custom-call | tf_op jit(solution)/shard_map/pallas_call | solution.py:357
  94.0 79.8 %shard_map.130 = (bf16[2,4,4,2,256,128]{5,4,3,2,1,0:T(8,128)(2,1)}, bf16[40,128,128]{2,1,0:T(8,128)(2,1)}, bf16[40,128,128]{2,1,0:T(8,128)(2,1)}, f32[40,16,128]...) custom-call(s32[40]{0:T(128)} %get-tuple-element.36.fetch_ref, ...), custom_call_target="tpu_custom_call" | custom-call | tf_op jit(solution)/shard_map/pallas_call | solution.py:621
  173.8 0.0 copy-start.1
  173.8 6.6 %shard_map.131 = (bf16[40,128,128]{2,1,0:T(8,128)(2,1)}, bf16[40,128,128]{2,1,0:T(8,128)(2,1)}) custom-call(s32[40]{0:T(128)} %add_select_fusion.2.fetch_ref, s32[40]{0:T(128)} %prompt_ref.3, s32[40]{0:T(128)} %length_ref.5, bf16[64,256,128]{2,1,0:T(8,128)(2,1)} %bitcast.11, bf16[64,256,128]{2,1,0:T(8,128)(2,1)} %bitcast.12, bf16[64,256,128]{2,1,0:T(8,128)(2,1)} %bitcast.13, ...), custom_call_target="tpu_custom_call" | custom-call | tf_op jit(solution)/shard_map/pallas_call | solution.py:664
  180.4 0.0 copy-done.1
  180.4 0.1 convert_bitcast_fusion.1
  180.5 0.0 copy-start
  180.6 1.1 copy.16
  181.6 0.0 copy-done
  181.6 0.1 convert_bitcast_fusion
  181.8 0.0 copy-start.3
  181.8 0.0 copy-start.2
  181.8 1.1 copy.17
  182.9 0.0 copy-done.3
  182.9 0.7 copy.20
  183.6 0.0 copy-done.2
  183.6 0.7 copy.21
  (1 shorter events, 0.0 us)
Async XLA Ops:
  173.8 6.6 %copy-start.1 = (bf16[8,4,64,128]{3,2,1,0:T(8,128)(2,1)S(1)}, bf16[8,4,64,128]{3,2,1,0:T(8,128)(2,1)}, u32[]{:S(2)}) copy-start(bf16[8,4,64,128]{3,2,1,0:T(8,128)(2,1)} %get-tuple-element.30) | copy-start | bytes 1572868
  180.5 1.1 copy-start
  181.8 1.1 copy-start.3
  181.8 1.8 copy-start.2

commit v3 on v2

--- a/solution.py
+++ b/solution.py
@@ -32,26 +32,20 @@
 def step_by(value, by):
     return lax.rem(value + by + SIDE, SIDE)
 
-def neighbours():
-    x, y, core = place()
-    out = [device(0, x, y, 1 - core)]
-    for by in (1, -1):
-        for c in range(2):
-            out.append(device(0, step_by(x, by), y, c))
-            out.append(device(0, x, step_by(y, by), c))
-    return out
-
 def everyone():
     x, y, core = place()
     me = (x * SIDE + y) * 2 + core
     return [{"dp": lax.rem(me + k, 2 * SIDE * SIDE)} for k in range(1, 2 * SIDE * SIDE)]
 
 
-def greet(near):
+def greet_start(near):
     barrier = pltpu.get_barrier_semaphore()
     for who in near:
         pl.semaphore_signal(barrier, inc=1, device_id=who, device_id_type=MESH)
-    pl.semaphore_wait(barrier, len(near))
+
+
+def greet_end(near):
+    pl.semaphore_wait(pltpu.get_barrier_semaphore(), len(near))
 
 def remote(src, dst, send, recv, who):
     return pltpu.make_async_remote_copy(src_ref=src, dst_ref=dst, send_sem=send, recv_sem=recv, device_id=who, device_id_type=MESH)
@@ -126,74 +120,101 @@
 
 def stages(routes):
     started = []
+
     def go(copy):
-        copy.start(); started.append(copy)
-    def second(route, r):
-        go(route.second_far(r))
-        for side in range(2):
-            for c in range(2):
-                go(route.second_direct(r, side, c))
-        go(route.cross(r)); go(route.own(r))
-    def s0():
+        copy.start()
+        started.append(copy)
+
+    def second_near(route, r, side):
+        for c in range(2):
+            go(route.second_direct(r, side, c))
+
+    def second_here(route, r):
+        go(route.cross(r))
+        go(route.own(r))
+
+    def relay(route, r):
+        route.second_far(r).wait_recv()
+        for c in range(2):
+            go(route.second_forward(r, c))
+
+    def begin():
         for j in range(2):
             for side in range(2):
-                for route in routes: go(route.first_far(side, j))
-        for route in routes: second(route, 0)
-        for j in (2, 1, 3, 0):
+                for route in routes:
+                    go(route.first_far(side, j))
+        for route in routes:
+            go(route.second_far(0))
             for side in range(2):
-                for route in routes: go(route.first_direct(side, j))
-    def s1():
+                second_near(route, 0, side)
+        for side in range(2):
+            for route in routes:
+                go(route.first_direct(side, 2))
+        for route in routes:
+            second_here(route, 0)
+
+    def forward():
         for j in range(2):
             for side in range(2):
                 for route in routes:
                     route.first_far(side, j).wait_recv()
                     go(route.first_forward(side, j))
-    def relay(route, r):
-        route.second_far(r).wait_recv()
-        for c in range(2): go(route.second_forward(r, c))
-    def s2():
-        for route in routes: relay(route, 0)
-    def s3():
+        for j in (1, 3, 0):
+            for side in range(2):
+                for route in routes:
+                    go(route.first_direct(side, j))
+
+    def relay_own():
+        for route in routes:
+            relay(route, 0)
+
+    def turn_far():
         for side in range(2):
-            r = 3 if side == 0 else 1
             for route in routes:
-                for j in range(4): route.first_direct(side, j).wait_recv()
-                second(route, r)
-    def s4():
+                route.first_direct(side, 2).wait_recv()
+                go(route.second_far(3 if side == 0 else 1))
+
+    def turn_forwarded():
         for route in routes:
             for side in range(2):
-                for j in range(2): route.first_forward(side, j).wait_recv()
-            second(route, 2)
-    def s5():
+                for j in range(2):
+                    route.first_forward(side, j).wait_recv()
+            go(route.second_far(2))
+            for side in range(2):
+                second_near(route, 2, side)
+            second_here(route, 2)
+
+    def turn_near():
+        for j, way in ((1, 0), (3, 1)):
+            for side in range(2):
+                for route in routes:
+                    route.first_direct(side, j).wait_recv()
+                    second_near(route, 3 if side == 0 else 1, way)
+        for side in range(2):
+            for route in routes:
+                route.first_direct(side, 0).wait_recv()
+                second_here(route, 3 if side == 0 else 1)
+
+    def relay_rest():
         for r in (3, 1, 2):
-            for route in routes: relay(route, r)
-    def s6():
+            for route in routes:
+                relay(route, r)
+
+    def arrive():
         for r in (0, 3, 1, 2):
             for route in routes:
-                for side in range(2): wait_second_direct(route, r, side)
-                wait_second_forward(route, r); wait_cross(route, r)
-    def s7():
+                for side in range(2):
+                    wait_second_direct(route, r, side)
+                wait_second_forward(route, r)
+                wait_cross(route, r)
+                route.own(r).wait()
+
+    def close():
         for copy in started:
-            if copy.is_remote: copy.wait_send()
-            else: copy.wait()
-    return [s0, s1, s2, s3, s4, s5, s6, s7]
-
-def exchange_kernel(send_ref, final_ref, *scratch):
-    greet(neighbours())
-    n = 3 + 15
-    routes = []
-    for k in range(2):
-        part = scratch[k * n:(k + 1) * n]
-        routes.append(Route(k, send_ref.at[k], final_ref.at[k], part[0], part[1], part[2], part[3:]))
-    for stage in stages(routes): stage()
-
-def torus_exchange(send, cid):
-    h, d = send.shape[-2:]
-    scratch = []
-    for _ in range(2): scratch += route_scratch(h, d, send.dtype) + route_sems()
-    return pl.pallas_call(exchange_kernel, out_shape=jax.ShapeDtypeStruct(send.shape, send.dtype),
-        in_specs=[pl.BlockSpec(memory_space=pl.ANY)], out_specs=pl.BlockSpec(memory_space=pl.ANY),
-        scratch_shapes=scratch, compiler_params=pltpu.CompilerParams(collective_id=cid, has_side_effects=True))(send)
+            if copy.is_remote:
+                copy.wait_send()
+
+    return [begin, forward, relay_own, turn_far, turn_forwarded, turn_near, relay_rest, arrive, close]
 
 
 def dot(a, b, dims):
@@ -234,45 +255,139 @@
     return lax.broadcasted_iota(jnp.int32, shape, 0) <= lax.broadcasted_iota(jnp.int32, shape, 1)
 
 
-def pack_kernel(scale, per_step, slot_ref, prompt_ref, length_ref, q_ref, g_ref, k_ref, v_ref, send_ref):
-    rows = q_ref.shape[1]
-    step = pl.program_id(0)
-    for j in range(per_step):
-        slot = slot_ref[step * per_step + j]
-        query = q_ref[slot]
-        grad = live_rows(g_ref[slot], length_ref[slot])
-        scores = dot(k_ref[slot], query, NT) * scale
-        scores = jnp.where(causal(scores.shape), scores, -1e30)
-        top = jnp.max(scores, axis=0, keepdims=True)
-        exps = jnp.exp2(scores - top)
-        total = jnp.sum(exps, axis=0, keepdims=True)
-        grad_prob = dot(v_ref[slot], grad, NT)
-        row_sum = jnp.sum(exps * grad_prob, axis=0, keepdims=True) / total
-        send_ref[j, 0:rows, :] = query
-        send_ref[j, rows : 2 * rows, :] = grad
-        prompt = prompt_ref[step * per_step + j].astype(F32)
-        send_ref[j, 2 * rows :, :] = pack_rows(top + jnp.log2(total), row_sum, prompt)
-
-
-def pack(slots, prompts, lengths, queries, grads, keys, values, scale):
-    items = slots.shape[0]
+def swap_stats(stat_send, stat_in, own_sem, send_sem, recv_sem):
+    x, y, core = place()
+    me = (x * SIDE + y) * 2 + core
+    n_dp = 2 * SIDE * SIDE
+    own = pltpu.make_async_copy(stat_send.at[me], stat_in.at[me], own_sem)
+    own.start()
+    copies = []
+    for i in range(1, n_dp):
+        peer = lax.rem(me + i, n_dp)
+        copy = remote(stat_send.at[peer], stat_in.at[me], send_sem.at[i], recv_sem.at[i], {"dp": peer})
+        copy.start()
+        copies.append(copy)
+    return own, copies
+
+
+def forward_slots(slots, scale, q, g, k, v):
+    query = [q[s] for s in slots]
+    grad = [g[s] for s in slots]
+    key = [k[s] for s in slots]
+    value = [v[s] for s in slots]
+    scores = [dot(a, b, NT) * scale for a, b in zip(key, query)]
+    grad_prob = [dot(a, b, NT) for a, b in zip(value, grad)]
+    mask = causal(scores[0].shape)
+    scores = [jnp.where(mask, a, -1e30) for a in scores]
+    top = [jnp.max(a, axis=0, keepdims=True) for a in scores]
+    exps = [jnp.exp2(a - b) for a, b in zip(scores, top)]
+    total = [jnp.sum(a, axis=0, keepdims=True) for a in exps]
+    row_sum = [jnp.sum(a * b, axis=0, keepdims=True) / c for a, b, c in zip(exps, grad_prob, total)]
+    return [(a + jnp.log2(b), c) for a, b, c in zip(top, total, row_sum)]
+
+
+def send_kernel(
+    scale, slot_ref, stat_slot_ref, prompt_ref, length_ref, q_ref, g_ref, k_ref, v_ref, final_ref, stat_in,
+    q, g, k, v, packed, stat, stat_send, load_sem, stat_s, stat_r, *scratch
+):
+    loads = [
+        pltpu.make_async_copy(src, dst, load_sem.at[i])
+        for i, (src, dst) in enumerate(((q_ref, q), (g_ref, g), (k_ref, k), (v_ref, v)))
+    ]
+    for load in loads:
+        load.start()
+    count, rows, _ = q.shape
+    n_dp = 2 * SIDE * SIDE
+    per = 5
+    greet_start(everyone())
+    loads[0].wait()
+    loads[1].wait()
+
+    def mask_rows(i, carry):
+        for j in range(per):
+            slot = i * per + j
+            g[slot] = live_rows(g[slot], length_ref[slot])
+        return carry
+
+    lax.fori_loop(0, count // per, mask_rows, 0)
+
+    def fill(i, carry):
+        for half in range(2):
+            for c in range(2):
+                slot = slot_ref[half * n_dp + i * 2 + c]
+                at = (half, i // SIDE, lax.rem(i, SIDE), c)
+                packed[at + (slice(0, rows), slice(None))] = q[slot]
+                packed[at + (slice(rows, 2 * rows), slice(None))] = g[slot]
+        return carry
+
+    lax.fori_loop(0, SIDE * SIDE, fill, 0)
+    greet_end(everyone())
+    n = 3 + 15
+    routes = []
+    for half in range(2):
+        part = scratch[half * n : (half + 1) * n]
+        routes.append(Route(half, packed.at[half], final_ref.at[half], part[0], part[1], part[2], part[3:]))
+    bulk = stages(routes)
+    bulk[0]()
+    loads[2].wait()
+    loads[3].wait()
+
+    def forward(i, carry):
+        slots = [i * per + j for j in range(per)]
+        for slot, (lse, row_sum) in zip(slots, forward_slots(slots, scale, q, g, k, v)):
+            stat[slot] = pack_rows(lse, row_sum, prompt_ref[slot].astype(F32))
+        return carry
+
+    steps = count // per
+    lax.fori_loop(0, steps // 2, forward, 0)
+    bulk[1]()
+    lax.fori_loop(steps // 2, steps, forward, 0)
+
+    def fill_stats(i, carry):
+        for half in range(2):
+            slot = stat_slot_ref[i * 2 + half]
+            row = lax.broadcasted_iota(jnp.int32, stat.shape[1:], 0)
+            block = stat[jnp.maximum(slot, 0)].astype(F32)
+            stat_send[i, half] = jnp.where((row >= 4) & (slot < 0), -1.0, block).astype(BF16)
+        return carry
+
+    lax.fori_loop(0, n_dp, fill_stats, 0)
+    bulk[2]()
+    own, copies = swap_stats(stat_send, stat_in, load_sem.at[4], stat_s, stat_r)
+    for stage in bulk[3:8]:
+        stage()
+    own.wait()
+    for copy in copies:
+        copy.wait_recv()
+    bulk[8]()
+    for copy in copies:
+        copy.wait_send()
+
+
+def send_out(slots, stat_slots, prompts, lengths, queries, grads, keys, values, scale):
     count, rows, dim = queries.shape
-    per_step = 8
-    whole = pl.BlockSpec((count, rows, dim), lambda i, a, b, c: (0, 0, 0))
+    n_dp = 2 * SIDE * SIDE
+    V, D = pltpu.VMEM, pltpu.SemaphoreType.DMA
+    resp = (count, rows, dim)
+    shape = (2, SIDE, SIDE, 2, 2 * rows, dim)
+    scratch = [V(resp, BF16)] * 4 + [V(shape, BF16), V((count, STAT, dim), BF16), V((n_dp, 2, STAT, dim), BF16)]
+    scratch += [D((5,)), D((n_dp,)), D((n_dp,))]
+    for _ in range(2):
+        scratch += route_scratch(2 * rows, dim, BF16) + route_sems()
+    smem = pl.BlockSpec(memory_space=pltpu.SMEM)
+    anywhere = pl.BlockSpec(memory_space=pl.ANY)
     return pl.pallas_call(
-        functools.partial(pack_kernel, scale, per_step),
-        out_shape=jax.ShapeDtypeStruct((items, 2 * rows + STAT, dim), BF16),
-        grid_spec=pltpu.PrefetchScalarGridSpec(
-            num_scalar_prefetch=3,
-            grid=(items // per_step,),
-            in_specs=[whole] * 4,
-            out_specs=pl.BlockSpec((per_step, 2 * rows + STAT, dim), lambda i, a, b, c: (i, 0, 0)),
-        ),
-    )(slots, prompts, lengths, queries, grads, keys, values)
+        functools.partial(send_kernel, scale),
+        out_shape=(jax.ShapeDtypeStruct(shape, BF16), jax.ShapeDtypeStruct((n_dp, 2, STAT, dim), BF16)),
+        in_specs=[smem] * 4 + [anywhere] * 4,
+        out_specs=(anywhere, anywhere),
+        scratch_shapes=scratch,
+        compiler_params=pltpu.CompilerParams(collective_id=1, has_side_effects=True),
+    )(slots, stat_slots, prompts, lengths, queries, grads, keys, values)
 
 
 def holder_kernel(
-    scale, factor, item_ref, back_ref, stat_to_ref, a_ref, b_ref, k_ref, v_ref,
+    scale, factor, item_ref, stat_at_ref, back_ref, a_ref, b_ref, sa_ref, sb_ref, k_ref, v_ref,
     out_ref, stat_ref, dk_ref, dv_ref, kt, vt, out_buf, stat_buf, out_sem, stat_sem,
 ):
     prompt, step = pl.program_id(0), pl.program_id(1)
@@ -288,18 +403,17 @@
 
     def leaving(at, j):
         slot = lax.rem(at, 2)
-        item = item_ref[2 * at + j]
+        item = stat_at_ref[2 * at + j]
         return (
             pltpu.make_async_copy(out_buf.at[slot, j], out_ref.at[back_ref[item]], out_sem.at[slot, j]),
-            pltpu.make_async_copy(stat_buf.at[slot, j], stat_ref.at[stat_to_ref[item]], stat_sem.at[slot, j]),
+            pltpu.make_async_copy(stat_buf.at[slot, j], stat_ref.at[item], stat_sem.at[slot, j]),
         )
 
-    half = a_ref.shape[1]
-    rows = (half - STAT) // 2
+    rows = a_ref.shape[1] // 2
     query = jnp.concatenate([a_ref[0, 0:rows, :], b_ref[0, 0:rows, :]], axis=0)
     grad = jnp.concatenate([a_ref[0, rows : 2 * rows, :], b_ref[0, rows : 2 * rows, :]], axis=0)
-    lse_a, sum_a = unpack_rows(a_ref[0, 2 * rows :, :])
-    lse_b, sum_b = unpack_rows(b_ref[0, 2 * rows :, :])
+    lse_a, sum_a = unpack_rows(sa_ref[0])
+    lse_b, sum_b = unpack_rows(sb_ref[0])
     resp_lse = jnp.concatenate([lse_a, lse_b], axis=1)
     resp_sum = jnp.concatenate([sum_a, sum_b], axis=1)
     scores = dot(k_ref[0], query, NT) * scale
@@ -344,14 +458,17 @@
                     copy.wait()
 
 
-def holder(items, back_to, stat_to, received, keys, values, scale, factor):
+def holder(items, stat_at, back_to, received, stats, keys, values, scale, factor):
     count, height, dim = received.shape
     held, length, _ = keys.shape
-    rows = (height - STAT) // 2
+    rows = height // 2
     steps = FANOUT // 2
 
     def one(k):
         return pl.BlockSpec((1, height, dim), lambda p, j, ids, b, c: (ids[p * FANOUT + 2 * j + k], 0, 0))
+
+    def stat(k):
+        return pl.BlockSpec((1, STAT, dim), lambda p, j, ids, b, c: (b[p * FANOUT + 2 * j + k], 0, 0))
 
     whole = pl.BlockSpec((1, length, dim), lambda p, j, ids, b, c: (p, 0, 0))
     return pl.pallas_call(
@@ -365,7 +482,7 @@
         grid_spec=pltpu.PrefetchScalarGridSpec(
             num_scalar_prefetch=3,
             grid=(held, steps),
-            in_specs=[one(0), one(1), whole, whole],
+            in_specs=[one(0), one(1), stat(0), stat(1), whole, whole],
             out_specs=(
                 pl.BlockSpec(memory_space=pl.ANY),
                 pl.BlockSpec(memory_space=pl.ANY),
@@ -381,7 +498,7 @@
                 pltpu.SemaphoreType.DMA((2, 2)),
             ],
         ),
-    )(items, back_to, stat_to, received, received, keys, values)
+    )(items, stat_at, back_to, received, received, stats, stats, keys, values)
 
 
 HEADS = 8
@@ -457,11 +574,33 @@
                 self.copy(by, number, base).wait_send()
 
 
+def local_slots(slots, scale, factor, fetch_ref, prompt_ref, length_ref, stat_in, q, g, k, v, dk, dv, out, dq):
+    query = [q[s] for s in slots]
+    grad = [live_rows(g[s], length_ref[s]) for s in slots]
+    key = [k[s] for s in slots]
+    value = [v[s] for s in slots]
+    stats = [unpack_rows(stat_in[fetch_ref[s] // 2, lax.rem(fetch_ref[s], 2)]) for s in slots]
+    lse = [jnp.where(prompt_ref[s] >= 0, a, 1e30) for s, (a, _) in zip(slots, stats)]
+    delta = [jnp.where(prompt_ref[s] >= 0, a, 0.0) for s, (_, a) in zip(slots, stats)]
+    scores = [dot(a, b, NT) * scale for a, b in zip(key, query)]
+    grad_prob = [dot(a, b, NT) for a, b in zip(value, grad)]
+    mask = causal(scores[0].shape)
+    prob = [jnp.exp2(jnp.where(mask, a - b, -1e30)) for a, b in zip(scores, lse)]
+    dscore = [(a * (b - c)).astype(BF16) for a, b, c in zip(prob, grad_prob, delta)]
+    prob = [a.astype(BF16) for a in prob]
+    part_k = [dot(a, b, NN) * factor for a, b in zip(dscore, query)]
+    part_v = [dot(a, b, NN) for a, b in zip(prob, grad)]
+    part_out = [dot(a, b, TN).astype(BF16) for a, b in zip(prob, value)]
+    part_dq = [(dot(a, b, TN) * factor).astype(BF16) for a, b in zip(dscore, key)]
+    for s, a, b, c, d in zip(slots, part_k, part_v, part_out, part_dq):
+        dk[s], dv[s], out[s], dq[s] = a, b, c, d
+
+
 def return_kernel(
-    scale, factor, fetch_ref, prompt_ref, length_ref,
+    scale, factor, fetch_ref, stat_fetch_ref, prompt_ref, length_ref,
     back_ref, stat_ref, pdk_ref, pdv_ref, q_ref, g_ref, k_ref, v_ref,
-    final_ref, out_ref, dq_ref, drk_ref, drv_ref, all_k, all_v,
-    q, g, k, v, pdk, pdv, dk, dv, stat_in, load_sem, stat_send, stat_recv, *scratch
+    out_ref, dq_ref, drk_ref, drv_ref, all_k, all_v,
+    q, g, k, v, pdk, pdv, dk, dv, out, dq, final, stat_in, load_sem, stat_s, stat_r, *scratch
 ):
     loads = [
         pltpu.make_async_copy(src, dst, load_sem.at[i])
@@ -471,146 +610,148 @@
     ]
     for load in loads:
         load.start()
-    x, y, core = place()
-    me = (x * SIDE + y) * 2 + core
-    n_dp = 2 * SIDE * SIDE
     head = lax.axis_index("head")
-    around = [{"head": lax.rem(head + by, HEADS)} for by in (1, HEADS - 1)]
-    greet(everyone() + around)
-
-    own_stat = pltpu.make_async_copy(stat_ref.at[me], stat_in.at[me], load_sem.at[6])
-    own_stat.start()
-    stats = []
-    for i in range(1, n_dp):
-        peer = lax.rem(me + i, n_dp)
-        copy = remote(stat_ref.at[peer], stat_in.at[me], stat_send.at[i], stat_recv.at[i], {"dp": peer})
-        copy.start()
-        stats.append(copy)
+    near = everyone() + [{"head": lax.rem(head + by, HEADS)} for by in (1, HEADS - 1)]
+    greet_start(near)
+    greet_end(near)
+    own_stat, stats = swap_stats(stat_ref, stat_in, load_sem.at[6], stat_s, stat_r)
 
     n = 3 + 15
     routes = []
     for half in range(2):
         part = scratch[half * n : (half + 1) * n]
-        routes.append(Route(half, back_ref.at[half], final_ref.at[half], part[0], part[1], part[2], part[3:]))
+        routes.append(Route(half, back_ref.at[half], final.at[half], part[0], part[1], part[2], part[3:]))
     ring_scratch = scratch[2 * n :]
     bulk = stages(routes)
     bulk[0]()
 
+    count = q.shape[0]
     prompt_rows = pdk.shape[1] // HEADS
     slot_rows = q.shape[1] // HEADS
 
     def prompt_part(ref):
         return lambda t: ref[:, pl.ds(pl.multiple_of(t * prompt_rows, prompt_rows), prompt_rows), :]
 
-    def slot_part(ref):
-        return lambda t: ref[:, pl.ds(pl.multiple_of(t * slot_rows, slot_rows), slot_rows), :]
-
+    def slot_part(ref, group):
+        some = slice(group * (count // GROUPS), (group + 1) * (count // GROUPS))
+        return lambda t: ref[some, pl.ds(pl.multiple_of(t * slot_rows, slot_rows), slot_rows), :]
+
+    owns = [prompt_part(pdk), prompt_part(pdv)]
+    for group in range(GROUPS):
+        owns += [slot_part(dk, group), slot_part(dv, group)]
     rings = []
-    for i, own in enumerate((prompt_part(pdk), prompt_part(pdv), slot_part(dk), slot_part(dv))):
+    for i, own in enumerate(owns):
         right, left = (4, 3) if i % 2 == 0 else (3, 4)
         rings.append(Ring(own, right, left, *ring_scratch[4 * i : 4 * i + 4]))
+    last = 4 * len(owns)
     spreads = [
-        Spread(all_k, 4, 3, *ring_scratch[16:18]),
-        Spread(all_v, 3, 4, *ring_scratch[18:20]),
+        Spread(all_k, 4, 3, *ring_scratch[last : last + 2]),
+        Spread(all_v, 3, 4, *ring_scratch[last + 2 : last + 4]),
     ]
+
+    def ring(which, number):
+        for one in rings[2 * which : 2 * which + 2]:
+            one.step(number)
+
+    def spread(number):
+        for one in spreads:
+            one.step(number)
+
+    per = 5
+
+    def local(group):
+        steps = count // per // GROUPS
+
+        def go(i, carry):
+            slots = [(group * steps + i) * per + j for j in range(per)]
+            local_slots(
+                slots, scale, factor, stat_fetch_ref, prompt_ref, length_ref, stat_in, q, g, k, v, dk, dv, out, dq
+            )
+            return carry
+
+        lax.fori_loop(0, steps, go, 0)
 
     loads[0].wait()
     loads[1].wait()
-    for ring in rings[:2]:
-        ring.step(1)
+    ring(0, 1)
     for load in loads[2:]:
         load.wait()
-    bulk[1]()
-    for ring in rings[:2]:
-        ring.step(2)
     own_stat.wait()
     for copy in stats:
         copy.wait_recv()
+    local(0)
+    ring(1, 1)
+    bulk[1]()
+    ring(0, 2)
+    local(1)
+    ring(2, 1)
     bulk[2]()
-
-    def local_slot(slot):
-        live = prompt_ref[slot] >= 0
-        lse, delta = unpack_rows(stat_in[fetch_ref[slot] // 2, lax.rem(fetch_ref[slot], 2)])
-        lse = jnp.where(live, lse, 1e30)
-        delta = jnp.where(live, delta, 0.0)
-        query = q[slot]
-        grad = live_rows(g[slot], length_ref[slot])
-        scores = dot(k[slot], query, NT) * scale
-        mask = causal(scores.shape)
-        prob = jnp.where(mask, jnp.exp2(jnp.where(mask, scores, -1e30) - lse), 0.0)
-        grad_prob = dot(v[slot], grad, NT)
-        dscore = (prob * (grad_prob - delta)).astype(BF16)
-        prob = prob.astype(BF16)
-        dk[slot] = dot(dscore, query, NN) * factor
-        dv[slot] = dot(prob, grad, NN)
-        out_ref[slot] = dot(prob, v[slot], TN).astype(BF16)
-        dq_ref[slot] = (dot(dscore, k[slot], TN) * factor).astype(BF16)
-
-    count = q.shape[0]
-    per = 5
-    pieces = 4
-
-    def local_piece(piece):
-        def go(i, carry):
-            for j in range(per):
-                local_slot((piece * (count // per // pieces) + i) * per + j)
-            return carry
-
-        lax.fori_loop(0, count // per // pieces, go, 0)
-
-    local_piece(0)
-    for ring in rings[:2]:
-        ring.step(3)
-    local_piece(1)
-    for ring in rings[:2]:
-        ring.step(4)
+    ring(1, 2)
+    ring(0, 3)
     bulk[3]()
-    local_piece(2)
+    ring(2, 2)
+    ring(0, 4)
+    bulk[4]()
+    ring(1, 3)
     all_k[head] = rings[0].result().astype(BF16)
     all_v[head] = rings[1].result().astype(BF16)
-    for spread in spreads:
-        spread.step(1)
-    local_piece(3)
-    for ring in rings[2:]:
-        ring.step(1)
-    bulk[4]()
-    for spread in spreads:
-        spread.step(2)
-    for ring in rings[2:]:
-        ring.step(2)
-    for spread in spreads:
-        spread.step(3)
+    spread(1)
+    ring(2, 3)
     bulk[5]()
-    for ring in rings[2:]:
-        ring.step(3)
-    for spread in spreads:
-        spread.step(4)
-    for ring in rings[2:]:
-        ring.step(4)
-    drk_ref[...] = rings[2].result()
-    drv_ref[...] = rings[3].result()
-    for spread in spreads:
-        spread.close()
+    spread(2)
+    ring(1, 4)
+    spread(3)
+    ring(2, 4)
     bulk[6]()
+    spread(4)
+    half_count = count // GROUPS
+    for group in range(GROUPS):
+        some = slice(group * half_count, (group + 1) * half_count)
+        drk_ref[some] = rings[2 + 2 * group].result()
+        drv_ref[some] = rings[3 + 2 * group].result()
+    for one in spreads:
+        one.close()
     bulk[7]()
-    for ring in rings:
-        ring.close()
+
+    rows = q.shape[1]
+    n_dp = 2 * SIDE * SIDE
+
+    def merge(i, carry):
+        for j in range(per):
+            slot = i * per + j
+            at = fetch_ref[slot]
+            back = final[at // n_dp, lax.rem(at // (2 * SIDE), SIDE), lax.rem(at // 2, SIDE), lax.rem(at, 2)]
+            row = lax.broadcasted_iota(jnp.int32, (rows, back.shape[1]), 0)
+            live = row < jnp.where(prompt_ref[slot] >= 0, length_ref[slot], 0)
+            both = back.astype(F32)
+            out_ref[slot] = jnp.where(live, both[0:rows] + out[slot].astype(F32), 0.0).astype(BF16)
+            dq_ref[slot] = jnp.where(live, both[rows:] + dq[slot].astype(F32), 0.0).astype(BF16)
+        return carry
+
+    lax.fori_loop(0, count // per, merge, 0)
+    bulk[8]()
+    for one in rings:
+        one.close()
     for copy in stats:
         copy.wait_send()
 
 
-def give_back(fetch, prompts, lengths, back, stats, pdk, pdv, queries, grads, keys, values, scale, factor):
+GROUPS = 2
+
+
+def give_back(fetch, stat_fetch, prompts, lengths, back, stats, pdk, pdv, queries, grads, keys, values, scale, factor):
     count, rows, dim = queries.shape
     held, length, _ = pdk.shape
     height = back.shape[-2]
     n_dp = 2 * SIDE * SIDE
     V, D = pltpu.VMEM, pltpu.SemaphoreType.DMA
     resp = (count, rows, dim)
-    scratch = [V(resp, BF16)] * 4 + [V(pdk.shape, F32)] * 2 + [V(resp, F32)] * 2
+    scratch = [V(resp, BF16)] * 4 + [V(pdk.shape, F32)] * 2 + [V(resp, F32)] * 2 + [V(resp, BF16)] * 2
+    scratch += [V(back.shape, BF16)]
     scratch += [V((n_dp, 2, STAT, dim), BF16), D((7,)), D((n_dp,)), D((n_dp,))]
     for _ in range(2):
         scratch += route_scratch(height, dim, BF16) + route_sems()
-    for shape in ((held, length // HEADS, dim),) * 2 + ((count, rows // HEADS, dim),) * 2:
+    for shape in ((held, length // HEADS, dim),) * 2 + ((count // GROUPS, rows // HEADS, dim),) * (2 * GROUPS):
         scratch += [V((7,) + shape, BF16), V((7,) + shape, BF16), D((7,)), D((7,))]
     scratch += [D((7,))] * 4
     smem = pl.BlockSpec(memory_space=pltpu.SMEM)
@@ -621,7 +762,6 @@
     return pl.pallas_call(
         functools.partial(return_kernel, scale, factor),
         out_shape=(
-            jax.ShapeDtypeStruct(back.shape, BF16),
             jax.ShapeDtypeStruct(resp, BF16),
             jax.ShapeDtypeStruct(resp, BF16),
             part,
@@ -629,48 +769,11 @@
             parts,
             parts,
         ),
-        in_specs=[smem] * 3 + [anywhere] * 8,
-        out_specs=(anywhere, vmem, vmem, vmem, vmem, vmem, vmem),
+        in_specs=[smem] * 4 + [anywhere] * 8,
+        out_specs=(vmem, vmem, vmem, vmem, vmem, vmem),
         scratch_shapes=scratch,
         compiler_params=pltpu.CompilerParams(collective_id=2, has_side_effects=True),
-    )(fetch, prompts, lengths, back, stats, pdk, pdv, queries, grads, keys, values)
-
-
-def merge_kernel(per_step, fetch_ref, prompt_ref, length_ref, *refs):
-    back_refs = refs[:per_step]
-    out_part, dq_part, out_ref, dq_ref = refs[per_step:]
-    rows = out_part.shape[1]
-    step = pl.program_id(0)
-    for j in range(per_step):
-        slot = step * per_step + j
-        live = prompt_ref[slot] >= 0
-        row = lax.broadcasted_iota(jnp.int32, out_part.shape[1:], 0)
-        back = back_refs[j]
-        out = back[0, 0:rows, :].astype(F32) + out_part[j].astype(F32)
-        dq = back[0, rows : 2 * rows, :].astype(F32) + dq_part[j].astype(F32)
-        length = jnp.where(live, length_ref[slot], 0)
-        out_ref[j] = jnp.where(row < length, out, 0.0).astype(BF16)
-        dq_ref[j] = jnp.where(row < length, dq, 0.0).astype(BF16)
-
-
-def merge(fetch, prompts, lengths, back, out_part, dq_part):
-    count, rows, dim = out_part.shape
-    per_step = 8
-    some = pl.BlockSpec((per_step, rows, dim), lambda i, a, b, c: (i, 0, 0))
-
-    def one(j):
-        return pl.BlockSpec((1, 2 * rows, dim), lambda i, a, b, c: (a[i * per_step + j], 0, 0))
-
-    return pl.pallas_call(
-        functools.partial(merge_kernel, per_step),
-        out_shape=(jax.ShapeDtypeStruct((count, rows, dim), BF16),) * 2,
-        grid_spec=pltpu.PrefetchScalarGridSpec(
-            num_scalar_prefetch=3,
-            grid=(count // per_step,),
-            in_specs=[one(j) for j in range(per_step)] + [some, some],
-            out_specs=(some, some),
-        ),
-    )(fetch, prompts, lengths, *([back] * per_step), out_part, dq_part)
+    )(fetch, stat_fetch, prompts, lengths, back, stats, pdk, pdv, queries, grads, keys, values)
 
 
 def body(queries, resp_keys, resp_values, prompt_keys, prompt_values, grad_out, slot_prompt, slot_length):
@@ -696,31 +799,36 @@
     stat_fetch = jnp.where(live, own * 2 + order, 0)
     hit = target[None, :] == at[:, None]
     send_slot = jnp.sum(jnp.where(hit, ids[None, :], 0), axis=1, dtype=jnp.int32)
-    send_prompt = jnp.sum(jnp.where(hit, (slot_prompt % held)[None, :] + 1, 0), axis=1, dtype=jnp.int32) - 1
-    half, r_first, r_second, from_core = at // n_dp, at // (2 * SIDE) % SIDE, at // 2 % SIDE, at % 2
-    from_first = (jnp.where(half == 0, x, y) + r_first) % SIDE
-    from_second = (jnp.where(half == 0, y, x) + r_second) % SIDE
-    back_to = ((half * SIDE + from_first) * SIDE + from_second) * 2 + from_core
-    from_x, from_y = jnp.where(half == 0, from_first, from_second), jnp.where(half == 0, from_second, from_first)
-    stat_to = ((from_x * SIDE + from_y) * 2 + from_core) * 2 + half
-
-    packed = pack(send_slot, send_prompt, slot_length, queries, grad_out, resp_keys, resp_values, scale)
-    grid = (2, SIDE, SIDE, 2)
-    received = torus_exchange(packed.reshape(grid + packed.shape[1:]), 1).reshape(packed.shape)
-    item_prompt = received[:, 2 * rows + 4, 0].astype(jnp.int32)
+    stat_hit = jnp.where(live, stat_fetch, -1)[None, :] == at[:, None]
+    stat_slot = jnp.sum(jnp.where(stat_hit, ids[None, :] + 1, 0), axis=1, dtype=jnp.int32) - 1
+    half, from_core = at % 2, at // 2 % 2
+    from_x, from_y = at // (4 * SIDE), at // 4 % SIDE
+    back_to, received_at = [], []
+    for dx, dy, to in ((0, 0, back_to), (x, y, received_at)):
+        ax, ay = (from_x - dx + SIDE) % SIDE, (from_y - dy + SIDE) % SIDE
+        first, second = jnp.where(half == 0, ax, ay), jnp.where(half == 0, ay, ax)
+        to.append(((half * SIDE + first) * SIDE + second) * 2 + from_core)
+
+    received, stats_in = send_out(
+        send_slot, stat_slot, slot_prompt % held, slot_length, queries, grad_out, resp_keys, resp_values, scale
+    )
+    received = received.reshape((items,) + received.shape[4:])
+    stats_in = stats_in.reshape((items,) + stats_in.shape[2:])
+    item_prompt = stats_in[:, 4, 0].astype(jnp.int32)
     order_in = jnp.sum((item_prompt[:, None] == item_prompt[None, :]) & (at[None, :] < at[:, None]), axis=1, dtype=jnp.int32)
     spot = jnp.where(item_prompt >= 0, item_prompt * FANOUT + order_in, -1)
     group_hit = spot[None, :] == jnp.arange(held * FANOUT, dtype=jnp.int32)[:, None]
-    group_item = jnp.sum(jnp.where(group_hit, at[None, :], 0), axis=1, dtype=jnp.int32)
+    group_stat = jnp.sum(jnp.where(group_hit, at[None, :], 0), axis=1, dtype=jnp.int32)
+    group_item = jnp.sum(jnp.where(group_hit, received_at[0][None, :], 0), axis=1, dtype=jnp.int32)
 
     result, stats, pdk, pdv = holder(
-        group_item, back_to, stat_to, received, prompt_keys, prompt_values, scale, factor
+        group_item, group_stat, back_to[0], received, stats_in, prompt_keys, prompt_values, scale, factor
     )
-    back, local_out, local_dq, drk, drv, all_k, all_v = give_back(
-        stat_fetch, slot_prompt, slot_length, result.reshape(grid + result.shape[1:]),
+    grid = (2, SIDE, SIDE, 2)
+    attn_out, grad_queries, drk, drv, all_k, all_v = give_back(
+        fetch, stat_fetch, slot_prompt, slot_length, result.reshape(grid + result.shape[1:]),
         stats.reshape((n_dp, 2) + stats.shape[1:]), pdk, pdv, queries, grad_out, resp_keys, resp_values, scale, factor,
     )
-    attn_out, grad_queries = merge(fetch, slot_prompt, slot_length, back.reshape(result.shape), local_out, local_dq)
 
     def joined(parts):
         return jnp.swapaxes(parts, 0, 1).reshape(held, length, dim).astype(F32)

time: 185 us -> 164 us (0.89)
  Pallas kernels: 173 us -> 148 us
  local copies, waits for them, and re-layouts: 3.63 us -> 7.18 us
    pallas_call x3 -> x1, Pallas kernels: 73.5 us -> 60 us  [send_out(): pl.pallas_call(functools.partial(send_kernel, scale), out_shape=(jax.Shap...]
    pallas_call x1, Pallas kernels: 79.8 us -> 67.3 us  [give_back(): pl.pallas_call(functools.partial(return_kernel, scale, factor), out_shape...]
    unnamed x10 -> x14, local copies, waits for them, and re-layouts: 1.47 us -> 5.01 us
where the time goes in v3:
time: 164 us
  Pallas kernels  148 us (90%)
  other arithmetic  8.29 us (5%)
  local copies, waits for them, and re-layouts  7.18 us (4%)
    pallas_call x1, Pallas kernels, give_back(): pl.pallas_call(functools.partial(return_kernel, scale, factor), out_shape...  67.3 us
    pallas_call x1, Pallas kernels, send_out(): pl.pallas_call(functools.partial(send_kernel, scale), out_shape=(jax.Shap...  60 us
    pallas_call x1, Pallas kernels, holder(): pl.pallas_call(functools.partial(holder_kernel, scale, factor), out_shape...  20.4 us
    unnamed x14, local copies, waits for them, and re-layouts  5.01 us

profile of v3, /device:TPU:1, one launch (start us, length us, event | category | flops | bytes accessed | tf_op | source)
XLA Modules:
  0.0 163.9 jit_solution(10324173826394687563)
XLA Ops:
  0.7 0.5 multiply_add_fusion.back_ref
  1.2 1.2 and_select_fusion.10
  2.4 0.2 convert_reduce_fusion.1
  2.6 0.5 add_select_fusion
  3.1 0.5 add_select_fusion.2.fetch_ref
  3.6 0.6 select_reduce_fusion
  4.2 0.5 broadcast_add_fusion.stat_slot_ref
  4.7 60.0 %shard_map.127 = (bf16[2,4,4,2,256,128]{5,4,3,2,1,0:T(8,128)(2,1)}, bf16[32,2,16,128]{3,2,1,0:T(8,128)(2,1)}) custom-call(s32[64]{0:T(128)} %get-tuple-element.39.slot_ref, s32[64]{0:T(128)} %broadcast_add_fusion.stat_slot_ref, s32[40]{0:T(128)} %get-tuple-element.36.prompt_ref, s32[40]{0:T(128)} %length_ref.3, bf16[40,128,128]{2,1,0:T(8,128)(2,1)} %q_ref.3, ...), custom_call_target="tpu_custom_call" | custom-call | tf_op jit(solution)/shard_map/pallas_call | solution.py:379
  64.7 2.1 %fusion = s32[64]{0:T(128)S(1)} fusion(bf16[64,16,128]{2,1,0:T(8,128)(2,1)} %bitcast.13), kind=kLoop, calls=%fused_computation.3 | loop fusion | flops 64 | bytes 384 | tf_op jit(solution)/shard_map/convert_element_type | solution.py:817
  66.9 0.2 convert_reduce_fusion
  67.1 0.7 select_reduce_fusion.2
  67.7 20.4 %shard_map.128 = (bf16[64,256,128]{2,1,0:T(8,128)(2,1)}, bf16[64,16,128]{2,1,0:T(8,128)(2,1)}, f32[4,512,128]{2,1,0:T(8,128)}, f32[4,512,128]{2,1,0:T(8,128)}) custom-call(s32[32]{0:T(128)} %get-tuple-element.31.item_ref, s32[32]{0:T(128)} %get-tuple-element.30.stat_at_ref, s32[64]{0:T(128)} %multiply_add_fusion.back_ref, bf16[64,256,128]{2,1,0:T(8,128)(2,1)} %bitcast.10, ...), custom_call_target="tpu_custom_call" | custom-call | tf_op jit(solution)/shard_map/pallas_call | solution.py:474
  88.1 67.3 %shard_map.129 = (bf16[40,128,128]{2,1,0:T(8,128)(2,1)}, bf16[40,128,128]{2,1,0:T(8,128)(2,1)}, f32[40,16,128]{2,1,0:T(8,128)}, f32[40,16,128]{2,1,0:T(8,128)}, ...) custom-call(s32[40]{0:T(128)} %add_select_fusion.2.fetch_ref, s32[40]{0:T(128)} %get-tuple-element.35.stat_fetch_ref, ...), custom_call_target="tpu_custom_call" | custom-call | tf_op jit(solution)/shard_map/pallas_call | solution.py:762
  155.4 1.1 convert_bitcast_fusion.1
  156.6 0.0 copy-start.2
  156.6 1.1 copy.16
  157.7 0.0 copy-done.2
  157.7 0.1 convert_bitcast_fusion
  157.8 0.0 copy-start.1
  157.8 1.1 copy.17
  158.9 0.6 copy-done.1
  159.5 0.0 copy-start
  159.5 1.1 copy.22
  160.5 0.7 copy-done
  161.3 0.0 copy-start.4
  161.3 0.0 copy-start.3
  161.3 1.1 copy.23
  162.3 0.1 copy-done.4
  162.4 0.7 copy.24
  163.1 0.0 copy-done.3
  163.1 0.7 copy.25
  (3 shorter events, 0.0 us)
Async XLA Ops:
  156.6 1.1 copy-start.2
  157.8 1.7 %copy-start.1 = (bf16[40,128,128]{2,1,0:T(8,128)(2,1)S(1)}, bf16[40,128,128]{2,1,0:T(8,128)(2,1)}, u32[]{:S(2)}) copy-start(bf16[40,128,128]{2,1,0:T(8,128)(2,1)} %get-tuple-element.46) | copy-start | bytes 3932164
  159.5 1.8 %copy-start = (bf16[40,128,128]{2,1,0:T(8,128)(2,1)S(1)}, bf16[40,128,128]{2,1,0:T(8,128)(2,1)}, u32[]{:S(2)}) copy-start(bf16[40,128,128]{2,1,0:T(8,128)(2,1)} %get-tuple-element.47) | copy-start | bytes 3932164
  161.3 1.2 copy-start.4
  161.3 1.9 %copy-start.3 = (f32[40,16,128]{2,1,0:T(8,128)S(1)}, f32[40,16,128]{2,1,0:T(8,128)}, u32[]{:S(2)}) copy-start(f32[40,16,128]{2,1,0:T(8,128)} %get-tuple-element.49) | copy-start | bytes 983044

commit v4 on v3

--- a/solution.py
+++ b/solution.py
@@ -287,8 +287,8 @@
 
 
 def send_kernel(
-    scale, slot_ref, stat_slot_ref, prompt_ref, length_ref, q_ref, g_ref, k_ref, v_ref, final_ref, stat_in,
-    q, g, k, v, packed, stat, stat_send, load_sem, stat_s, stat_r, *scratch
+    scale, held, table_ref, prompt_ref, length_ref, q_ref, g_ref, k_ref, v_ref, final_ref, stat_in, group_ref,
+    q, g, k, v, packed, stat, stat_send, ids, load_sem, stat_s, stat_r, *scratch
 ):
     loads = [
         pltpu.make_async_copy(src, dst, load_sem.at[i])
@@ -303,21 +303,13 @@
     loads[0].wait()
     loads[1].wait()
 
-    def mask_rows(i, carry):
-        for j in range(per):
-            slot = i * per + j
-            g[slot] = live_rows(g[slot], length_ref[slot])
-        return carry
-
-    lax.fori_loop(0, count // per, mask_rows, 0)
-
     def fill(i, carry):
         for half in range(2):
             for c in range(2):
-                slot = slot_ref[half * n_dp + i * 2 + c]
+                slot = table_ref[2, half * n_dp + i * 2 + c]
                 at = (half, i // SIDE, lax.rem(i, SIDE), c)
                 packed[at + (slice(0, rows), slice(None))] = q[slot]
-                packed[at + (slice(rows, 2 * rows), slice(None))] = g[slot]
+                packed[at + (slice(rows, 2 * rows), slice(None))] = live_rows(g[slot], length_ref[slot])
         return carry
 
     lax.fori_loop(0, SIDE * SIDE, fill, 0)
@@ -335,7 +327,9 @@
     def forward(i, carry):
         slots = [i * per + j for j in range(per)]
         for slot, (lse, row_sum) in zip(slots, forward_slots(slots, scale, q, g, k, v)):
-            stat[slot] = pack_rows(lse, row_sum, prompt_ref[slot].astype(F32))
+            lane = lax.broadcasted_iota(jnp.int32, row_sum.shape, 1)
+            row_sum = jnp.where(lane < length_ref[slot], row_sum, 0.0)
+            stat[slot] = pack_rows(lse, row_sum, jnp.bitwise_and(prompt_ref[slot], held - 1).astype(F32))
         return carry
 
     steps = count // per
@@ -345,7 +339,7 @@
 
     def fill_stats(i, carry):
         for half in range(2):
-            slot = stat_slot_ref[i * 2 + half]
+            slot = table_ref[3, i * 2 + half]
             row = lax.broadcasted_iota(jnp.int32, stat.shape[1:], 0)
             block = stat[jnp.maximum(slot, 0)].astype(F32)
             stat_send[i, half] = jnp.where((row >= 4) & (slot < 0), -1.0, block).astype(BF16)
@@ -359,37 +353,70 @@
     own.wait()
     for copy in copies:
         copy.wait_recv()
+    x, y, _ = place()
+
+    def name(i, carry):
+        for half in range(2):
+            ids[pl.ds(2 * i + half, 1), :] = stat_in[i, half].astype(F32)[4:5]
+        return carry
+
+    lax.fori_loop(0, n_dp, name, 0)
+    items = 2 * n_dp
+    column = ids[...]
+    item = lax.broadcasted_iota(jnp.int32, column.shape, 0)
+    lane = lax.broadcasted_iota(jnp.int32, column.shape, 1)
+    row = jnp.sum(jnp.where(item == lane, column, 0.0), axis=0, keepdims=True)
+    earlier = jnp.where((column == row) & (lane < item), 1.0, 0.0)
+    order = jnp.sum(earlier, axis=1, keepdims=True)
+    spot = jnp.where(column >= 0.0, column * FANOUT + order, -1.0)
+    hit = spot == lane.astype(F32)
+    half, core = jnp.bitwise_and(item, 1), jnp.bitwise_and(jnp.right_shift(item, 1), 1)
+    ax = jnp.bitwise_and(jnp.right_shift(item, 4) - x + SIDE, SIDE - 1)
+    ay = jnp.bitwise_and(jnp.bitwise_and(jnp.right_shift(item, 2), SIDE - 1) - y + SIDE, SIDE - 1)
+    first, second = jnp.where(half == 0, ax, ay), jnp.where(half == 0, ay, ax)
+    where = ((half * SIDE + first) * SIDE + second) * 2 + core
+    group_ref[0:1] = jnp.sum(jnp.where(hit, item, 0), axis=0, keepdims=True)
+    group_ref[1:2] = jnp.sum(jnp.where(hit, where, 0), axis=0, keepdims=True)
+    group_ref[2:] = jnp.zeros((6, group_ref.shape[1]), jnp.int32)
     bulk[8]()
     for copy in copies:
         copy.wait_send()
 
 
-def send_out(slots, stat_slots, prompts, lengths, queries, grads, keys, values, scale):
+def send_out(held, table, prompts, lengths, queries, grads, keys, values, scale):
     count, rows, dim = queries.shape
     n_dp = 2 * SIDE * SIDE
     V, D = pltpu.VMEM, pltpu.SemaphoreType.DMA
     resp = (count, rows, dim)
     shape = (2, SIDE, SIDE, 2, 2 * rows, dim)
     scratch = [V(resp, BF16)] * 4 + [V(shape, BF16), V((count, STAT, dim), BF16), V((n_dp, 2, STAT, dim), BF16)]
+    scratch += [V((2 * n_dp, 128), F32)]
     scratch += [D((5,)), D((n_dp,)), D((n_dp,))]
     for _ in range(2):
         scratch += route_scratch(2 * rows, dim, BF16) + route_sems()
     smem = pl.BlockSpec(memory_space=pltpu.SMEM)
     anywhere = pl.BlockSpec(memory_space=pl.ANY)
     return pl.pallas_call(
-        functools.partial(send_kernel, scale),
-        out_shape=(jax.ShapeDtypeStruct(shape, BF16), jax.ShapeDtypeStruct((n_dp, 2, STAT, dim), BF16)),
-        in_specs=[smem] * 4 + [anywhere] * 4,
-        out_specs=(anywhere, anywhere),
+        functools.partial(send_kernel, scale, held),
+        out_shape=(
+            jax.ShapeDtypeStruct(shape, BF16),
+            jax.ShapeDtypeStruct((n_dp, 2, STAT, dim), BF16),
+            jax.ShapeDtypeStruct((8, 128), jnp.int32),
+        ),
+        in_specs=[smem] * 3 + [anywhere] * 4,
+        out_specs=(anywhere, pl.BlockSpec(memory_space=pltpu.VMEM), pl.BlockSpec(memory_space=pltpu.VMEM)),
         scratch_shapes=scratch,
         compiler_params=pltpu.CompilerParams(collective_id=1, has_side_effects=True),
-    )(slots, stat_slots, prompts, lengths, queries, grads, keys, values)
-
-
-def holder_kernel(
-    scale, factor, item_ref, stat_at_ref, back_ref, a_ref, b_ref, sa_ref, sb_ref, k_ref, v_ref,
-    out_ref, stat_ref, dk_ref, dv_ref, kt, vt, out_buf, stat_buf, out_sem, stat_sem,
-):
+    )(table, prompts, lengths, queries, grads, keys, values)
+
+
+PAIRS = 4
+WIDE = 2 * PAIRS
+
+
+def holder_kernel(scale, factor, group_ref, table_ref, *refs):
+    slot_refs, stat_refs = refs[:WIDE], refs[WIDE : 2 * WIDE]
+    k_ref, v_ref, out_ref, stat_ref, dk_ref, dv_ref, kt, vt, out_buf, stat_buf, out_sem, stat_sem = refs[2 * WIDE :]
     prompt, step = pl.program_id(0), pl.program_id(1)
     count = pl.num_programs(1)
     index = prompt * count + step
@@ -403,74 +430,100 @@
 
     def leaving(at, j):
         slot = lax.rem(at, 2)
-        item = stat_at_ref[2 * at + j]
+        item = group_ref[0, WIDE * at + j]
         return (
-            pltpu.make_async_copy(out_buf.at[slot, j], out_ref.at[back_ref[item]], out_sem.at[slot, j]),
+            pltpu.make_async_copy(out_buf.at[slot, j], out_ref.at[table_ref[4, item]], out_sem.at[slot, j]),
             pltpu.make_async_copy(stat_buf.at[slot, j], stat_ref.at[item], stat_sem.at[slot, j]),
         )
 
-    rows = a_ref.shape[1] // 2
-    query = jnp.concatenate([a_ref[0, 0:rows, :], b_ref[0, 0:rows, :]], axis=0)
-    grad = jnp.concatenate([a_ref[0, rows : 2 * rows, :], b_ref[0, rows : 2 * rows, :]], axis=0)
-    lse_a, sum_a = unpack_rows(sa_ref[0])
-    lse_b, sum_b = unpack_rows(sb_ref[0])
-    resp_lse = jnp.concatenate([lse_a, lse_b], axis=1)
-    resp_sum = jnp.concatenate([sum_a, sum_b], axis=1)
-    scores = dot(k_ref[0], query, NT) * scale
-    grad_prob = dot(v_ref[0], grad, NT)
-    top = jnp.max(scores, axis=0, keepdims=True)
-    exps = jnp.exp2(scores - top)
-    total = jnp.sum(exps, axis=0, keepdims=True)
-    row_sum = jnp.sum(exps * grad_prob, axis=0, keepdims=True)
-    prefix_lse = top + jnp.log2(total)
-    high = jnp.maximum(prefix_lse, resp_lse)
-    lse = high + jnp.log2(jnp.exp2(prefix_lse - high) + jnp.exp2(resp_lse - high))
-    weight = jnp.exp2(prefix_lse - lse) / total
-    delta = weight * row_sum + jnp.exp2(resp_lse - lse) * resp_sum
-    prob = exps * weight
-    dscore = (prob * (grad_prob - delta)).astype(BF16)
-    prob = prob.astype(BF16)
-    dk_ref[0] += dot(dscore, query, NN) * factor
-    dv_ref[0] += dot(prob, grad, NN)
-    out = jnp.transpose(dot(vt[...], prob, NN)).astype(BF16)
-    dq = jnp.transpose(dot(kt[...], dscore, NN) * factor).astype(BF16)
-
     @pl.when(index >= 2)
     def _():
-        for j in range(2):
+        for j in range(WIDE):
             for copy in leaving(index - 2, j):
                 copy.wait()
 
+    rows = slot_refs[0].shape[1] // 2
+    pairs = [(2 * i, 2 * i + 1) for i in range(PAIRS)]
+
+    def both(part):
+        return [jnp.concatenate([slot_refs[i][0, part, :], slot_refs[j][0, part, :]], axis=0) for i, j in pairs]
+
+    query, grad = both(slice(0, rows)), both(slice(rows, 2 * rows))
+    own = [unpack_rows(ref[0]) for ref in stat_refs]
+    resp_lse = [jnp.concatenate([own[i][0], own[j][0]], axis=1) for i, j in pairs]
+    resp_sum = [jnp.concatenate([own[i][1], own[j][1]], axis=1) for i, j in pairs]
     slot = lax.rem(index, 2)
-    for j in range(2):
-        part = slice(j * rows, (j + 1) * rows)
-        out_buf[slot, j, 0:rows, :] = out[part]
-        out_buf[slot, j, rows:, :] = dq[part]
-        stat_buf[slot, j] = pack_rows(lse[:, part], delta[:, part])
+    chunk = 128
+    parts = [slice(c, c + chunk) for c in range(0, k_ref.shape[1], chunk)]
+
+    def products(n):
+        return dot(k_ref[0], query[n], NT), dot(v_ref[0], grad[n], NT)
+
+    def weights(n, scores, grad_prob):
+        tops, exps, totals, sums = [], [], [], []
+        for part in parts:
+            some = scores[part] * scale
+            tops.append(jnp.max(some, axis=0, keepdims=True))
+            exps.append(jnp.exp2(some - tops[-1]))
+            totals.append(jnp.sum(exps[-1], axis=0, keepdims=True))
+            sums.append(jnp.sum(exps[-1] * grad_prob[part], axis=0, keepdims=True))
+        top = functools.reduce(jnp.maximum, tops)
+        shares = [jnp.exp2(a - top) for a in tops]
+        total = sum(a * b for a, b in zip(shares, totals))
+        row_sum = sum(a * b for a, b in zip(shares, sums))
+        prefix_lse = top + jnp.log2(total)
+        high = jnp.maximum(prefix_lse, resp_lse[n])
+        lse = high + jnp.log2(jnp.exp2(prefix_lse - high) + jnp.exp2(resp_lse[n] - high))
+        weight = jnp.exp2(prefix_lse - lse) / total
+        delta = weight * row_sum + jnp.exp2(resp_lse[n] - lse) * resp_sum[n]
+        probs = [a * (weight * b) for a, b in zip(exps, shares)]
+        dscore = [(a * (grad_prob[part] - delta)).astype(BF16) for a, part in zip(probs, parts)]
+        for m, at in enumerate(pairs[n]):
+            part = slice(m * rows, (m + 1) * rows)
+            stat_buf[slot, at] = pack_rows(lse[:, part], delta[:, part])
+        return jnp.concatenate([a.astype(BF16) for a in probs], axis=0), jnp.concatenate(dscore, axis=0)
+
+    def close(n, prob, dscore):
+        dk_ref[0] += dot(dscore, query[n], NN)
+        dv_ref[0] += dot(prob, grad[n], NN)
+        out = jnp.transpose(dot(vt[...], prob, NN)).astype(BF16)
+        dq = jnp.transpose(dot(kt[...], dscore, NN) * factor).astype(BF16)
+        for m, at in enumerate(pairs[n]):
+            part = slice(m * rows, (m + 1) * rows)
+            out_buf[slot, at, 0:rows, :] = out[part]
+            out_buf[slot, at, rows:, :] = dq[part]
+
+    after = products(0)
+    for n in range(PAIRS):
+        now = after
+        if n + 1 < PAIRS:
+            after = products(n + 1)
+        close(n, *weights(n, *now))
+    for j in range(WIDE):
         for copy in leaving(index, j):
             copy.start()
 
     @pl.when(index == pl.num_programs(0) * count - 1)
     def _():
         for at in (index - 1, index):
-            for j in range(2):
+            for j in range(WIDE):
                 for copy in leaving(at, j):
                     copy.wait()
 
 
-def holder(items, stat_at, back_to, received, stats, keys, values, scale, factor):
+def holder(groups, table, received, stats, keys, values, scale, factor):
     count, height, dim = received.shape
     held, length, _ = keys.shape
     rows = height // 2
-    steps = FANOUT // 2
+    steps = FANOUT // WIDE
 
     def one(k):
-        return pl.BlockSpec((1, height, dim), lambda p, j, ids, b, c: (ids[p * FANOUT + 2 * j + k], 0, 0))
+        return pl.BlockSpec((1, height, dim), lambda p, j, ids, b: (ids[1, p * FANOUT + WIDE * j + k], 0, 0))
 
     def stat(k):
-        return pl.BlockSpec((1, STAT, dim), lambda p, j, ids, b, c: (b[p * FANOUT + 2 * j + k], 0, 0))
-
-    whole = pl.BlockSpec((1, length, dim), lambda p, j, ids, b, c: (p, 0, 0))
+        return pl.BlockSpec((1, STAT, dim), lambda p, j, ids, b: (ids[0, p * FANOUT + WIDE * j + k], 0, 0))
+
+    whole = pl.BlockSpec((1, length, dim), lambda p, j, ids, b: (p, 0, 0))
     return pl.pallas_call(
         functools.partial(holder_kernel, scale, factor),
         out_shape=(
@@ -480,9 +533,9 @@
             jax.ShapeDtypeStruct((held, length, dim), F32),
         ),
         grid_spec=pltpu.PrefetchScalarGridSpec(
-            num_scalar_prefetch=3,
+            num_scalar_prefetch=2,
             grid=(held, steps),
-            in_specs=[one(0), one(1), stat(0), stat(1), whole, whole],
+            in_specs=[one(k) for k in range(WIDE)] + [stat(k) for k in range(WIDE)] + [whole, whole],
             out_specs=(
                 pl.BlockSpec(memory_space=pl.ANY),
                 pl.BlockSpec(memory_space=pl.ANY),
@@ -492,13 +545,13 @@
             scratch_shapes=[
                 pltpu.VMEM((dim, length), BF16),
                 pltpu.VMEM((dim, length), BF16),
-                pltpu.VMEM((2, 2, 2 * rows, dim), BF16),
-                pltpu.VMEM((2, 2, STAT, dim), BF16),
-                pltpu.SemaphoreType.DMA((2, 2)),
-                pltpu.SemaphoreType.DMA((2, 2)),
+                pltpu.VMEM((2, WIDE, 2 * rows, dim), BF16),
+                pltpu.VMEM((2, WIDE, STAT, dim), BF16),
+                pltpu.SemaphoreType.DMA((2, WIDE)),
+                pltpu.SemaphoreType.DMA((2, WIDE)),
             ],
         ),
-    )(items, stat_at, back_to, received, received, stats, stats, keys, values)
+    )(groups, table, *([received] * WIDE), *([stats] * WIDE), keys, values)
 
 
 HEADS = 8
@@ -574,12 +627,12 @@
                 self.copy(by, number, base).wait_send()
 
 
-def local_slots(slots, scale, factor, fetch_ref, prompt_ref, length_ref, stat_in, q, g, k, v, dk, dv, out, dq):
+def local_slots(slots, scale, factor, table_ref, prompt_ref, length_ref, stat_in, q, g, k, v, dk, dv, out, dq):
     query = [q[s] for s in slots]
     grad = [live_rows(g[s], length_ref[s]) for s in slots]
     key = [k[s] for s in slots]
     value = [v[s] for s in slots]
-    stats = [unpack_rows(stat_in[fetch_ref[s] // 2, lax.rem(fetch_ref[s], 2)]) for s in slots]
+    stats = [unpack_rows(stat_in[table_ref[1, s] // 2, lax.rem(table_ref[1, s], 2)]) for s in slots]
     lse = [jnp.where(prompt_ref[s] >= 0, a, 1e30) for s, (a, _) in zip(slots, stats)]
     delta = [jnp.where(prompt_ref[s] >= 0, a, 0.0) for s, (_, a) in zip(slots, stats)]
     scores = [dot(a, b, NT) * scale for a, b in zip(key, query)]
@@ -597,10 +650,10 @@
 
 
 def return_kernel(
-    scale, factor, fetch_ref, stat_fetch_ref, prompt_ref, length_ref,
+    scale, factor, table_ref, prompt_ref, length_ref,
     back_ref, stat_ref, pdk_ref, pdv_ref, q_ref, g_ref, k_ref, v_ref,
-    out_ref, dq_ref, drk_ref, drv_ref, all_k, all_v,
-    q, g, k, v, pdk, pdv, dk, dv, out, dq, final, stat_in, load_sem, stat_s, stat_r, *scratch
+    final, out_ref, dq_ref, drk_ref, drv_ref, all_k, all_v,
+    q, g, k, v, pdk, pdv, dk, dv, out, dq, stat_in, load_sem, stat_s, stat_r, *scratch
 ):
     loads = [
         pltpu.make_async_copy(src, dst, load_sem.at[i])
@@ -629,14 +682,14 @@
     prompt_rows = pdk.shape[1] // HEADS
     slot_rows = q.shape[1] // HEADS
 
-    def prompt_part(ref):
-        return lambda t: ref[:, pl.ds(pl.multiple_of(t * prompt_rows, prompt_rows), prompt_rows), :]
+    def prompt_part(ref, by):
+        return lambda t: ref[:, pl.ds(pl.multiple_of(t * prompt_rows, prompt_rows), prompt_rows), :] * by
 
     def slot_part(ref, group):
         some = slice(group * (count // GROUPS), (group + 1) * (count // GROUPS))
         return lambda t: ref[some, pl.ds(pl.multiple_of(t * slot_rows, slot_rows), slot_rows), :]
 
-    owns = [prompt_part(pdk), prompt_part(pdv)]
+    owns = [prompt_part(pdk, factor), prompt_part(pdv, 1.0)]
     for group in range(GROUPS):
         owns += [slot_part(dk, group), slot_part(dv, group)]
     rings = []
@@ -665,7 +718,7 @@
         def go(i, carry):
             slots = [(group * steps + i) * per + j for j in range(per)]
             local_slots(
-                slots, scale, factor, stat_fetch_ref, prompt_ref, length_ref, stat_in, q, g, k, v, dk, dv, out, dq
+                slots, scale, factor, table_ref, prompt_ref, length_ref, stat_in, q, g, k, v, dk, dv, out, dq
             )
             return carry
 
@@ -684,6 +737,11 @@
     bulk[1]()
     ring(0, 2)
     local(1)
+    leaving = [
+        pltpu.make_async_copy(src, dst, load_sem.at[i]) for i, (src, dst) in enumerate(((out, out_ref), (dq, dq_ref)))
+    ]
+    for copy in leaving:
+        copy.start()
     ring(2, 1)
     bulk[2]()
     ring(1, 2)
@@ -713,22 +771,8 @@
         one.close()
     bulk[7]()
 
-    rows = q.shape[1]
-    n_dp = 2 * SIDE * SIDE
-
-    def merge(i, carry):
-        for j in range(per):
-            slot = i * per + j
-            at = fetch_ref[slot]
-            back = final[at // n_dp, lax.rem(at // (2 * SIDE), SIDE), lax.rem(at // 2, SIDE), lax.rem(at, 2)]
-            row = lax.broadcasted_iota(jnp.int32, (rows, back.shape[1]), 0)
-            live = row < jnp.where(prompt_ref[slot] >= 0, length_ref[slot], 0)
-            both = back.astype(F32)
-            out_ref[slot] = jnp.where(live, both[0:rows] + out[slot].astype(F32), 0.0).astype(BF16)
-            dq_ref[slot] = jnp.where(live, both[rows:] + dq[slot].astype(F32), 0.0).astype(BF16)
-        return carry
-
-    lax.fori_loop(0, count // per, merge, 0)
+    for copy in leaving:
+        copy.wait()
     bulk[8]()
     for one in rings:
         one.close()
@@ -739,7 +783,7 @@
 GROUPS = 2
 
 
-def give_back(fetch, stat_fetch, prompts, lengths, back, stats, pdk, pdv, queries, grads, keys, values, scale, factor):
+def give_back(table, prompts, lengths, back, stats, pdk, pdv, queries, grads, keys, values, scale, factor):
     count, rows, dim = queries.shape
     held, length, _ = pdk.shape
     height = back.shape[-2]
@@ -747,7 +791,6 @@
     V, D = pltpu.VMEM, pltpu.SemaphoreType.DMA
     resp = (count, rows, dim)
     scratch = [V(resp, BF16)] * 4 + [V(pdk.shape, F32)] * 2 + [V(resp, F32)] * 2 + [V(resp, BF16)] * 2
-    scratch += [V(back.shape, BF16)]
     scratch += [V((n_dp, 2, STAT, dim), BF16), D((7,)), D((n_dp,)), D((n_dp,))]
     for _ in range(2):
         scratch += route_scratch(height, dim, BF16) + route_sems()
@@ -762,6 +805,7 @@
     return pl.pallas_call(
         functools.partial(return_kernel, scale, factor),
         out_shape=(
+            jax.ShapeDtypeStruct(back.shape, BF16),
             jax.ShapeDtypeStruct(resp, BF16),
             jax.ShapeDtypeStruct(resp, BF16),
             part,
@@ -769,11 +813,90 @@
             parts,
             parts,
         ),
-        in_specs=[smem] * 4 + [anywhere] * 8,
-        out_specs=(vmem, vmem, vmem, vmem, vmem, vmem),
+        in_specs=[smem] * 3 + [anywhere] * 8,
+        out_specs=(anywhere, anywhere, anywhere, vmem, vmem, vmem, vmem),
         scratch_shapes=scratch,
         compiler_params=pltpu.CompilerParams(collective_id=2, has_side_effects=True),
-    )(fetch, stat_fetch, prompts, lengths, back, stats, pdk, pdv, queries, grads, keys, values)
+    )(table, prompts, lengths, back, stats, pdk, pdv, queries, grads, keys, values)
+
+
+def finish_kernel(per_step, table_ref, prompt_ref, length_ref, *refs):
+    back_refs = refs[:per_step]
+    out_part, dq_part, drk, drv, pk, pv, out_ref, dq_ref, drk_ref, drv_ref, pk_ref, pv_ref = refs[per_step:]
+    rows = out_part.shape[1]
+    step = pl.program_id(0)
+    for j in range(per_step):
+        slot = step * per_step + j
+        row = lax.broadcasted_iota(jnp.int32, out_part.shape[1:], 0)
+        live = row < jnp.where(prompt_ref[slot] >= 0, length_ref[slot], 0)
+        back = back_refs[j]
+        out = back[0, 0:rows, :].astype(F32) + out_part[j].astype(F32)
+        dq = back[0, rows : 2 * rows, :].astype(F32) + dq_part[j].astype(F32)
+        out_ref[j] = jnp.where(live, out, 0.0).astype(BF16)
+        dq_ref[j] = jnp.where(live, dq, 0.0).astype(BF16)
+    drk_ref[...] = drk[...]
+    drv_ref[...] = drv[...]
+    pk_ref[...] = pk[0].astype(F32)
+    pv_ref[...] = pv[0].astype(F32)
+
+
+def finish(table, prompts, lengths, back, out_part, dq_part, drk, drv, all_k, all_v):
+    count, rows, dim = out_part.shape
+    _, held, part, _ = all_k.shape
+    per_step = count // HEADS
+    some = pl.BlockSpec((per_step, rows, dim), lambda i, a, b, c: (i, 0, 0))
+    own = pl.BlockSpec((per_step, rows // HEADS, dim), lambda i, a, b, c: (i, 0, 0))
+    piece = pl.BlockSpec((1, held, part, dim), lambda i, a, b, c: (i, 0, 0, 0))
+    placed = pl.BlockSpec((held, part, dim), lambda i, a, b, c: (0, i, 0))
+
+    def one(j):
+        return pl.BlockSpec((1, 2 * rows, dim), lambda i, a, b, c: (a[0, i * per_step + j], 0, 0))
+
+    return pl.pallas_call(
+        functools.partial(finish_kernel, per_step),
+        out_shape=(jax.ShapeDtypeStruct((count, rows, dim), BF16),) * 2
+        + (jax.ShapeDtypeStruct(drk.shape, F32),) * 2
+        + (jax.ShapeDtypeStruct((held, HEADS * part, dim), F32),) * 2,
+        grid_spec=pltpu.PrefetchScalarGridSpec(
+            num_scalar_prefetch=3,
+            grid=(HEADS,),
+            in_specs=[one(j) for j in range(per_step)] + [some, some, own, own, piece, piece],
+            out_specs=(some, some, own, own, placed, placed),
+        ),
+    )(table, prompts, lengths, *([back] * per_step), out_part, dq_part, drk, drv, all_k, all_v)
+
+
+def table_kernel(held, prompt_ref, table_ref):
+    x, y, _ = place()
+    count = prompt_ref.shape[1]
+    prompts = prompt_ref[...]
+    own_row = jnp.where(prompts >= 0, jnp.right_shift(prompts, held.bit_length() - 1), -1)
+    one = lax.broadcasted_iota(jnp.int32, (count, count), 0)
+    two = lax.broadcasted_iota(jnp.int32, (count, count), 1)
+    own_column = jnp.sum(jnp.where(one == two, own_row, 0), axis=1, keepdims=True)
+    same = own_column == own_row
+    order_column = jnp.sum(jnp.where(same & (two < one), 1, 0), axis=1, keepdims=True)
+    order_row = jnp.sum(jnp.where(same & (one < two), 1, 0), axis=0, keepdims=True)
+
+    def position(own, order, x_from, y_from, stand):
+        hx, hy, hc = jnp.right_shift(own, 3), jnp.bitwise_and(jnp.right_shift(own, 1), 3), jnp.bitwise_and(own, 1)
+        hx, hy = jnp.bitwise_and(hx - x_from, SIDE - 1), jnp.bitwise_and(hy - y_from, SIDE - 1)
+        first, second = jnp.where(order == 0, hx, hy), jnp.where(order == 0, hy, hx)
+        at = ((order * SIDE + first) * SIDE + second) * 2 + hc
+        return jnp.where(own >= 0, at, stand)
+
+    table_ref[...] = jnp.zeros_like(table_ref)
+    table_ref[0:1, 0:count] = position(own_row, order_row, x, y, 0)
+    table_ref[1:2, 0:count] = jnp.where(own_row >= 0, own_row * 2 + order_row, 0)
+    items = 4 * SIDE * SIDE
+    slot = lax.broadcasted_iota(jnp.int32, (count, items), 0)
+    item = lax.broadcasted_iota(jnp.int32, (count, items), 1)
+    target = position(own_column, order_column, 0, 0, -1)
+    table_ref[2:3, 0:items] = jnp.sum(jnp.where(target == item, slot, 0), axis=0, keepdims=True)
+    stat = jnp.where(own_column >= 0, own_column * 2 + order_column, -1)
+    table_ref[3:4, 0:items] = jnp.sum(jnp.where(stat == item, slot + 1, 0), axis=0, keepdims=True) - 1
+    item = lax.broadcasted_iota(jnp.int32, (1, items), 1)
+    table_ref[4:5, 0:items] = position(jnp.right_shift(item, 1), jnp.bitwise_and(item, 1), 0, 0, 0)
 
 
 def body(queries, resp_keys, resp_values, prompt_keys, prompt_values, grad_out, slot_prompt, slot_length):
@@ -783,57 +906,23 @@
     scale = factor * LOG2E
     n_dp = 2 * SIDE * SIDE
     items = 2 * n_dp
-    x, y, core = place()
-    ids = jnp.arange(slot_count, dtype=jnp.int32)
-    at = jnp.arange(items, dtype=jnp.int32)
-    own = jnp.where(slot_prompt >= 0, slot_prompt // held, -1)
-    before = ids[None, :] < ids[:, None]
-    order = jnp.sum((own[:, None] == own[None, :]) & before, axis=1, dtype=jnp.int32)
-    hx, hy, hc = own // (2 * SIDE), own // 2 % SIDE, own % 2
-    first, second = jnp.where(order == 0, hx, hy), jnp.where(order == 0, hy, hx)
-    here_first, here_second = jnp.where(order == 0, x, y), jnp.where(order == 0, y, x)
-    live = own >= 0
-    target = jnp.where(live, ((order * SIDE + first) * SIDE + second) * 2 + hc, -1)
-    near_first, near_second = (first - here_first + SIDE) % SIDE, (second - here_second + SIDE) % SIDE
-    fetch = jnp.where(live, ((order * SIDE + near_first) * SIDE + near_second) * 2 + hc, 0)
-    stat_fetch = jnp.where(live, own * 2 + order, 0)
-    hit = target[None, :] == at[:, None]
-    send_slot = jnp.sum(jnp.where(hit, ids[None, :], 0), axis=1, dtype=jnp.int32)
-    stat_hit = jnp.where(live, stat_fetch, -1)[None, :] == at[:, None]
-    stat_slot = jnp.sum(jnp.where(stat_hit, ids[None, :] + 1, 0), axis=1, dtype=jnp.int32) - 1
-    half, from_core = at % 2, at // 2 % 2
-    from_x, from_y = at // (4 * SIDE), at // 4 % SIDE
-    back_to, received_at = [], []
-    for dx, dy, to in ((0, 0, back_to), (x, y, received_at)):
-        ax, ay = (from_x - dx + SIDE) % SIDE, (from_y - dy + SIDE) % SIDE
-        first, second = jnp.where(half == 0, ax, ay), jnp.where(half == 0, ay, ax)
-        to.append(((half * SIDE + first) * SIDE + second) * 2 + from_core)
-
-    received, stats_in = send_out(
-        send_slot, stat_slot, slot_prompt % held, slot_length, queries, grad_out, resp_keys, resp_values, scale
+    table = pl.pallas_call(
+        functools.partial(table_kernel, held), out_shape=jax.ShapeDtypeStruct((8, 128), jnp.int32)
+    )(slot_prompt.reshape(1, slot_count))
+    received, stats_in, groups = send_out(
+        held, table, slot_prompt, slot_length, queries, grad_out, resp_keys, resp_values, scale
     )
     received = received.reshape((items,) + received.shape[4:])
     stats_in = stats_in.reshape((items,) + stats_in.shape[2:])
-    item_prompt = stats_in[:, 4, 0].astype(jnp.int32)
-    order_in = jnp.sum((item_prompt[:, None] == item_prompt[None, :]) & (at[None, :] < at[:, None]), axis=1, dtype=jnp.int32)
-    spot = jnp.where(item_prompt >= 0, item_prompt * FANOUT + order_in, -1)
-    group_hit = spot[None, :] == jnp.arange(held * FANOUT, dtype=jnp.int32)[:, None]
-    group_stat = jnp.sum(jnp.where(group_hit, at[None, :], 0), axis=1, dtype=jnp.int32)
-    group_item = jnp.sum(jnp.where(group_hit, received_at[0][None, :], 0), axis=1, dtype=jnp.int32)
-
-    result, stats, pdk, pdv = holder(
-        group_item, group_stat, back_to[0], received, stats_in, prompt_keys, prompt_values, scale, factor
-    )
+    result, stats, pdk, pdv = holder(groups, table, received, stats_in, prompt_keys, prompt_values, scale, factor)
     grid = (2, SIDE, SIDE, 2)
-    attn_out, grad_queries, drk, drv, all_k, all_v = give_back(
-        fetch, stat_fetch, slot_prompt, slot_length, result.reshape(grid + result.shape[1:]),
+    back, local_out, local_dq, drk, drv, all_k, all_v = give_back(
+        table, slot_prompt, slot_length, result.reshape(grid + result.shape[1:]),
         stats.reshape((n_dp, 2) + stats.shape[1:]), pdk, pdv, queries, grad_out, resp_keys, resp_values, scale, factor,
     )
-
-    def joined(parts):
-        return jnp.swapaxes(parts, 0, 1).reshape(held, length, dim).astype(F32)
-
-    return (attn_out, grad_queries, drk, drv, joined(all_k), joined(all_v))
+    return finish(
+        table, slot_prompt, slot_length, back.reshape(result.shape), local_out, local_dq, drk, drv, all_k, all_v
+    )
 
 
 def solution(mesh):

time: 164 us -> 151 us (0.921)
  other arithmetic: 8.29 us -> 0 us
  local copies, waits for them, and re-layouts: 7.18 us -> 0 us
  Pallas kernels: 148 us -> 150 us
    pallas_call x1 -> x3, Pallas kernels: 60 us -> 70.8 us  [the longest x1 61.1 us: send_out(): pl.pallas_call(functools.partial(send_kernel, scale, held), out_shape=(ja...]
    pallas_call x1, Pallas kernels: 20.4 us -> 13.6 us  [holder(): pl.pallas_call(functools.partial(holder_kernel, scale, factor), out_shape...]
    unnamed x14 -> x0, local copies, waits for them, and re-layouts: 5.01 us -> none
    convert_element_type x3 -> x0, other arithmetic: 3.38 us -> none  [the longest x1 2.13 us: body(): item_prompt = stats_in[:, 4, 0].astype(jnp.int32)]
    select_n x4 -> x0, other arithmetic: 2.23 us -> none  [the longest x1 1.17 us: body(): slot_prompt % held]
    convert_element_type x2 -> x0, local copies, waits for them, and re-layouts: 2.17 us -> none  [joined(): return jnp.swapaxes(parts, 0, 1).reshape(held, length, dim).astype(F32)]
    pallas_call x1, Pallas kernels: 67.3 us -> 65.6 us  [give_back(): pl.pallas_call(functools.partial(return_kernel, scale, factor), out_shape...]
where the time goes in v4:
time: 151 us
  Pallas kernels  150 us (99%)
    pallas_call x1, Pallas kernels, give_back(): pl.pallas_call(functools.partial(return_kernel, scale, factor), out_shape...  65.6 us
    pallas_call x1, Pallas kernels, send_out(): pl.pallas_call(functools.partial(send_kernel, scale, held), out_shape=(ja...  61.1 us
    pallas_call x1, Pallas kernels, holder(): pl.pallas_call(functools.partial(holder_kernel, scale, factor), out_shape...  13.6 us
    pallas_call x1, Pallas kernels, finish(): pl.pallas_call(functools.partial(finish_kernel, per_step), out_shape=(jax...  8.29 us

profile of v4, /device:TPU:1, one launch (start us, length us, event | category | flops | bytes accessed | tf_op | source)
XLA Modules:
  0.0 150.7 jit_solution(1074269798569079298)
XLA Ops:
  0.6 1.4 shard_map.127.table_ref
  2.1 61.1 %shard_map.128 = (bf16[2,4,4,2,256,128]{5,4,3,2,1,0:T(8,128)(2,1)}, bf16[32,2,16,128]{3,2,1,0:T(8,128)(2,1)}, s32[8,128]{1,0:T(8,128)}) custom-call(s32[8,128]{1,0:T(8,128)} %shard_map.127.table_ref, s32[40]{0:T(128)} %prompt_ref.5, s32[40]{0:T(128)} %length_ref.5, bf16[40,128,128]{2,1,0:T(8,128)(2,1)} %q_ref.3, bf16[40,128,128]{2,1,0:T(8,128)(2,1)} %g_ref.3, ...), custom_call_target="tpu_custom_call" | custom-call | tf_op jit(solution)/shard_map/pallas_call | solution.py:399
  63.2 13.6 %shard_map.129 = (bf16[64,256,128]{2,1,0:T(8,128)(2,1)}, bf16[64,16,128]{2,1,0:T(8,128)(2,1)}, f32[4,512,128]{2,1,0:T(8,128)}, f32[4,512,128]{2,1,0:T(8,128)}) custom-call(s32[8,128]{1,0:T(8,128)} %get-tuple-element.20.group_ref, s32[8,128]{1,0:T(8,128)} %shard_map.127.table_ref, bf16[64,256,128]{2,1,0:T(8,128)(2,1)} %bitcast.6, ...), custom_call_target="tpu_custom_call" | custom-call | tf_op jit(solution)/shard_map/pallas_call | solution.py:527
  76.8 65.6 %shard_map.130 = (bf16[2,4,4,2,256,128]{5,4,3,2,1,0:T(8,128)(2,1)}, bf16[40,128,128]{2,1,0:T(8,128)(2,1)}, bf16[40,128,128]{2,1,0:T(8,128)(2,1)}, f32[40,16,128]...) custom-call(s32[8,128]{1,0:T(8,128)} %shard_map.127.table_ref, ...), custom_call_target="tpu_custom_call" | custom-call | tf_op jit(solution)/shard_map/pallas_call | solution.py:805
  142.4 8.3 %shard_map.131 = (bf16[40,128,128]{2,1,0:T(8,128)(2,1)}, bf16[40,128,128]{2,1,0:T(8,128)(2,1)}, f32[40,16,128]{2,1,0:T(8,128)}, f32[40,16,128]{2,1,0:T(8,128)}, ...) custom-call(s32[8,128]{1,0:T(8,128)} %shard_map.127.table_ref, s32[40]{0:T(128)} %prompt_ref.5, s32[40]{0:T(128)} %length_ref.5, ...), custom_call_target="tpu_custom_call" | custom-call | tf_op jit(solution)/shard_map/pallas_call | solution.py:855

commit v5 on v4

--- a/solution.py
+++ b/solution.py
@@ -143,13 +143,15 @@
             for side in range(2):
                 for route in routes:
                     go(route.first_far(side, j))
-        for route in routes:
-            go(route.second_far(0))
-            for side in range(2):
-                second_near(route, 0, side)
         for side in range(2):
             for route in routes:
                 go(route.first_direct(side, 2))
+        for route in routes:
+            go(route.second_far(0))
+        for j in (1, 3):
+            for side in range(2):
+                for route in routes:
+                    go(route.first_direct(side, j))
         for route in routes:
             second_here(route, 0)
 
@@ -159,20 +161,20 @@
                 for route in routes:
                     route.first_far(side, j).wait_recv()
                     go(route.first_forward(side, j))
-        for j in (1, 3, 0):
-            for side in range(2):
-                for route in routes:
-                    go(route.first_direct(side, j))
-
-    def relay_own():
-        for route in routes:
-            relay(route, 0)
+        for side in range(2):
+            for route in routes:
+                go(route.first_direct(side, 0))
 
     def turn_far():
         for side in range(2):
             for route in routes:
                 route.first_direct(side, 2).wait_recv()
                 go(route.second_far(3 if side == 0 else 1))
+        for route in routes:
+            relay(route, 0)
+        for route in routes:
+            for side in range(2):
+                second_near(route, 0, side)
 
     def turn_forwarded():
         for route in routes:
@@ -180,9 +182,6 @@
                 for j in range(2):
                     route.first_forward(side, j).wait_recv()
             go(route.second_far(2))
-            for side in range(2):
-                second_near(route, 2, side)
-            second_here(route, 2)
 
     def turn_near():
         for j, way in ((1, 0), (3, 1)):
@@ -190,15 +189,23 @@
                 for route in routes:
                     route.first_direct(side, j).wait_recv()
                     second_near(route, 3 if side == 0 else 1, way)
+
+    def relay_rest():
+        for r in (3, 1):
+            for route in routes:
+                relay(route, r)
+        for route in routes:
+            for side in range(2):
+                second_near(route, 2, side)
+
+    def turn_here():
         for side in range(2):
             for route in routes:
                 route.first_direct(side, 0).wait_recv()
                 second_here(route, 3 if side == 0 else 1)
-
-    def relay_rest():
-        for r in (3, 1, 2):
-            for route in routes:
-                relay(route, r)
+        for route in routes:
+            second_here(route, 2)
+            relay(route, 2)
 
     def arrive():
         for r in (0, 3, 1, 2):
@@ -214,7 +221,7 @@
             if copy.is_remote:
                 copy.wait_send()
 
-    return [begin, forward, relay_own, turn_far, turn_forwarded, turn_near, relay_rest, arrive, close]
+    return [begin, forward, turn_far, turn_forwarded, turn_near, relay_rest, turn_here, arrive, close]
 
 
 def dot(a, b, dims):
@@ -241,8 +248,9 @@
     return jnp.where(rows < 4, packed, third).astype(BF16)
 
 
-def unpack_rows(packed):
+def unpack_rows(packed, half):
     rows = packed.astype(F32)
+    rows = jnp.where(half > 0, pltpu.roll(rows, STAT - 4, 0), rows)
     return rows[0:1] + rows[1:2], rows[2:3] + rows[3:4]
 
 
@@ -338,17 +346,19 @@
     lax.fori_loop(steps // 2, steps, forward, 0)
 
     def fill_stats(i, carry):
-        for half in range(2):
-            slot = table_ref[3, i * 2 + half]
-            row = lax.broadcasted_iota(jnp.int32, stat.shape[1:], 0)
-            block = stat[jnp.maximum(slot, 0)].astype(F32)
-            stat_send[i, half] = jnp.where((row >= 4) & (slot < 0), -1.0, block).astype(BF16)
+        slots = [table_ref[3, i * 2 + half] for half in range(2)]
+        one, two = [stat[jnp.maximum(slot, 0)].astype(F32) for slot in slots]
+        row = lax.broadcasted_iota(jnp.int32, one.shape, 0)
+        name_one = jnp.where(slots[0] < 0, -1.0, one)
+        name_two = jnp.where(slots[1] < 0, -1.0, two)
+        names = jnp.where(row == 8, name_one, name_two)
+        numbers = jnp.where(row < 4, one, pltpu.roll(two, 4, 0))
+        stat_send[i] = jnp.where(row < 8, numbers, names).astype(BF16)
         return carry
 
     lax.fori_loop(0, n_dp, fill_stats, 0)
-    bulk[2]()
     own, copies = swap_stats(stat_send, stat_in, load_sem.at[4], stat_s, stat_r)
-    for stage in bulk[3:8]:
+    for stage in bulk[2:8]:
         stage()
     own.wait()
     for copy in copies:
@@ -357,7 +367,7 @@
 
     def name(i, carry):
         for half in range(2):
-            ids[pl.ds(2 * i + half, 1), :] = stat_in[i, half].astype(F32)[4:5]
+            ids[pl.ds(2 * i + half, 1), :] = stat_in[i].astype(F32)[8 + half : 9 + half]
         return carry
 
     lax.fori_loop(0, n_dp, name, 0)
@@ -389,7 +399,7 @@
     V, D = pltpu.VMEM, pltpu.SemaphoreType.DMA
     resp = (count, rows, dim)
     shape = (2, SIDE, SIDE, 2, 2 * rows, dim)
-    scratch = [V(resp, BF16)] * 4 + [V(shape, BF16), V((count, STAT, dim), BF16), V((n_dp, 2, STAT, dim), BF16)]
+    scratch = [V(resp, BF16)] * 4 + [V(shape, BF16), V((count, STAT, dim), BF16), V((n_dp, STAT, dim), BF16)]
     scratch += [V((2 * n_dp, 128), F32)]
     scratch += [D((5,)), D((n_dp,)), D((n_dp,))]
     for _ in range(2):
@@ -400,7 +410,7 @@
         functools.partial(send_kernel, scale, held),
         out_shape=(
             jax.ShapeDtypeStruct(shape, BF16),
-            jax.ShapeDtypeStruct((n_dp, 2, STAT, dim), BF16),
+            jax.ShapeDtypeStruct((n_dp, STAT, dim), BF16),
             jax.ShapeDtypeStruct((8, 128), jnp.int32),
         ),
         in_specs=[smem] * 3 + [anywhere] * 4,
@@ -414,42 +424,49 @@
 WIDE = 2 * PAIRS
 
 
-def holder_kernel(scale, factor, group_ref, table_ref, *refs):
-    slot_refs, stat_refs = refs[:WIDE], refs[WIDE : 2 * WIDE]
-    k_ref, v_ref, out_ref, stat_ref, dk_ref, dv_ref, kt, vt, out_buf, stat_buf, out_sem, stat_sem = refs[2 * WIDE :]
-    prompt, step = pl.program_id(0), pl.program_id(1)
-    count = pl.num_programs(1)
-    index = prompt * count + step
-
-    @pl.when(step == 0)
+def holder_kernel(
+    scale, factor, group_ref, table_ref, in_ref, stat_in, k_ref, v_ref, out_ref, stat_ref, dk_ref, dv_ref,
+    kt, vt, slots_in, out_buf, in_sem, out_sem,
+):
+    index = pl.program_id(0)
+    rows = in_ref.shape[1] // 2
+
+    def coming(at):
+        return pltpu.make_async_copy(in_ref.at[group_ref[1, at]], slots_in.at[at], in_sem.at[at])
+
+    @pl.when(index == 0)
     def _():
-        kt[...] = jnp.transpose(k_ref[0])
-        vt[...] = jnp.transpose(v_ref[0])
-        dk_ref[...] = jnp.zeros_like(dk_ref)
-        dv_ref[...] = jnp.zeros_like(dv_ref)
+        for at in range(slots_in.shape[0]):
+            coming(at).start()
+
+    kt[...] = jnp.transpose(k_ref[0])
+    vt[...] = jnp.transpose(v_ref[0])
+    dk_ref[...] = jnp.zeros_like(dk_ref)
+    dv_ref[...] = jnp.zeros_like(dv_ref)
 
     def leaving(at, j):
         slot = lax.rem(at, 2)
         item = group_ref[0, WIDE * at + j]
-        return (
-            pltpu.make_async_copy(out_buf.at[slot, j], out_ref.at[table_ref[4, item]], out_sem.at[slot, j]),
-            pltpu.make_async_copy(stat_buf.at[slot, j], stat_ref.at[item], stat_sem.at[slot, j]),
-        )
+        return pltpu.make_async_copy(out_buf.at[slot, j], out_ref.at[table_ref[4, item]], out_sem.at[slot, j])
 
     @pl.when(index >= 2)
     def _():
         for j in range(WIDE):
-            for copy in leaving(index - 2, j):
-                copy.wait()
-
-    rows = slot_refs[0].shape[1] // 2
+            leaving(index - 2, j).wait()
+
+    for j in range(WIDE):
+        coming(WIDE * index + j).wait()
     pairs = [(2 * i, 2 * i + 1) for i in range(PAIRS)]
+    items = [group_ref[0, WIDE * index + j] for j in range(WIDE)]
 
     def both(part):
-        return [jnp.concatenate([slot_refs[i][0, part, :], slot_refs[j][0, part, :]], axis=0) for i, j in pairs]
+        return [
+            jnp.concatenate([slots_in[WIDE * index + i, part, :], slots_in[WIDE * index + j, part, :]], axis=0)
+            for i, j in pairs
+        ]
 
     query, grad = both(slice(0, rows)), both(slice(rows, 2 * rows))
-    own = [unpack_rows(ref[0]) for ref in stat_refs]
+    own = [unpack_rows(stat_in[jnp.right_shift(item, 1)], jnp.bitwise_and(item, 1)) for item in items]
     resp_lse = [jnp.concatenate([own[i][0], own[j][0]], axis=1) for i, j in pairs]
     resp_sum = [jnp.concatenate([own[i][1], own[j][1]], axis=1) for i, j in pairs]
     slot = lax.rem(index, 2)
@@ -480,7 +497,12 @@
         dscore = [(a * (grad_prob[part] - delta)).astype(BF16) for a, part in zip(probs, parts)]
         for m, at in enumerate(pairs[n]):
             part = slice(m * rows, (m + 1) * rows)
-            stat_buf[slot, at] = pack_rows(lse[:, part], delta[:, part])
+            block, half = jnp.right_shift(items[at], 1), jnp.bitwise_and(items[at], 1)
+            numbers = pack_rows(lse[:, part], delta[:, part]).astype(F32)
+            row = lax.broadcasted_iota(jnp.int32, numbers.shape, 0)
+            placed = jnp.where(half > 0, pltpu.roll(numbers, 4, 0), numbers)
+            mine = jnp.right_shift(row, 2) == half
+            stat_ref[block] = jnp.where(mine, placed, stat_ref[block].astype(F32)).astype(BF16)
         return jnp.concatenate([a.astype(BF16) for a in probs], axis=0), jnp.concatenate(dscore, axis=0)
 
     def close(n, prob, dscore):
@@ -500,58 +522,45 @@
             after = products(n + 1)
         close(n, *weights(n, *now))
     for j in range(WIDE):
-        for copy in leaving(index, j):
-            copy.start()
-
-    @pl.when(index == pl.num_programs(0) * count - 1)
+        leaving(index, j).start()
+
+    @pl.when(index == pl.num_programs(0) - 1)
     def _():
         for at in (index - 1, index):
             for j in range(WIDE):
-                for copy in leaving(at, j):
-                    copy.wait()
+                leaving(at, j).wait()
 
 
 def holder(groups, table, received, stats, keys, values, scale, factor):
     count, height, dim = received.shape
     held, length, _ = keys.shape
     rows = height // 2
-    steps = FANOUT // WIDE
-
-    def one(k):
-        return pl.BlockSpec((1, height, dim), lambda p, j, ids, b: (ids[1, p * FANOUT + WIDE * j + k], 0, 0))
-
-    def stat(k):
-        return pl.BlockSpec((1, STAT, dim), lambda p, j, ids, b: (ids[0, p * FANOUT + WIDE * j + k], 0, 0))
-
-    whole = pl.BlockSpec((1, length, dim), lambda p, j, ids, b: (p, 0, 0))
+    whole = pl.BlockSpec((1, length, dim), lambda p, ids, b: (p, 0, 0))
+    small = pl.BlockSpec(stats.shape, lambda p, ids, b: (0, 0, 0))
+    anywhere = pl.BlockSpec(memory_space=pl.ANY)
     return pl.pallas_call(
         functools.partial(holder_kernel, scale, factor),
         out_shape=(
             jax.ShapeDtypeStruct((count, 2 * rows, dim), BF16),
-            jax.ShapeDtypeStruct((count, STAT, dim), BF16),
+            jax.ShapeDtypeStruct(stats.shape, BF16),
             jax.ShapeDtypeStruct((held, length, dim), F32),
             jax.ShapeDtypeStruct((held, length, dim), F32),
         ),
         grid_spec=pltpu.PrefetchScalarGridSpec(
             num_scalar_prefetch=2,
-            grid=(held, steps),
-            in_specs=[one(k) for k in range(WIDE)] + [stat(k) for k in range(WIDE)] + [whole, whole],
-            out_specs=(
-                pl.BlockSpec(memory_space=pl.ANY),
-                pl.BlockSpec(memory_space=pl.ANY),
-                whole,
-                whole,
-            ),
+            grid=(held,),
+            in_specs=[anywhere, small, whole, whole],
+            out_specs=(anywhere, small, whole, whole),
             scratch_shapes=[
                 pltpu.VMEM((dim, length), BF16),
                 pltpu.VMEM((dim, length), BF16),
+                pltpu.VMEM((held * FANOUT, 2 * rows, dim), BF16),
                 pltpu.VMEM((2, WIDE, 2 * rows, dim), BF16),
-                pltpu.VMEM((2, WIDE, STAT, dim), BF16),
-                pltpu.SemaphoreType.DMA((2, WIDE)),
+                pltpu.SemaphoreType.DMA((held * FANOUT,)),
                 pltpu.SemaphoreType.DMA((2, WIDE)),
             ],
         ),
-    )(groups, table, *([received] * WIDE), *([stats] * WIDE), keys, values)
+    )(groups, table, received, stats, keys, values)
 
 
 HEADS = 8
@@ -632,7 +641,7 @@
     grad = [live_rows(g[s], length_ref[s]) for s in slots]
     key = [k[s] for s in slots]
     value = [v[s] for s in slots]
-    stats = [unpack_rows(stat_in[table_ref[1, s] // 2, lax.rem(table_ref[1, s], 2)]) for s in slots]
+    stats = [unpack_rows(stat_in[table_ref[1, s] // 2], lax.rem(table_ref[1, s], 2)) for s in slots]
     lse = [jnp.where(prompt_ref[s] >= 0, a, 1e30) for s, (a, _) in zip(slots, stats)]
     delta = [jnp.where(prompt_ref[s] >= 0, a, 0.0) for s, (_, a) in zip(slots, stats)]
     scores = [dot(a, b, NT) * scale for a, b in zip(key, query)]
@@ -712,11 +721,11 @@
 
     per = 5
 
-    def local(group):
-        steps = count // per // GROUPS
+    def local(piece):
+        steps = count // per // 4
 
         def go(i, carry):
-            slots = [(group * steps + i) * per + j for j in range(per)]
+            slots = [(piece * steps + i) * per + j for j in range(per)]
             local_slots(
                 slots, scale, factor, table_ref, prompt_ref, length_ref, stat_in, q, g, k, v, dk, dv, out, dq
             )
@@ -724,6 +733,7 @@
 
         lax.fori_loop(0, steps, go, 0)
 
+    begin, forward, turn_far, turn_forwarded, turn_near, relay_rest, turn_here, arrive, close = bulk
     loads[0].wait()
     loads[1].wait()
     ring(0, 1)
@@ -733,34 +743,36 @@
     for copy in stats:
         copy.wait_recv()
     local(0)
-    ring(1, 1)
-    bulk[1]()
     ring(0, 2)
     local(1)
+    ring(1, 1)
+    forward()
+    local(2)
+    ring(0, 3)
+    local(3)
+    ring(2, 1)
     leaving = [
         pltpu.make_async_copy(src, dst, load_sem.at[i]) for i, (src, dst) in enumerate(((out, out_ref), (dq, dq_ref)))
     ]
     for copy in leaving:
         copy.start()
-    ring(2, 1)
-    bulk[2]()
+    ring(0, 4)
     ring(1, 2)
-    ring(0, 3)
-    bulk[3]()
+    turn_far()
     ring(2, 2)
-    ring(0, 4)
-    bulk[4]()
-    ring(1, 3)
     all_k[head] = rings[0].result().astype(BF16)
     all_v[head] = rings[1].result().astype(BF16)
     spread(1)
+    ring(1, 3)
+    turn_forwarded()
     ring(2, 3)
-    bulk[5]()
     spread(2)
+    turn_near()
     ring(1, 4)
+    relay_rest()
     spread(3)
     ring(2, 4)
-    bulk[6]()
+    turn_here()
     spread(4)
     half_count = count // GROUPS
     for group in range(GROUPS):
@@ -769,11 +781,10 @@
         drv_ref[some] = rings[3 + 2 * group].result()
     for one in spreads:
         one.close()
-    bulk[7]()
-
+    arrive()
     for copy in leaving:
         copy.wait()
-    bulk[8]()
+    close()
     for one in rings:
         one.close()
     for copy in stats:
@@ -791,7 +802,7 @@
     V, D = pltpu.VMEM, pltpu.SemaphoreType.DMA
     resp = (count, rows, dim)
     scratch = [V(resp, BF16)] * 4 + [V(pdk.shape, F32)] * 2 + [V(resp, F32)] * 2 + [V(resp, BF16)] * 2
-    scratch += [V((n_dp, 2, STAT, dim), BF16), D((7,)), D((n_dp,)), D((n_dp,))]
+    scratch += [V((n_dp, STAT, dim), BF16), D((7,)), D((n_dp,)), D((n_dp,))]
     for _ in range(2):
         scratch += route_scratch(height, dim, BF16) + route_sems()
     for shape in ((held, length // HEADS, dim),) * 2 + ((count // GROUPS, rows // HEADS, dim),) * (2 * GROUPS):
@@ -820,38 +831,47 @@
     )(table, prompts, lengths, back, stats, pdk, pdv, queries, grads, keys, values)
 
 
-def finish_kernel(per_step, table_ref, prompt_ref, length_ref, *refs):
-    back_refs = refs[:per_step]
-    out_part, dq_part, drk, drv, pk, pv, out_ref, dq_ref, drk_ref, drv_ref, pk_ref, pv_ref = refs[per_step:]
+def finish_kernel(
+    per_step, table_ref, prompt_ref, length_ref, in_ref, out_part, dq_part, drk, drv, pk, pv,
+    out_ref, dq_ref, drk_ref, drv_ref, pk_ref, pv_ref, back, in_sem,
+):
     rows = out_part.shape[1]
     step = pl.program_id(0)
+
+    def coming(slot):
+        return pltpu.make_async_copy(in_ref.at[table_ref[0, slot]], back.at[slot], in_sem.at[slot])
+
+    @pl.when(step == 0)
+    def _():
+        for slot in range(back.shape[0]):
+            coming(slot).start()
+
+    drk_ref[...] = drk[...]
+    drv_ref[...] = drv[...]
+    part = pk.shape[2]
+    for i in range(pk.shape[0]):
+        pk_ref[:, i * part : (i + 1) * part, :] = pk[i].astype(F32)
+        pv_ref[:, i * part : (i + 1) * part, :] = pv[i].astype(F32)
     for j in range(per_step):
         slot = step * per_step + j
+        coming(slot).wait()
         row = lax.broadcasted_iota(jnp.int32, out_part.shape[1:], 0)
         live = row < jnp.where(prompt_ref[slot] >= 0, length_ref[slot], 0)
-        back = back_refs[j]
-        out = back[0, 0:rows, :].astype(F32) + out_part[j].astype(F32)
-        dq = back[0, rows : 2 * rows, :].astype(F32) + dq_part[j].astype(F32)
+        out = back[slot, 0:rows, :].astype(F32) + out_part[j].astype(F32)
+        dq = back[slot, rows : 2 * rows, :].astype(F32) + dq_part[j].astype(F32)
         out_ref[j] = jnp.where(live, out, 0.0).astype(BF16)
         dq_ref[j] = jnp.where(live, dq, 0.0).astype(BF16)
-    drk_ref[...] = drk[...]
-    drv_ref[...] = drv[...]
-    pk_ref[...] = pk[0].astype(F32)
-    pv_ref[...] = pv[0].astype(F32)
 
 
 def finish(table, prompts, lengths, back, out_part, dq_part, drk, drv, all_k, all_v):
     count, rows, dim = out_part.shape
     _, held, part, _ = all_k.shape
-    per_step = count // HEADS
+    steps = 4
+    per_step = count // steps
     some = pl.BlockSpec((per_step, rows, dim), lambda i, a, b, c: (i, 0, 0))
     own = pl.BlockSpec((per_step, rows // HEADS, dim), lambda i, a, b, c: (i, 0, 0))
-    piece = pl.BlockSpec((1, held, part, dim), lambda i, a, b, c: (i, 0, 0, 0))
-    placed = pl.BlockSpec((held, part, dim), lambda i, a, b, c: (0, i, 0))
-
-    def one(j):
-        return pl.BlockSpec((1, 2 * rows, dim), lambda i, a, b, c: (a[0, i * per_step + j], 0, 0))
-
+    piece = pl.BlockSpec((HEADS // steps, held, part, dim), lambda i, a, b, c: (i, 0, 0, 0))
+    placed = pl.BlockSpec((held, part * HEADS // steps, dim), lambda i, a, b, c: (0, i, 0))
     return pl.pallas_call(
         functools.partial(finish_kernel, per_step),
         out_shape=(jax.ShapeDtypeStruct((count, rows, dim), BF16),) * 2
@@ -859,11 +879,12 @@
         + (jax.ShapeDtypeStruct((held, HEADS * part, dim), F32),) * 2,
         grid_spec=pltpu.PrefetchScalarGridSpec(
             num_scalar_prefetch=3,
-            grid=(HEADS,),
-            in_specs=[one(j) for j in range(per_step)] + [some, some, own, own, piece, piece],
+            grid=(steps,),
+            in_specs=[pl.BlockSpec(memory_space=pl.ANY), some, some, own, own, piece, piece],
             out_specs=(some, some, own, own, placed, placed),
+            scratch_shapes=[pltpu.VMEM((count, 2 * rows, dim), BF16), pltpu.SemaphoreType.DMA((count,))],
         ),
-    )(table, prompts, lengths, *([back] * per_step), out_part, dq_part, drk, drv, all_k, all_v)
+    )(table, prompts, lengths, back, out_part, dq_part, drk, drv, all_k, all_v)
 
 
 def table_kernel(held, prompt_ref, table_ref):
@@ -904,8 +925,7 @@
     held, length, _ = prompt_keys.shape
     factor = dim ** (-0.5)
     scale = factor * LOG2E
-    n_dp = 2 * SIDE * SIDE
-    items = 2 * n_dp
+    items = 4 * SIDE * SIDE
     table = pl.pallas_call(
         functools.partial(table_kernel, held), out_shape=jax.ShapeDtypeStruct((8, 128), jnp.int32)
     )(slot_prompt.reshape(1, slot_count))
@@ -913,12 +933,11 @@
         held, table, slot_prompt, slot_length, queries, grad_out, resp_keys, resp_values, scale
     )
     received = received.reshape((items,) + received.shape[4:])
-    stats_in = stats_in.reshape((items,) + stats_in.shape[2:])
     result, stats, pdk, pdv = holder(groups, table, received, stats_in, prompt_keys, prompt_values, scale, factor)
     grid = (2, SIDE, SIDE, 2)
     back, local_out, local_dq, drk, drv, all_k, all_v = give_back(
         table, slot_prompt, slot_length, result.reshape(grid + result.shape[1:]),
-        stats.reshape((n_dp, 2) + stats.shape[1:]), pdk, pdv, queries, grad_out, resp_keys, resp_values, scale, factor,
+        stats, pdk, pdv, queries, grad_out, resp_keys, resp_values, scale, factor,
     )
     return finish(
         table, slot_prompt, slot_length, back.reshape(result.shape), local_out, local_dq, drk, drv, all_k, all_v

time: 151 us -> 147 us (0.974)
  Pallas kernels: 150 us -> 146 us
    pallas_call x1, Pallas kernels: 65.6 us -> 63.5 us  [give_back(): pl.pallas_call(functools.partial(return_kernel, scale, factor), out_shape...]
where the time goes in v5:
time: 147 us; the launch traced here: 146 us
  Pallas kernels  146 us (99%)
    pallas_call x1, Pallas kernels, give_back(): pl.pallas_call(functools.partial(return_kernel, scale, factor), out_shape...  63.5 us
    pallas_call x1, Pallas kernels, send_out(): pl.pallas_call(functools.partial(send_kernel, scale, held), out_shape=(ja...  59.6 us
    pallas_call x1, Pallas kernels, holder(): pl.pallas_call(functools.partial(holder_kernel, scale, factor), out_shape...  13.7 us
    pallas_call x1, Pallas kernels, finish(): pl.pallas_call(functools.partial(finish_kernel, per_step), out_shape=(jax...  7.46 us

profile of v5, /device:TPU:1, one launch (start us, length us, event | category | flops | bytes accessed | tf_op | source)
XLA Modules:
  0.0 146.3 jit_solution(176978694079706843)
XLA Ops:
  0.6 1.4 shard_map.127.table_ref
  2.1 59.6 %shard_map.128 = (bf16[2,4,4,2,256,128]{5,4,3,2,1,0:T(8,128)(2,1)}, bf16[32,16,128]{2,1,0:T(8,128)(2,1)}, s32[8,128]{1,0:T(8,128)}) custom-call(s32[8,128]{1,0:T(8,128)} %shard_map.127.table_ref, s32[40]{0:T(128)} %prompt_ref.5, s32[40]{0:T(128)} %length_ref.5, bf16[40,128,128]{2,1,0:T(8,128)(2,1)} %q_ref.3, bf16[40,128,128]{2,1,0:T(8,128)(2,1)} %g_ref.3, ...), custom_call_target="tpu_custom_call" | custom-call | tf_op jit(solution)/shard_map/pallas_call | solution.py:409
  61.7 13.7 %shard_map.129 = (bf16[64,256,128]{2,1,0:T(8,128)(2,1)}, bf16[32,16,128]{2,1,0:T(8,128)(2,1)}, f32[4,512,128]{2,1,0:T(8,128)}, f32[4,512,128]{2,1,0:T(8,128)}) custom-call(s32[8,128]{1,0:T(8,128)} %get-tuple-element.20.group_ref, s32[8,128]{1,0:T(8,128)} %shard_map.127.table_ref, bf16[64,256,128]{2,1,0:T(8,128)(2,1)} %bitcast.6, ...), custom_call_target="tpu_custom_call" | custom-call | tf_op jit(solution)/shard_map/pallas_call | solution.py:541
  75.4 63.5 %shard_map.130 = (bf16[2,4,4,2,256,128]{5,4,3,2,1,0:T(8,128)(2,1)}, bf16[40,128,128]{2,1,0:T(8,128)(2,1)}, bf16[40,128,128]{2,1,0:T(8,128)(2,1)}, f32[40,16,128]...) custom-call(s32[8,128]{1,0:T(8,128)} %shard_map.127.table_ref, ...), custom_call_target="tpu_custom_call" | custom-call | tf_op jit(solution)/shard_map/pallas_call | solution.py:816
  138.9 7.5 %shard_map.131 = (bf16[40,128,128]{2,1,0:T(8,128)(2,1)}, bf16[40,128,128]{2,1,0:T(8,128)(2,1)}, f32[40,16,128]{2,1,0:T(8,128)}, f32[40,16,128]{2,1,0:T(8,128)}, ...) custom-call(s32[8,128]{1,0:T(8,128)} %shard_map.127.table_ref, s32[40]{0:T(128)} %prompt_ref.5, s32[40]{0:T(128)} %length_ref.5, ...), custom_call_target="tpu_custom_call" | custom-call | tf_op jit(solution)/shard_map/pallas_call | solution.py:875
